TPU v7x, 128 devices: a whole 4x4x4 slice. The times are simulated.
128 devices in a mesh: pool: 32 (over x, z, core), exp: 4 (over y).
Axes of the slice: x: 4, y: 4, z: 4, core: 2. Of those that a mesh axis runs over, the one named last changes fastest.
Arguments:
- tokens: bfloat16 [512, 1024], P('pool'), as said below
- block_table: int32 [512, 128], replicated, may hold values from -1 to 4607, as said below
- lengths: int32 [512], replicated, may hold values from 1 to 16384, as said below
- k_cache: bfloat16 [4096, 128, 512], P('pool', None, 'exp'), as said below
- v_cache: bfloat16 [4096, 128, 512], P('pool', None, 'exp'), may hold values from -9 to 9
- hidden_store: bfloat16 [512, 128, 1024], P('pool'), may hold values from -6 to 6
- norm_attn: bfloat16 [1024], replicated, may hold values from 0.5 to 1.5
- w_query: bfloat16 [1024, 1024], P(None, 'exp'), as said below
- w_key: bfloat16 [1024, 512], P(None, 'exp'), may hold values from -0.1875 to 0.1875
- w_value: bfloat16 [1024, 512], P(None, 'exp'), may hold values from -0.1875 to 0.1875
- w_out: bfloat16 [1024, 1024], P('exp'), may hold values from -0.1875 to 0.1875
- norm_moe: bfloat16 [1024], replicated, may hold values from 0.5 to 1.5
- expert_ids: int32 [512, 8], P('pool'), may hold values from 0 to 31, all different within a row; in each aligned block of 16 rows (0 to 15, 16 to 31, ...) at most 8 rows name the same one
- gate_weights: float32 [512, 8], P('pool'), may hold values from 0.1 to 1
- w_gate: bfloat16 [32, 1024, 512], P('pool'), may hold values from -0.1875 to 0.1875
- w_up: bfloat16 [32, 1024, 512], P('pool'), may hold values from -0.1875 to 0.1875
- w_down: bfloat16 [32, 512, 1024], P('pool'), may hold values from -0.25 to 0.25
Outputs:
- layer_out: bfloat16 [512, 1024], P('pool', 'exp')
Inputs may be any that keep to these rules, and one draw needn't show every extreme that they name: `block_table`: every block number 0 to 4607 stands exactly once in the table; a request's blocks fill the start of its row and -1 fills the rest; each request has 1 to 128 blocks and some request has exactly 128. `lengths`: A request with n blocks has a length above (n - 1) * 128 and at most n * 128; some request has the length 16384. `expert_ids`: in the rows of one pool index no expert is named by more than 8 rows. `tokens`: entries lie within -8 to 8. `k_cache`: entries lie within -8 to 8. `w_query`: entries are of magnitude below 7 / sqrt(1024).
All inputs are finite; a program needn't handle non-finite values.
Results may differ from a plain program's by a relative error of at most 0.009.
Values may be sent and summed in bfloat16 or wider, within the bound.
No kernel may reach another device: no remote copies, remote signals or barrier semaphores. Data moves between devices by JAX's collectives and lax.ppermute only.
A program may use at most 128 MiB of HBM per device.

v0:
```python
import jax
import jax.numpy as jnp
from jax import lax
from jax.sharding import PartitionSpec as P

HEAD_SIZE = 64


NEG_FILL = -1e30
EPSILON = 1e-05
SCORE_SCALE = 0.125
HIGHEST = lax.Precision.HIGHEST


def merged(value, axis, join):
    pieces = jax.tree.map(lambda part: lax.all_gather(part, axis), value)
    head = jax.tree.map(lambda part: part[0], pieces)
    tail = jax.tree.map(lambda part: part[1:], pieces)
    so_far, _ = lax.scan(lambda so_far, piece: (join(so_far, piece), None), head, tail)
    return so_far


def rms_scale(row_vals, gain_row):
    mean_sq = jnp.mean(row_vals * row_vals, axis=-1, keepdims=True)
    return row_vals * lax.rsqrt(mean_sq + EPSILON) * gain_row


def merge_pair(first, second):
    top_a, sum_a, out_a = first
    top_b, sum_b, out_b = second
    row_top = jnp.maximum(top_a, top_b)
    weight_a = jnp.exp(top_a - row_top)
    weight_b = jnp.exp(top_b - row_top)
    spread = out_a.shape[-1] // top_a.shape[-1]
    merged_out = out_a * jnp.repeat(weight_a, spread, axis=-1) + out_b * jnp.repeat(
        weight_b, spread, axis=-1
    )
    return (row_top, sum_a * weight_a + sum_b * weight_b, merged_out)


def on_device(
    tokens,
    block_table,
    lengths,
    k_cache,
    v_cache,
    hidden_store,
    norm_attn,
    w_query,
    w_key,
    w_value,
    w_out,
    norm_moe,
    expert_ids,
    gate_weights,
    w_gate,
    w_up,
    w_down,
):
    pool_count = lax.axis_size("pool")
    exp_count = lax.axis_size("exp")
    pool_index = lax.axis_index("pool")
    exp_index = lax.axis_index("exp")
    req_dev = tokens.shape[0]
    model_width = tokens.shape[1]
    quarter = model_width // exp_count
    x_rows = tokens.astype(jnp.float32)
    normed = rms_scale(x_rows, norm_attn.astype(jnp.float32)).astype(jnp.bfloat16)
    queries = jnp.dot(normed, w_query, preferred_element_type=jnp.float32).astype(jnp.bfloat16)
    all_queries = lax.all_gather(queries, "pool", axis=0, tiled=True)
    stored_rows = hidden_store.reshape(-1, model_width)
    stored_shape = (hidden_store.shape[0], hidden_store.shape[1], w_key.shape[1])
    key_new = (
        jnp.dot(stored_rows, w_key, preferred_element_type=jnp.float32)
        .astype(jnp.bfloat16)
        .reshape(stored_shape)
    )
    value_new = (
        jnp.dot(stored_rows, w_value, preferred_element_type=jnp.float32)
        .astype(jnp.bfloat16)
        .reshape(stored_shape)
    )
    keys_here = jnp.concatenate([k_cache, key_new], axis=0)
    values_here = jnp.concatenate([v_cache, value_new], axis=0)
    slot_count, page_len, key_width = keys_here.shape
    query_width = queries.shape[1]
    kv_groups = key_width // HEAD_SIZE
    per_group = query_width // key_width
    head_count = query_width // HEAD_SIZE
    requests = block_table.shape[0]
    list_len = block_table.shape[1]
    flat_ids = block_table.reshape(-1)
    entry_index = jnp.arange(requests * list_len, dtype=jnp.int32)
    global_slot = pool_index * slot_count + jnp.arange(slot_count, dtype=jnp.int32)
    found_entry = jnp.sum(
        jnp.where(flat_ids[None, :] == global_slot[:, None], entry_index[None, :], 0), axis=1
    )
    slot_req = found_entry // list_len
    slot_block = found_entry % list_len
    member = slot_req[:, None] == jnp.arange(requests, dtype=jnp.int32)[None, :]
    member_low = member.astype(jnp.bfloat16)
    slot_queries = jnp.dot(member_low, all_queries, preferred_element_type=jnp.float32).astype(
        jnp.bfloat16
    )
    slot_length = jnp.sum(jnp.where(member, lengths[None, :], 0), axis=1)
    q_grouped = slot_queries.reshape(slot_count, kv_groups, per_group, HEAD_SIZE)
    k_grouped = keys_here.reshape(slot_count, page_len, kv_groups, HEAD_SIZE)
    v_grouped = values_here.reshape(slot_count, page_len, kv_groups, HEAD_SIZE)
    scores = (
        jnp.einsum("sgqd,stgd->sgqt", q_grouped, k_grouped, preferred_element_type=jnp.float32)
        * SCORE_SCALE
    )
    positions = slot_block[:, None] * page_len + jnp.arange(page_len, dtype=jnp.int32)[None, :]
    is_valid = (positions < slot_length[:, None])[:, None, None, :]
    masked = jnp.where(is_valid, scores, NEG_FILL)
    block_top = jnp.max(masked, axis=-1)
    weights = jnp.where(is_valid, jnp.exp(masked - block_top[..., None]), 0.0)
    block_sum = jnp.sum(weights, axis=-1)
    block_out = jnp.einsum(
        "sgqt,stgd->sgqd",
        weights.astype(jnp.bfloat16),
        v_grouped,
        preferred_element_type=jnp.float32,
    )
    slot_top = block_top.reshape(slot_count, head_count)
    slot_sum = block_sum.reshape(slot_count, head_count)
    slot_out = block_out.reshape(slot_count, query_width)
    local_top = jnp.max(jnp.where(member[:, :, None], slot_top[:, None, :], NEG_FILL), axis=0)
    own_top = jnp.max(jnp.where(member[:, :, None], local_top[None, :, :], NEG_FILL), axis=1)
    factor = jnp.exp(slot_top - own_top)
    one_hot = member.astype(jnp.float32)
    local_sum = jnp.einsum("sr,sh->rh", one_hot, slot_sum * factor, precision=HIGHEST)
    local_out = jnp.einsum(
        "sr,sc->rc", one_hot, slot_out * jnp.repeat(factor, HEAD_SIZE, axis=1), precision=HIGHEST
    )
    all_top, all_sum, all_out = merged((local_top, local_sum, local_out), "pool", merge_pair)
    row_start = pool_index * req_dev
    total_sum = lax.dynamic_slice_in_dim(all_sum, row_start, req_dev, 0)
    accum = lax.dynamic_slice_in_dim(all_out, row_start, req_dev, 0)
    attended = (accum / jnp.repeat(total_sum, HEAD_SIZE, axis=-1)).astype(jnp.bfloat16)
    projected = lax.psum(jnp.dot(attended, w_out, preferred_element_type=jnp.float32), "exp")
    mixed = x_rows + projected
    normed_moe = rms_scale(mixed, norm_moe.astype(jnp.float32)).astype(jnp.bfloat16)
    top_count = expert_ids.shape[1]
    capacity = min(req_dev, 2 * ((req_dev * top_count + pool_count - 1) // pool_count))
    route_flat = expert_ids.reshape(-1)
    expert_hit = (route_flat[:, None] == jnp.arange(pool_count, dtype=jnp.int32)[None, :]).astype(
        jnp.int32
    )
    slot_rank = jnp.sum(jnp.cumsum(expert_hit, axis=0) * expert_hit, axis=1) - 1
    slot_pos = route_flat * capacity + slot_rank
    placed = (
        slot_pos[:, None] == jnp.arange(pool_count * capacity, dtype=jnp.int32)[None, :]
    ).astype(jnp.float32)
    placed = placed.reshape(req_dev, top_count, pool_count * capacity)
    send_map = jnp.sum(placed, axis=1).astype(jnp.bfloat16)
    combine_map = jnp.einsum("tk,tkc->tc", gate_weights, placed, precision=HIGHEST)
    outgoing = jnp.einsum("tc,td->cd", send_map, normed_moe, preferred_element_type=jnp.float32)
    outgoing = outgoing.astype(jnp.bfloat16).reshape(pool_count, capacity, model_width)
    arrived = lax.all_to_all(outgoing, "pool", split_axis=0, concat_axis=0, tiled=True)
    sources = arrived.shape[0]
    slots_here = arrived.shape[1]
    row_block = arrived.reshape(-1, model_width)
    gate_act = jnp.dot(row_block, w_gate[0], preferred_element_type=jnp.float32)
    up_act = jnp.dot(row_block, w_up[0], preferred_element_type=jnp.float32)
    hidden = (jax.nn.silu(gate_act) * up_act).astype(jnp.bfloat16)
    expert_low = jnp.dot(hidden, w_down[0], preferred_element_type=jnp.float32).astype(jnp.bfloat16)
    expert_low = expert_low.reshape(sources, slots_here, model_width)
    expert_out = lax.dynamic_slice_in_dim(expert_low, exp_index * quarter, quarter, 2)
    returned = lax.all_to_all(expert_out, "pool", split_axis=0, concat_axis=0, tiled=True)
    moe_share = jnp.dot(
        combine_map,
        returned.reshape(pool_count * capacity, quarter).astype(jnp.float32),
        precision=HIGHEST,
    )
    mixed_share = lax.dynamic_slice_in_dim(mixed, exp_index * quarter, quarter, 1)
    return (mixed_share + moe_share).astype(jnp.bfloat16)


def solution(mesh):
    placed = (
        P("pool", None),
        P(),
        P(),
        P("pool", None, "exp"),
        P("pool", None, "exp"),
        P("pool", None, None),
        P(),
        P(None, "exp"),
        P(None, "exp"),
        P(None, "exp"),
        P("exp", None),
        P(),
        P("pool", None),
        P("pool", None),
        P("pool", None, None),
        P("pool", None, None),
        P("pool", None, None),
    )
    return jax.shard_map(
        on_device, mesh=mesh, in_specs=placed, out_specs=P("pool", "exp"), check_vma=False
    )
```

profile of v0, /device:TPU:1, one launch (start us, length us, event | category | flops | bytes accessed | tf_op | source)
XLA Modules:
  0.0 319.9 jit_solution(11277620771074689597)
XLA Ops:
  6.5 6.6 %select_reduce_fusion = s32[144]{0:T(256)S(1)} fusion(s32[65536]{0:T(1024)} %bitcast.87, s32[144]{0:T(256)S(1)} %iota_add_fusion), kind=kLoop, calls=%fused_computation.10 | loop fusion | flops 28311408 | bytes 263296 | tf_op jit(solution)/shard_map/reduce_sum | solution.py:95
  15.8 1.3 convolution_convert_fusion.5
  17.1 27.6 %all_gather.21 = bf16[512,256]{1,0:T(8,128)(2,1)S(1)} all-gather(bf16[16,256]{1,0:T(8,128)(2,1)S(1)} %convolution_convert_fusion.5), channel_id=1, replica_groups=mesh['pool'=32,'exp'=4] {'pool'}, dimensions={0}, use_global_device_ids=true | all-gather | bytes 270336 | tf_op jit(solution)/shard_map/all_gather | solution.py:70
  45.1 3.5 %convolution_convert_fusion.1 = bf16[2048,128]{1,0:T(8,128)(2,1)S(1)} fusion(bf16[2048,1024]{1,0:T(8,128)(2,1)} %bitcast.89, bf16[1024,128]{1,0:T(8,128)(2,1)} %param.27), kind=kOutput, calls=%fused_computation.20 | convolution fusion | flops 537133056 | bytes 4980736 | tf_op jit(solution)/shard_map/dot_general | solution.py:74
  49.6 6.4 %copy.75 = bf16[128,128,128]{1,2,0:T(8,128)(2,1)} copy(bf16[128,128,128]{2,1,0:T(8,128)(2,1)} %param.22) | data formatting | bytes 8388608 | tf_op args[3]
  56.1 3.7 %fusion.67 = (f32[144,2,2]{2,1,0:T(2,128)S(1)}, f32[144,2,2,128]{3,2,1,0:T(2,128)S(1)}) fusion(bf16[144,2,2,64]{3,2,1,0:T(2,128)(2,1)S(1)} %reshape.185, bf16[16,128,2,64]{1,3,2,0:T(8,128)(2,1)S(1)} %copy.77, bf16[128,128,2,64]{1,3,2,0:T(8,128)(2,1)} %bitcast.84, pred[144,128]{1,0:T(8,128)(4,1)S(1)} %add_compare_fusion), kind=kOutput, calls=%fused_computation.105 | convolution fusion | flops 12017088 | bytes 5107968 | tf_op jit(solution)/shard_map/sgqd,stgd->sgqt/dot_general | solution.py:110
  61.0 3.4 %convolution_convert_fusion = bf16[2048,128]{1,0:T(8,128)(2,1)S(1)} fusion(bf16[2048,1024]{1,0:T(8,128)(2,1)} %bitcast.90, bf16[1024,128]{1,0:T(8,128)(2,1)S(1)} %copy-done.6), kind=kOutput, calls=%fused_computation.19 | convolution fusion | flops 537133056 | bytes 4980736 | tf_op jit(solution)/shard_map/dot_general | solution.py:79
  65.5 6.4 %copy.80 = bf16[128,128,128]{1,2,0:T(8,128)(2,1)} copy(bf16[128,128,128]{2,1,0:T(8,128)(2,1)} %param.23) | data formatting | bytes 8388608 | tf_op args[4]
  71.9 4.8 %fusion.7 = f32[144,2,2,64]{3,2,1,0:T(2,128)S(1)} fusion(bf16[16,128,2,64]{1,3,2,0:T(8,128)(2,1)S(1)} %copy.82, bf16[128,128,2,64]{1,3,2,0:T(8,128)(2,1)} %bitcast.85, f32[144,2,2,128]{3,2,1,0:T(2,128)S(1)} %get-tuple-element.103, pred[144,128]{1,0:T(8,128)(4,1)S(1)} %add_compare_fusion, f32[144,2,2]{2,1,0:T(2,128)S(1)} %get-tuple-element.102), kind=kOutput, calls=%fused_computation.15 | convolution fusion | flops 12017664 | bytes 5181696 | tf_op jit(solution)/shard_map/sgqt,stgd->sgqd/dot_general | solution.py:119
  77.0 1.5 fusion.35
  79.9 24.3 %all-gather.1 = f32[16384,4]{0,1:T(4,128)S(1)} all-gather(f32[512,4]{0,1:T(4,128)S(1)} %fusion.36), channel_id=3, replica_groups=mesh['pool'=32,'exp'=4] {'pool'}, dimensions={0}, use_global_device_ids=true | all-gather | bytes 270336 | tf_op jit(solution)/shard_map/all_gather | solution.py:16
  104.3 22.6 %all-gather = f32[16384,4]{0,1:T(4,128)S(1)} all-gather(f32[512,4]{0,1:T(4,128)S(1)} %select_reduce_fusion.2), channel_id=2, replica_groups=mesh['pool'=32,'exp'=4] {'pool'}, dimensions={0}, use_global_device_ids=true | all-gather | bytes 270336 | tf_op jit(solution)/shard_map/all_gather | solution.py:16
  128.3 23.1 %all-gather.5.cloned.1.call-done = f32[16384,256]{1,0:T(8,128)} async-done(((f32[512,256]{1,0:T(8,128)}), f32[16384,256]{1,0:T(8,128)}) %all-gather.5.cloned.1.call-update) | async-done | bytes 16777232 | tf_op jit(solution)/shard_map/all_gather | solution.py:16
  152.7 11.1 %slice.35 = f32[15872,256]{1,0:T(8,128)} slice(f32[16384,256]{1,0:T(8,128)} %all-gather.5.cloned.1.call-done), slice={[512:16384], [0:256]} | slice | bytes 32505856 | tf_op jit(solution)/shard_map/slice | solution.py:18
  163.9 70.2 %while.14 = (s32[]{:T(128)}, f32[512,4]{0,1:T(4,128)S(1)}, f32[512,4]{0,1:T(4,128)S(1)}, f32[512,256]{0,1:T(8,128)S(1)}, f32[31,512,4]{1,2,0:T(4,128)}, /*index=...) while((s32[]{:T(128)}, f32[512,4]{0,1:T(4,128)S(1)}, f32[512,4]{0,1:T(4,128)S(1)}, ...), condition=%wide.region_8.9_spmd, body=%wide.region_7.8_spmd.sunk | while | flops 405506 | bytes 3752029 | solution.py:19
  166.9 1.1 constant_dynamic-slice_fusion.4
  235.3 37.8 %all-reduce.2.cloned.1.call-done = f32[16,1024]{1,0:T(8,128)} async-done(((f32[16,1024]{1,0:T(8,128)}), f32[16,1024]{1,0:T(8,128)}) %all-reduce.2.cloned.1.call-update) | async-done | bytes 65552 | tf_op jit(solution)/shard_map/psum | solution.py:141
  274.1 1.1 fusion.11
  275.2 9.7 %all-to-all-start = ((bf16[32,8,1024]{2,1,0:T(8,128)(2,1)}), bf16[32,8,1024]{2,1,0:T(8,128)(2,1)S(1)}, u32[]{:S(2)}, u32[]{:S(2)}) async-start(bf16[32,8,1024]{2,1,0:T(8,128)(2,1)} %fusion.11), calls=%async_computation | async-start | bytes 1048576 | tf_op jit(solution)/shard_map/all_to_all | solution.py:160
  285.0 11.5 %all-to-all-done = bf16[32,8,1024]{2,1,0:T(8,128)(2,1)S(1)} async-done(((bf16[32,8,1024]{2,1,0:T(8,128)(2,1)}), bf16[32,8,1024]{2,1,0:T(8,128)(2,1)S(1)}, u32[]{:S(2)}, u32[]{:S(2)}) %all-to-all-start) | async-done | bytes 524320 | tf_op jit(solution)/shard_map/all_to_all | solution.py:160
  296.5 1.7 fusion.20
  298.2 2.0 fusion.12
  300.9 3.6 %all-to-all-start.1 = ((bf16[32,8,256]{2,1,0:T(8,128)(2,1)}), bf16[32,8,256]{2,1,0:T(8,128)(2,1)S(1)}, u32[]{:S(2)}, u32[]{:S(2)}) async-start(bf16[32,8,256]{2,1,0:T(8,128)(2,1)} %constant_dynamic-slice_fusion.2), calls=%async_computation.1 | async-start | bytes 262144 | tf_op jit(solution)/shard_map/all_to_all | solution.py:170
  304.8 7.4 %all-to-all-done.1 = bf16[32,8,256]{2,1,0:T(8,128)(2,1)S(1)} async-done(((bf16[32,8,256]{2,1,0:T(8,128)(2,1)}), bf16[32,8,256]{2,1,0:T(8,128)(2,1)S(1)}, u32[]{:S(2)}, u32[]{:S(2)}) %all-to-all-start.1) | async-done | bytes 131104 | tf_op jit(solution)/shard_map/all_to_all | solution.py:170
  (193 shorter events, 82.8 us)
Async XLA Ops:
  6.5 291.6 %copy-start = (bf16[1,512,1024]{2,1,0:T(8,128)(2,1)S(1)}, bf16[1,512,1024]{2,1,0:T(8,128)(2,1)}, u32[]{:S(2)}) copy-start(bf16[1,512,1024]{2,1,0:T(8,128)(2,1)} %param.35) | copy-start | bytes 3145732
  6.5 144.9 %all-gather.5.cloned.1.call-start = ((), (), s32[]{:S(2)}) async-start(), calls=%async_computation.3 | async-start | bytes 17301504 | tf_op jit(solution)/shard_map/all_gather | solution.py:16
  56.1 4.9 %copy-start.6 = (bf16[1024,128]{1,0:T(8,128)(2,1)S(1)}, bf16[1024,128]{1,0:T(8,128)(2,1)}, u32[]{:S(2)}) copy-start(bf16[1024,128]{1,0:T(8,128)(2,1)} %param.28) | copy-start | bytes 786436
  76.7 50.9 %copy-start.3 = (s32[16,8]{0,1:T(8,128)S(1)}, s32[16,8]{0,1:T(8,128)}, u32[]{:S(2)}) copy-start(s32[16,8]{0,1:T(8,128)} %param.31) | copy-start | bytes 1540
  76.7 51.6 %copy-start.5 = (bf16[1024]{0:T(1024)(128)(2,1)S(1)}, bf16[1024]{0:T(1024)(128)(2,1)}, u32[]{:S(2)}) copy-start(bf16[1024]{0:T(1024)(128)(2,1)} %param.30) | copy-start | bytes 6148
  78.5 194.6 %all-reduce.2.cloned.1.call-start = ((), (), s32[]{:S(2)}) async-start(), calls=%async_computation.2 | async-start | bytes 131072 | tf_op jit(solution)/shard_map/psum | solution.py:141
  163.9 70.4 %copy-start.1 = (bf16[256,1024]{1,0:T(8,128)(2,1)S(1)}, bf16[256,1024]{1,0:T(8,128)(2,1)}, u32[]{:S(2)}) copy-start(bf16[256,1024]{1,0:T(8,128)(2,1)} %param.29) | copy-start | bytes 1572868
  163.9 109.2 %copy-start.2 = (bf16[16,1024]{1,0:T(8,128)(2,1)S(1)}, bf16[16,1024]{1,0:T(8,128)(2,1)}, u32[]{:S(2)}) copy-start(bf16[16,1024]{1,0:T(8,128)(2,1)} %param.19) | copy-start | bytes 98308
  163.9 121.0 %copy-start.4 = (f32[16,8]{0,1:T(8,128)S(1)}, f32[16,8]{0,1:T(8,128)}, u32[]{:S(2)}) copy-start(f32[16,8]{0,1:T(8,128)} %param.32) | copy-start | bytes 1540
  275.2 21.3 %all-to-all-start = ((bf16[32,8,1024]{2,1,0:T(8,128)(2,1)}), bf16[32,8,1024]{2,1,0:T(8,128)(2,1)S(1)}, u32[]{:S(2)}, u32[]{:S(2)}) async-start(bf16[32,8,1024]{2,1,0:T(8,128)(2,1)} %fusion.11), calls=%async_computation | async-start | bytes 1048576 | tf_op jit(solution)/shard_map/all_to_all | solution.py:160
  300.9 11.3 %all-to-all-start.1 = ((bf16[32,8,256]{2,1,0:T(8,128)(2,1)}), bf16[32,8,256]{2,1,0:T(8,128)(2,1)S(1)}, u32[]{:S(2)}, u32[]{:S(2)}) async-start(bf16[32,8,256]{2,1,0:T(8,128)(2,1)} %constant_dynamic-slice_fusion.2), calls=%async_computation.1 | async-start | bytes 262144 | tf_op jit(solution)/shard_map/all_to_all | solution.py:170
Sparse Core Ops, SparseCore 0:
  78.6 72.7 all-gather.4
  235.3 37.7 all-reduce.1
where the time goes:
time: 324 us; the launch traced here: 320 us
  waiting for transfers between devices  79.9 us (25%)
  blocking collectives  74.6 us (23%)
  local copies, waits for them, and re-layouts  70 us (22%)
  other arithmetic  42 us (13%)
  matrix products  25.4 us (8%)
  between operations  13.7 us (4%)
  starting transfers between devices  13.4 us (4%)
    all_gather x2, blocking collectives, merged(): pieces = jax.tree.map(lambda part: lax.all_gather(part, axis), value)  47 us
    dynamic_slice x62, local copies, waits for them, and re-layouts, merged(): lax.scan(lambda so_far, piece: (join(so_far, piece), None), head, tail)  39.6 us
    psum x1, waiting for transfers between devices, on_device(): lax.psum(jnp.dot(attended, w_out, preferred_element_type=jnp.float32), 'e...  37.8 us
    all_gather x1, blocking collectives, on_device(): all_queries = lax.all_gather(queries, 'pool', axis=0, tiled=True)  27.6 us
    all_gather x1, waiting for transfers between devices, merged(): pieces = jax.tree.map(lambda part: lax.all_gather(part, axis), value)  23.1 us
    add x31, other arithmetic, merge_pair(): return (row_top, sum_a * weight_a + sum_b * weight_b, merged_out)  22.5 us
    unnamed x18, local copies, waits for them, and re-layouts  13 us
    slice x3, local copies, waits for them, and re-layouts, merged(): tail = jax.tree.map(lambda part: part[1:], pieces)  11.9 us
  transfers between devices with their start and end apart: 4, of which 4 were waited for; matrix products, arithmetic and copies ran while one was open for 1% of the time, Pallas kernels for 0%

commit v1 on v0

--- a/solution.py
+++ b/solution.py
@@ -12,30 +12,29 @@
 HIGHEST = lax.Precision.HIGHEST
 
 
-def merged(value, axis, join):
-    pieces = jax.tree.map(lambda part: lax.all_gather(part, axis), value)
-    head = jax.tree.map(lambda part: part[0], pieces)
-    tail = jax.tree.map(lambda part: part[1:], pieces)
-    so_far, _ = lax.scan(lambda so_far, piece: (join(so_far, piece), None), head, tail)
-    return so_far
+def gather_pool(value):
+    copies = jnp.broadcast_to(value[None], (lax.axis_size("pool"),) + value.shape)
+    return lax.all_to_all(copies, "pool", split_axis=0, concat_axis=0, tiled=True)
+
+
+def sum_exp(value):
+    size = lax.axis_size("exp")
+    if size != 4:
+        return lax.psum(value, "exp")
+    value = value + lax.ppermute(value, "exp", [(0, 1), (1, 0), (2, 3), (3, 2)])
+    return value + lax.ppermute(value, "exp", [(0, 3), (3, 0), (1, 2), (2, 1)])
+
+
+def split_three(value):
+    high = lax.reduce_precision(value, 8, 7)
+    rest = value - high
+    middle = lax.reduce_precision(rest, 8, 7)
+    return [part.astype(jnp.bfloat16) for part in (high, middle, rest - middle)]
 
 
 def rms_scale(row_vals, gain_row):
     mean_sq = jnp.mean(row_vals * row_vals, axis=-1, keepdims=True)
     return row_vals * lax.rsqrt(mean_sq + EPSILON) * gain_row
-
-
-def merge_pair(first, second):
-    top_a, sum_a, out_a = first
-    top_b, sum_b, out_b = second
-    row_top = jnp.maximum(top_a, top_b)
-    weight_a = jnp.exp(top_a - row_top)
-    weight_b = jnp.exp(top_b - row_top)
-    spread = out_a.shape[-1] // top_a.shape[-1]
-    merged_out = out_a * jnp.repeat(weight_a, spread, axis=-1) + out_b * jnp.repeat(
-        weight_b, spread, axis=-1
-    )
-    return (row_top, sum_a * weight_a + sum_b * weight_b, merged_out)
 
 
 def on_device(
@@ -67,7 +66,7 @@
     x_rows = tokens.astype(jnp.float32)
     normed = rms_scale(x_rows, norm_attn.astype(jnp.float32)).astype(jnp.bfloat16)
     queries = jnp.dot(normed, w_query, preferred_element_type=jnp.float32).astype(jnp.bfloat16)
-    all_queries = lax.all_gather(queries, "pool", axis=0, tiled=True)
+    all_queries = gather_pool(queries).reshape(-1, queries.shape[1])
     stored_rows = hidden_store.reshape(-1, model_width)
     stored_shape = (hidden_store.shape[0], hidden_store.shape[1], w_key.shape[1])
     key_new = (
@@ -130,15 +129,25 @@
     factor = jnp.exp(slot_top - own_top)
     one_hot = member.astype(jnp.float32)
     local_sum = jnp.einsum("sr,sh->rh", one_hot, slot_sum * factor, precision=HIGHEST)
+    scaled_out = (slot_out * jnp.repeat(factor, HEAD_SIZE, axis=1)).astype(jnp.bfloat16)
     local_out = jnp.einsum(
-        "sr,sc->rc", one_hot, slot_out * jnp.repeat(factor, HEAD_SIZE, axis=1), precision=HIGHEST
-    )
-    all_top, all_sum, all_out = merged((local_top, local_sum, local_out), "pool", merge_pair)
-    row_start = pool_index * req_dev
-    total_sum = lax.dynamic_slice_in_dim(all_sum, row_start, req_dev, 0)
-    accum = lax.dynamic_slice_in_dim(all_out, row_start, req_dev, 0)
+        "sr,sc->rc", member_low, scaled_out, preferred_element_type=jnp.float32
+    ).astype(jnp.bfloat16)
+    pieces = split_three(local_top) + split_three(local_sum)
+    parcel = jnp.concatenate([local_out] + pieces, axis=1)
+    parcel = jnp.pad(parcel, ((0, 0), (0, -parcel.shape[1] % 128)))
+    parcel = parcel.reshape(pool_count, req_dev, -1)
+    landed = lax.all_to_all(parcel, "pool", split_axis=0, concat_axis=0, tiled=True)
+    part_out = landed[:, :, :query_width].astype(jnp.float32)
+    part_stats = landed[:, :, query_width : query_width + 6 * head_count].astype(jnp.float32)
+    part_stats = part_stats.reshape(pool_count, req_dev, 2, 3, head_count)
+    part_stats = part_stats[:, :, :, 0] + part_stats[:, :, :, 1] + part_stats[:, :, :, 2]
+    part_top = part_stats[:, :, 0]
+    part_weight = jnp.exp(part_top - jnp.max(part_top, axis=0, keepdims=True))
+    total_sum = jnp.sum(part_weight * part_stats[:, :, 1], axis=0)
+    accum = jnp.sum(part_out * jnp.repeat(part_weight, HEAD_SIZE, axis=-1), axis=0)
     attended = (accum / jnp.repeat(total_sum, HEAD_SIZE, axis=-1)).astype(jnp.bfloat16)
-    projected = lax.psum(jnp.dot(attended, w_out, preferred_element_type=jnp.float32), "exp")
+    projected = sum_exp(jnp.dot(attended, w_out, preferred_element_type=jnp.float32))
     mixed = x_rows + projected
     normed_moe = rms_scale(mixed, norm_moe.astype(jnp.float32)).astype(jnp.bfloat16)
     top_count = expert_ids.shape[1]

time: 324 us -> 120 us (0.37)
  blocking collectives: 74.6 us -> 0 us
  waiting for transfers between devices: 79.9 us -> 31.4 us
  local copies, waits for them, and re-layouts: 70 us -> 22.3 us
  other arithmetic: 42 us -> 13.2 us
  starting transfers between devices: 13.4 us -> 29.9 us
  between operations: 13.7 us -> 0.37 us
  matrix products: 25.4 us -> 21.4 us
    all_gather x3 -> x0, blocking collectives: 74.6 us -> none  [the longest x2 47 us: merged(): pieces = jax.tree.map(lambda part: lax.all_gather(part, axis), value)]
    dynamic_slice x63 -> x0, local copies, waits for them, and re-layouts: 39.7 us -> none  [the longest x62 39.6 us: merged(): lax.scan(lambda so_far, piece: (join(so_far, piece), None), head, tail)]
    psum x1 -> x0, waiting for transfers between devices: 37.8 us -> none  [on_device(): lax.psum(jnp.dot(attended, w_out, preferred_element_type=jnp.float32), 'e...]
    add x62 -> x2, other arithmetic: 29.7 us -> 0.02 us  [the longest x1 0.01 us: on_device(): part_stats[:, :, :, 0] + part_stats[:, :, :, 1] + part_stats[:, :, :, 2]]
    all_gather x1 -> x0, waiting for transfers between devices: 23.1 us -> none  [merged(): pieces = jax.tree.map(lambda part: lax.all_gather(part, axis), value)]
    all_to_all x0 -> x2, starting transfers between devices: none -> 16.8 us  [the longest x1 9.43 us: gather_pool(): lax.all_to_all(copies, 'pool', split_axis=0, concat_axis=0, tiled=True)]
    slice x6 -> x1, local copies, waits for them, and re-layouts: 13 us -> 0.02 us  [on_device(): landed[:, :, query_width:query_width + 6 * head_count].astype(jnp.float32)]
    all_to_all x0 -> x2, waiting for transfers between devices: none -> 9.78 us  [the longest x1 9.78 us: on_device(): lax.all_to_all(parcel, 'pool', split_axis=0, concat_axis=0, tiled=True)]
  transfers between devices with their start and end apart: 4 -> 6, of which waited for: 4 -> 5; matrix products, arithmetic and copies ran while one was open for 1% -> 25% of each run, Pallas kernels for 0% -> 0%
where the time goes in v1:
time: 120 us; the launch traced here: 119 us
  waiting for transfers between devices  31.4 us (26%)
  starting transfers between devices  29.9 us (25%)
  local copies, waits for them, and re-layouts  22.3 us (19%)
  matrix products  21.4 us (18%)
  other arithmetic  13.2 us (11%)
    unnamed x18, local copies, waits for them, and re-layouts  14 us
    all_to_all x1, waiting for transfers between devices, on_device(): lax.all_to_all(outgoing, 'pool', split_axis=0, concat_axis=0, tiled=True)  11 us
    all_to_all x1, waiting for transfers between devices, on_device(): lax.all_to_all(parcel, 'pool', split_axis=0, concat_axis=0, tiled=True)  9.78 us
    all_to_all x1, starting transfers between devices, gather_pool(): lax.all_to_all(copies, 'pool', split_axis=0, concat_axis=0, tiled=True)  9.43 us
    all_to_all x1, waiting for transfers between devices, on_device(): lax.all_to_all(expert_out, 'pool', split_axis=0, concat_axis=0, tiled=True)  7.38 us
    all_to_all x1, starting transfers between devices, on_device(): lax.all_to_all(parcel, 'pool', split_axis=0, concat_axis=0, tiled=True)  7.37 us
    reduce_sum x1, other arithmetic, on_device(): jnp.sum(jnp.where(flat_ids[None, :] == global_slot[:, None], entry_index[...  6.7 us
    all_to_all x1, starting transfers between devices, on_device(): lax.all_to_all(outgoing, 'pool', split_axis=0, concat_axis=0, tiled=True)  5.36 us
  transfers between devices with their start and end apart: 6, of which 5 were waited for; matrix products, arithmetic and copies ran while one was open for 25% of the time, Pallas kernels for 0%

profile of v1, /device:TPU:1, one launch (start us, length us, event | category | flops | bytes accessed | tf_op | source)
XLA Modules:
  0.0 118.7 jit_solution(10264509838345780731)
XLA Ops:
  1.7 1.3 %convolution_convert_fusion.6 = bf16[16,256]{1,0:T(8,128)(2,1)S(1)} fusion(bf16[1024,256]{1,0:T(8,128)(2,1)} %param.24, bf16[16,1024]{1,0:T(8,128)(2,1)} %param.17, f32[1024]{0:T(1024)S(1)} %convert_element_type.89, f32[16]{0:T(128)S(1)} %add_rsqrt_fusion.1), kind=kOutput, calls=%fused_computation.22 | convolution fusion | flops 8458240 | bytes 569408 | tf_op jit(solution)/shard_map/dot_general | solution.py:68
  3.7 9.4 %all-to-all-start = ((bf16[32,16,256]{2,1,0:T(8,128)(2,1)}), bf16[32,16,256]{2,1,0:T(8,128)(2,1)S(1)}, u32[]{:S(2)}, u32[]{:S(2)}) async-start(bf16[32,16,256]{2,1,0:T(8,128)(2,1)} %broadcast_in_dim.119), calls=%async_computation | async-start | bytes 524288 | tf_op jit(solution)/shard_map/all_to_all | solution.py:17
  13.2 6.7 %select_reduce_fusion = s32[144]{0:T(256)S(1)} fusion(s32[65536]{0:T(1024)} %bitcast.70, s32[144]{0:T(256)S(1)} %iota_add_fusion), kind=kLoop, calls=%fused_computation | loop fusion | flops 28311408 | bytes 263296 | tf_op jit(solution)/shard_map/reduce_sum | solution.py:94
  19.9 3.5 %convolution_convert_fusion.1 = bf16[2048,128]{1,0:T(8,128)(2,1)S(1)} fusion(bf16[2048,1024]{1,0:T(8,128)(2,1)} %bitcast.72, bf16[1024,128]{1,0:T(8,128)(2,1)} %param.25), kind=kOutput, calls=%fused_computation.10 | convolution fusion | flops 537133056 | bytes 4980736 | tf_op jit(solution)/shard_map/dot_general | solution.py:73
  23.4 1.3 %convolution_convert_fusion = bf16[2048,128]{1,0:T(8,128)(2,1)S(1)} fusion(bf16[2048,1024]{1,0:T(8,128)(2,1)S(1)} %bitcast.73, bf16[1024,128]{1,0:T(8,128)(2,1)S(1)} %copy-done.5), kind=kOutput, calls=%fused_computation.9 | convolution fusion | flops 537133056 | bytes 4980736 | tf_op jit(solution)/shard_map/dot_general | solution.py:78
  26.1 6.4 %copy.102 = bf16[128,128,128]{1,2,0:T(8,128)(2,1)} copy(bf16[128,128,128]{2,1,0:T(8,128)(2,1)} %param.20) | data formatting | bytes 8388608 | tf_op args[3]
  33.6 6.4 %copy.105 = bf16[128,128,128]{1,2,0:T(8,128)(2,1)} copy(bf16[128,128,128]{2,1,0:T(8,128)(2,1)} %param.21) | data formatting | bytes 8388608 | tf_op args[4]
  40.6 3.7 %fusion.68 = (f32[144,2,2]{2,1,0:T(2,128)S(1)}, f32[144,2,2,128]{3,2,1,0:T(2,128)S(1)}) fusion(bf16[144,2,2,64]{3,2,1,0:T(2,128)(2,1)S(1)} %reshape.201, bf16[16,128,2,64]{1,3,2,0:T(8,128)(2,1)S(1)} %copy.104, bf16[128,128,2,64]{1,3,2,0:T(8,128)(2,1)} %bitcast.67, pred[144,128]{1,0:T(8,128)(4,1)S(1)} %add_compare_fusion), kind=kOutput, calls=%fused_computation.114 | convolution fusion | flops 12017088 | bytes 5107968 | tf_op jit(solution)/shard_map/sgqd,stgd->sgqt/dot_general | solution.py:109
  44.9 0.9 fusion.61
  46.8 4.8 %fusion.4 = f32[144,2,2,64]{3,2,1,0:T(2,128)S(1)} fusion(bf16[16,128,2,64]{1,3,2,0:T(8,128)(2,1)S(1)} %copy.107, bf16[128,128,2,64]{1,3,2,0:T(8,128)(2,1)} %bitcast.66, f32[144,2,2,128]{3,2,1,0:T(2,128)S(1)} %get-tuple-element.18, pred[144,128]{1,0:T(8,128)(4,1)S(1)} %add_compare_fusion, f32[144,2,2]{2,1,0:T(2,128)S(1)} %get-tuple-element.17), kind=kOutput, calls=%fused_computation.5 | convolution fusion | flops 12017664 | bytes 5181696 | tf_op jit(solution)/shard_map/sgqt,stgd->sgqd/dot_general | solution.py:118
  53.4 7.4 %all-to-all-start.1 = ((bf16[32,16,384]{2,1,0:T(8,128)(2,1)}), bf16[32,16,384]{2,1,0:T(8,128)(2,1)S(1)}, u32[]{:S(2)}, u32[]{:S(2)}) async-start(bf16[32,16,384]{2,1,0:T(8,128)(2,1)} %bitcast.5), calls=%async_computation.1 | async-start | bytes 786432 | tf_op jit(solution)/shard_map/all_to_all | solution.py:140
  61.3 9.8 %all-to-all-done.1 = bf16[32,16,384]{2,1,0:T(8,128)(2,1)S(1)} async-done(((bf16[32,16,384]{2,1,0:T(8,128)(2,1)}), bf16[32,16,384]{2,1,0:T(8,128)(2,1)S(1)}, u32[]{:S(2)}, u32[]{:S(2)}) %all-to-all-start.1) | async-done | bytes 393248 | tf_op jit(solution)/shard_map/all_to_all | solution.py:140
  74.8 1.3 %collective-permute-start = (f32[16,1024]{1,0:T(8,128)S(1)}, f32[16,1024]{1,0:T(8,128)S(1)}, u32[]{:S(2)}, u32[]{:S(2)}) collective-permute-start(f32[16,1024]{1,0:T(8,128)S(1)} %fusion.58), channel_id=1, source_target_pairs={{0,1},{1,0},{2,3},{3,2},{4,5},{5,4},{6,7},{7,6},{8,9},{9,8},{10,11... | collective-permute-start | bytes 196616 | tf_op jit(solution)/shard_map/ppermute | solution.py:24
  76.8 1.8 %collective-permute-done = f32[16,1024]{1,0:T(8,128)S(1)} collective-permute-done((f32[16,1024]{1,0:T(8,128)S(1)}, f32[16,1024]{1,0:T(8,128)S(1)}, u32[]{:S(2)}, u32[]{:S(2)}) %collective-permute-start) | collective-permute-done | bytes 65568 | tf_op jit(solution)/shard_map/ppermute | solution.py:24
  78.6 2.8 %collective-permute-start.1 = (f32[16,1024]{1,0:T(8,128)S(1)}, f32[16,1024]{1,0:T(8,128)S(1)}, u32[]{:S(2)}, u32[]{:S(2)}) collective-permute-start(f32[16,1024]{1,0:T(8,128)S(1)} %add.113), channel_id=1, source_target_pairs={{0,3},{3,0},{1,2},{2,1},{4,7},{7,4},{5,6},{6,5},{8,11},{11,8},{9,1... | collective-permute-start | bytes 196616 | tf_op jit(solution)/shard_map/ppermute | solution.py:25
  81.6 1.5 %collective-permute-done.1 = f32[16,1024]{1,0:T(8,128)S(1)} collective-permute-done((f32[16,1024]{1,0:T(8,128)S(1)}, f32[16,1024]{1,0:T(8,128)S(1)}, u32[]{:S(2)}, u32[]{:S(2)}) %collective-permute-start.1) | collective-permute-done | bytes 65568 | tf_op jit(solution)/shard_map/ppermute | solution.py:25
  83.1 0.9 multiply_reduce_fusion.1
  84.0 1.1 fusion.8
  85.1 5.4 %all-to-all-start.2 = ((bf16[32,8,1024]{2,1,0:T(8,128)(2,1)}), bf16[32,8,1024]{2,1,0:T(8,128)(2,1)S(1)}, u32[]{:S(2)}, u32[]{:S(2)}) async-start(bf16[32,8,1024]{2,1,0:T(8,128)(2,1)} %fusion.8), calls=%async_computation.2 | async-start | bytes 1048576 | tf_op jit(solution)/shard_map/all_to_all | solution.py:169
  91.3 11.0 %all-to-all-done.2 = bf16[32,8,1024]{2,1,0:T(8,128)(2,1)S(1)} async-done(((bf16[32,8,1024]{2,1,0:T(8,128)(2,1)}), bf16[32,8,1024]{2,1,0:T(8,128)(2,1)S(1)}, u32[]{:S(2)}, u32[]{:S(2)}) %all-to-all-start.2) | async-done | bytes 524320 | tf_op jit(solution)/shard_map/all_to_all | solution.py:169
  102.2 1.7 %fusion.16 = f32[256,512]{1,0:T(8,128)S(1)} fusion(bf16[1,1024,512]{2,1,0:T(8,128)(2,1)} %param.31, bf16[32,8,1024]{2,1,0:T(8,128)(2,1)S(1)} %all-to-all-done.2), kind=kOutput, calls=%fused_computation.25 | convolution fusion | flops 268435456 | bytes 2097152 | tf_op jit(solution)/shard_map/dot_general | solution.py:173
  103.9 2.0 %fusion.9 = bf16[32,8,1024]{2,1,0:T(8,128)(2,1)S(1)} fusion(bf16[1,512,1024]{2,1,0:T(8,128)(2,1)S(1)} %copy-done, bf16[1,1024,512]{2,1,0:T(8,128)(2,1)} %param.32, bf16[32,8,1024]{2,1,0:T(8,128)(2,1)S(1)} %all-to-all-done.2, f32[256,512]{1,0:T(8,128)S(1)} %fusion.16), kind=kOutput, calls=%fused_computation.15 | convolution fusion | flops 537919488 | bytes 3670016 | tf_op jit(solution)/shard_map/dot_general | solution.py:176
  106.6 3.6 %all-to-all-start.3 = ((bf16[32,8,256]{2,1,0:T(8,128)(2,1)}), bf16[32,8,256]{2,1,0:T(8,128)(2,1)S(1)}, u32[]{:S(2)}, u32[]{:S(2)}) async-start(bf16[32,8,256]{2,1,0:T(8,128)(2,1)} %constant_dynamic-slice_fusion), calls=%async_computation.3 | async-start | bytes 262144 | tf_op jit(solution)/shard_map/all_to_all | solution.py:179
  110.5 7.4 %all-to-all-done.3 = bf16[32,8,256]{2,1,0:T(8,128)(2,1)S(1)} async-done(((bf16[32,8,256]{2,1,0:T(8,128)(2,1)}), bf16[32,8,256]{2,1,0:T(8,128)(2,1)S(1)}, u32[]{:S(2)}, u32[]{:S(2)}) %all-to-all-start.3) | async-done | bytes 131104 | tf_op jit(solution)/shard_map/all_to_all | solution.py:179
  (75 shorter events, 16.4 us)
Async XLA Ops:
  0.0 103.9 %copy-start = (bf16[1,512,1024]{2,1,0:T(8,128)(2,1)S(1)}, bf16[1,512,1024]{2,1,0:T(8,128)(2,1)}, u32[]{:S(2)}) copy-start(bf16[1,512,1024]{2,1,0:T(8,128)(2,1)} %param.33) | copy-start | bytes 3145732
  0.0 23.4 %copy-start.5 = (bf16[1024,128]{1,0:T(8,128)(2,1)S(1)}, bf16[1024,128]{1,0:T(8,128)(2,1)}, u32[]{:S(2)}) copy-start(bf16[1024,128]{1,0:T(8,128)(2,1)} %param.26) | copy-start | bytes 786436
  3.7 36.6 %all-to-all-start = ((bf16[32,16,256]{2,1,0:T(8,128)(2,1)}), bf16[32,16,256]{2,1,0:T(8,128)(2,1)S(1)}, u32[]{:S(2)}, u32[]{:S(2)}) async-start(bf16[32,16,256]{2,1,0:T(8,128)(2,1)} %broadcast_in_dim.119), calls=%async_computation | async-start | bytes 524288 | tf_op jit(solution)/shard_map/all_to_all | solution.py:17
  13.1 10.2 %copy-start.4 = (bf16[16,128,1024]{2,1,0:T(8,128)(2,1)S(1)}, bf16[16,128,1024]{2,1,0:T(8,128)(2,1)}, u32[]{:S(2)}) copy-start(bf16[16,128,1024]{2,1,0:T(8,128)(2,1)} %param.22) | copy-start | bytes 12582916
  23.4 1.3 %copy-start.3 = (s32[512]{0:T(512)S(1)}, s32[512]{0:T(512)}, u32[]{:S(2)}) copy-start(s32[512]{0:T(512)} %param.19) | copy-start | bytes 6148
  33.6 6.4 %copy-start.2 = (s32[16,8]{0,1:T(8,128)S(1)}, s32[16,8]{0,1:T(8,128)}, u32[]{:S(2)}) copy-start(s32[16,8]{0,1:T(8,128)} %param.29) | copy-start | bytes 1540
  52.2 22.4 %copy-start.1 = (bf16[256,1024]{1,0:T(8,128)(2,1)S(1)}, bf16[256,1024]{1,0:T(8,128)(2,1)}, u32[]{:S(2)}) copy-start(bf16[256,1024]{1,0:T(8,128)(2,1)} %param.27) | copy-start | bytes 1572868
  53.4 17.7 %all-to-all-start.1 = ((bf16[32,16,384]{2,1,0:T(8,128)(2,1)}), bf16[32,16,384]{2,1,0:T(8,128)(2,1)S(1)}, u32[]{:S(2)}, u32[]{:S(2)}) async-start(bf16[32,16,384]{2,1,0:T(8,128)(2,1)} %bitcast.5), calls=%async_computation.1 | async-start | bytes 786432 | tf_op jit(solution)/shard_map/all_to_all | solution.py:140
  74.8 3.8 %collective-permute-start = (f32[16,1024]{1,0:T(8,128)S(1)}, f32[16,1024]{1,0:T(8,128)S(1)}, u32[]{:S(2)}, u32[]{:S(2)}) collective-permute-start(f32[16,1024]{1,0:T(8,128)S(1)} %fusion.58), channel_id=1, source_target_pairs={{0,1},{1,0},{2,3},{3,2},{4,5},{5,4},{6,7},{7,6},{8,9},{9,8},{10,11... | collective-permute-start | bytes 196616 | tf_op jit(solution)/shard_map/ppermute | solution.py:24
  78.6 4.5 %collective-permute-start.1 = (f32[16,1024]{1,0:T(8,128)S(1)}, f32[16,1024]{1,0:T(8,128)S(1)}, u32[]{:S(2)}, u32[]{:S(2)}) collective-permute-start(f32[16,1024]{1,0:T(8,128)S(1)} %add.113), channel_id=1, source_target_pairs={{0,3},{3,0},{1,2},{2,1},{4,7},{7,4},{5,6},{6,5},{8,11},{11,8},{9,1... | collective-permute-start | bytes 196616 | tf_op jit(solution)/shard_map/ppermute | solution.py:25
  85.1 17.1 %all-to-all-start.2 = ((bf16[32,8,1024]{2,1,0:T(8,128)(2,1)}), bf16[32,8,1024]{2,1,0:T(8,128)(2,1)S(1)}, u32[]{:S(2)}, u32[]{:S(2)}) async-start(bf16[32,8,1024]{2,1,0:T(8,128)(2,1)} %fusion.8), calls=%async_computation.2 | async-start | bytes 1048576 | tf_op jit(solution)/shard_map/all_to_all | solution.py:169
  106.6 11.3 %all-to-all-start.3 = ((bf16[32,8,256]{2,1,0:T(8,128)(2,1)}), bf16[32,8,256]{2,1,0:T(8,128)(2,1)S(1)}, u32[]{:S(2)}, u32[]{:S(2)}) async-start(bf16[32,8,256]{2,1,0:T(8,128)(2,1)} %constant_dynamic-slice_fusion), calls=%async_computation.3 | async-start | bytes 262144 | tf_op jit(solution)/shard_map/all_to_all | solution.py:179

commit v2 on v1

--- a/solution.py
+++ b/solution.py
@@ -1,6 +1,8 @@
 import jax
 import jax.numpy as jnp
 from jax import lax
+from jax.experimental import pallas as pl
+from jax.experimental.pallas import tpu as pltpu
 from jax.sharding import PartitionSpec as P
 
 HEAD_SIZE = 64
@@ -26,10 +28,176 @@
 
 
 def split_three(value):
-    high = lax.reduce_precision(value, 8, 7)
+    high = value.astype(jnp.bfloat16).astype(jnp.float32)
     rest = value - high
-    middle = lax.reduce_precision(rest, 8, 7)
-    return [part.astype(jnp.bfloat16) for part in (high, middle, rest - middle)]
+    middle = rest.astype(jnp.bfloat16).astype(jnp.float32)
+    return high, middle, rest - middle
+
+
+HEADS = 4
+QUAD = 4
+ROWS = HEADS * QUAD
+CHUNK = 64
+
+
+def attend_kernel(k_ref, v_ref, kn_ref, vn_ref, q_ref, cols_ref, req_ref, out_ref, qs, sc, ob, cb):
+    rows, page_len = sc.shape
+    requests = q_ref.shape[0]
+    half = page_len // 2
+    old_quads = k_ref.shape[0] // QUAD
+    quads = rows // ROWS
+
+    def head_of(shape):
+        return lax.broadcasted_iota(jnp.int32, shape, 0) % HEADS
+
+    def lane_of(shape):
+        return lax.broadcasted_iota(jnp.int32, shape, 1)
+
+    for c in range(rows // CHUNK):
+        at = slice(c * CHUNK, (c + 1) * CHUNK)
+        hit = cols_ref[at, 0:1] == lane_of((CHUNK, requests))
+        picked = jnp.dot(
+            jnp.where(hit, 1.0, 0.0).astype(jnp.bfloat16),
+            q_ref[...],
+            preferred_element_type=jnp.float32,
+        )
+        low, high = picked[:, :page_len], picked[:, page_len:]
+        head = head_of((CHUNK, page_len))
+        first = lane_of((CHUNK, page_len)) < half
+        near = jnp.where(head == 0, low, pltpu.roll(low, half, 1))
+        far = jnp.where(head == 2, pltpu.roll(high, half, 1), high)
+        keep = first == (head < 2)
+        qs[at, :] = jnp.where(keep, jnp.where(head < 2, near, far), 0.0).astype(jnp.bfloat16)
+
+    quad_row = lax.broadcasted_iota(jnp.int32, (ROWS, page_len), 0) // HEADS
+
+    def score(i, keys):
+        q16 = qs[pl.ds(pl.multiple_of(i * ROWS, ROWS), ROWS), :]
+        wide = lax.dot_general(
+            q16,
+            keys.reshape(QUAD * page_len, page_len),
+            (((1,), (1,)), ((), ())),
+            preferred_element_type=jnp.float32,
+        )
+        got = wide[:, :page_len]
+        for n in range(1, QUAD):
+            got = jnp.where(quad_row == n, wide[:, n * page_len : (n + 1) * page_len], got)
+        sc[pl.ds(pl.multiple_of(i * ROWS, ROWS), ROWS), :] = got * SCORE_SCALE
+
+    @pl.loop(0, old_quads, step=4)
+    def _(i):
+        for n in range(4):
+            score(i + n, k_ref[pl.ds((i + n) * QUAD, QUAD)])
+
+    for i in range(old_quads, quads):
+        score(i, kn_ref[(i - old_quads) * QUAD : (i - old_quads + 1) * QUAD])
+
+    tops, sums = [], []
+    ceiling = jnp.full((8, requests), NEG_FILL, jnp.float32)
+    for c in range(rows // CHUNK):
+        at = slice(c * CHUNK, (c + 1) * CHUNK)
+        valid = lane_of((CHUNK, page_len)) < cols_ref[at, 1:2]
+        masked = jnp.where(valid, sc[at, :], NEG_FILL)
+        top = jnp.max(masked, axis=1, keepdims=True)
+        weight = jnp.where(valid, jnp.exp(masked - top), 0.0)
+        sc[at, :] = weight
+        tops.append(top)
+        sums.append(jnp.sum(weight, axis=1, keepdims=True))
+        hit = cols_ref[at, 0:1] == lane_of((CHUNK, requests))
+        spread = jnp.where(hit, top, NEG_FILL).reshape(CHUNK // 8, 8, requests)
+        ceiling = jnp.maximum(ceiling, jnp.max(spread, axis=0))
+    ceiling = jnp.maximum(ceiling, pltpu.roll(ceiling, HEADS, 0))
+
+    def blend(i, values):
+        p16 = sc[pl.ds(pl.multiple_of(i * ROWS, ROWS), ROWS), :]
+        parts = [jnp.where(quad_row == n, p16, 0.0) for n in range(QUAD)]
+        sc[pl.ds(pl.multiple_of(i * ROWS, ROWS), ROWS), :] = jnp.dot(
+            jnp.concatenate(parts, axis=1).astype(jnp.bfloat16),
+            values.reshape(QUAD * page_len, page_len),
+            preferred_element_type=jnp.float32,
+        )
+
+    @pl.loop(0, old_quads, step=4)
+    def _(i):
+        for n in range(4):
+            blend(i + n, v_ref[pl.ds((i + n) * QUAD, QUAD)])
+
+    for i in range(old_quads, quads):
+        blend(i, vn_ref[(i - old_quads) * QUAD : (i - old_quads + 1) * QUAD])
+
+    ob[rows:, :] = jnp.zeros((ob.shape[0] - rows, ob.shape[1]), ob.dtype)
+    cb[rows:, :] = jnp.zeros((cb.shape[0] - rows, cb.shape[1]), cb.dtype)
+    for c in range(rows // CHUNK):
+        at = slice(c * CHUNK, (c + 1) * CHUNK)
+        hit = cols_ref[at, 0:1] == lane_of((CHUNK, requests))
+        limit = jnp.broadcast_to(ceiling[None], (CHUNK // 8, 8, requests))
+        own = jnp.max(
+            jnp.where(hit, limit.reshape(CHUNK, requests), NEG_FILL), axis=1, keepdims=True
+        )
+        factor = jnp.exp(tops[c] - own)
+        value = sc[at, :] * factor
+        turned = pltpu.roll(value, half, 1)
+        head = head_of((CHUNK, page_len))
+        lane = lane_of((CHUNK, page_len))
+        first = lane < half
+        low = jnp.where(first, jnp.where(head == 0, value, 0.0), jnp.where(head == 1, turned, 0.0))
+        high = jnp.where(first, jnp.where(head == 2, turned, 0.0), jnp.where(head == 3, value, 0.0))
+        ob[at, :page_len] = low.astype(jnp.bfloat16)
+        ob[at, page_len:] = high.astype(jnp.bfloat16)
+        stats = jnp.zeros((CHUNK, page_len), jnp.float32)
+        leader = jnp.where(cols_ref[at, 2:3] > 0, own, 0.0)
+        pieces = split_three(sums[c] * factor) + split_three(leader)
+        for n, piece in enumerate(pieces):
+            stats = jnp.where(lane == n * HEADS + head, piece, stats)
+        cb[at, :] = stats.astype(jnp.bfloat16)
+
+    step = requests // 4
+    for c in range(4):
+        at = slice(c * step, (c + 1) * step)
+        owner = lax.broadcasted_iota(jnp.int32, (step, ob.shape[0]), 0) + c * step
+        member = jnp.where(owner == req_ref[0:1, :], 1.0, 0.0).astype(jnp.bfloat16)
+        total = jnp.dot(member, ob[...], preferred_element_type=jnp.float32)
+        out_ref[at, : 2 * page_len] = total.astype(jnp.bfloat16)
+        stats = jnp.dot(member, cb[...], preferred_element_type=jnp.float32)
+        lane = lane_of((step, page_len))
+        joined = (
+            stats
+            + pltpu.roll(stats, page_len - HEADS, 1)
+            + pltpu.roll(stats, page_len - 2 * HEADS, 1)
+        )
+        high, middle, rest = split_three(joined)
+        middle, rest = pltpu.roll(middle, HEADS, 1), pltpu.roll(rest, 2 * HEADS, 1)
+        stats = jnp.where(lane < 3 * HEADS, rest, stats)
+        stats = jnp.where(lane < 2 * HEADS, middle, stats)
+        stats = jnp.where(lane < HEADS, high, stats)
+        out_ref[at, 2 * page_len :] = stats.astype(jnp.bfloat16)
+
+
+def attend(k_cache, v_cache, key_new, value_new, all_queries, columns, owner_row):
+    slots = k_cache.shape[0] + key_new.shape[0]
+    page_len, width = k_cache.shape[1:]
+    rows = slots * HEADS
+    padded = owner_row.shape[1]
+    requests = all_queries.shape[0]
+    return pl.pallas_call(
+        attend_kernel,
+        out_shape=jax.ShapeDtypeStruct((requests, 3 * width), jnp.bfloat16),
+        in_specs=[pl.BlockSpec(memory_space=pltpu.VMEM)] * 7,
+        out_specs=pl.BlockSpec(memory_space=pltpu.VMEM),
+        scratch_shapes=[
+            pltpu.VMEM((rows, width), jnp.bfloat16),
+            pltpu.VMEM((rows, page_len), jnp.float32),
+            pltpu.VMEM((padded, 2 * width), jnp.bfloat16),
+            pltpu.VMEM((padded, width), jnp.bfloat16),
+        ],
+        compiler_params=pltpu.CompilerParams(vmem_limit_bytes=40 << 20),
+        cost_estimate=pl.CostEstimate(
+            flops=4 * slots * ROWS * page_len * width * 4,
+            bytes_accessed=4 * slots * page_len * width + (2 << 20),
+            transcendentals=rows * page_len,
+        ),
+        name="attend",
+    )(k_cache, v_cache, key_new, value_new, all_queries, columns, owner_row)
 
 
 def rms_scale(row_vals, gain_row):
@@ -79,12 +247,9 @@
         .astype(jnp.bfloat16)
         .reshape(stored_shape)
     )
-    keys_here = jnp.concatenate([k_cache, key_new], axis=0)
-    values_here = jnp.concatenate([v_cache, value_new], axis=0)
-    slot_count, page_len, key_width = keys_here.shape
+    slot_count = k_cache.shape[0] + key_new.shape[0]
+    page_len = k_cache.shape[1]
     query_width = queries.shape[1]
-    kv_groups = key_width // HEAD_SIZE
-    per_group = query_width // key_width
     head_count = query_width // HEAD_SIZE
     requests = block_table.shape[0]
     list_len = block_table.shape[1]
@@ -97,54 +262,26 @@
     slot_req = found_entry // list_len
     slot_block = found_entry % list_len
     member = slot_req[:, None] == jnp.arange(requests, dtype=jnp.int32)[None, :]
-    member_low = member.astype(jnp.bfloat16)
-    slot_queries = jnp.dot(member_low, all_queries, preferred_element_type=jnp.float32).astype(
-        jnp.bfloat16
-    )
     slot_length = jnp.sum(jnp.where(member, lengths[None, :], 0), axis=1)
-    q_grouped = slot_queries.reshape(slot_count, kv_groups, per_group, HEAD_SIZE)
-    k_grouped = keys_here.reshape(slot_count, page_len, kv_groups, HEAD_SIZE)
-    v_grouped = values_here.reshape(slot_count, page_len, kv_groups, HEAD_SIZE)
-    scores = (
-        jnp.einsum("sgqd,stgd->sgqt", q_grouped, k_grouped, preferred_element_type=jnp.float32)
-        * SCORE_SCALE
-    )
-    positions = slot_block[:, None] * page_len + jnp.arange(page_len, dtype=jnp.int32)[None, :]
-    is_valid = (positions < slot_length[:, None])[:, None, None, :]
-    masked = jnp.where(is_valid, scores, NEG_FILL)
-    block_top = jnp.max(masked, axis=-1)
-    weights = jnp.where(is_valid, jnp.exp(masked - block_top[..., None]), 0.0)
-    block_sum = jnp.sum(weights, axis=-1)
-    block_out = jnp.einsum(
-        "sgqt,stgd->sgqd",
-        weights.astype(jnp.bfloat16),
-        v_grouped,
-        preferred_element_type=jnp.float32,
-    )
-    slot_top = block_top.reshape(slot_count, head_count)
-    slot_sum = block_sum.reshape(slot_count, head_count)
-    slot_out = block_out.reshape(slot_count, query_width)
-    local_top = jnp.max(jnp.where(member[:, :, None], slot_top[:, None, :], NEG_FILL), axis=0)
-    own_top = jnp.max(jnp.where(member[:, :, None], local_top[None, :, :], NEG_FILL), axis=1)
-    factor = jnp.exp(slot_top - own_top)
-    one_hot = member.astype(jnp.float32)
-    local_sum = jnp.einsum("sr,sh->rh", one_hot, slot_sum * factor, precision=HIGHEST)
-    scaled_out = (slot_out * jnp.repeat(factor, HEAD_SIZE, axis=1)).astype(jnp.bfloat16)
-    local_out = jnp.einsum(
-        "sr,sc->rc", member_low, scaled_out, preferred_element_type=jnp.float32
-    ).astype(jnp.bfloat16)
-    pieces = split_three(local_top) + split_three(local_sum)
-    parcel = jnp.concatenate([local_out] + pieces, axis=1)
-    parcel = jnp.pad(parcel, ((0, 0), (0, -parcel.shape[1] % 128)))
+    slot_ids = jnp.arange(slot_count, dtype=jnp.int32)
+    earlier = (slot_req[:, None] == slot_req[None, :]) & (slot_ids[None, :] < slot_ids[:, None])
+    leads = 1 - jnp.max(earlier.astype(jnp.int32), axis=1)
+    columns = jnp.stack([slot_req, slot_length - slot_block * page_len, leads], axis=1)
+    columns = jnp.repeat(columns, head_count, axis=0)
+    owner_row = jnp.pad(
+        jnp.repeat(slot_req, head_count), (0, -slot_count * head_count % 128), constant_values=-1
+    )[None, :]
+    parcel = attend(k_cache, v_cache, key_new, value_new, all_queries, columns, owner_row)
     parcel = parcel.reshape(pool_count, req_dev, -1)
     landed = lax.all_to_all(parcel, "pool", split_axis=0, concat_axis=0, tiled=True)
     part_out = landed[:, :, :query_width].astype(jnp.float32)
     part_stats = landed[:, :, query_width : query_width + 6 * head_count].astype(jnp.float32)
     part_stats = part_stats.reshape(pool_count, req_dev, 2, 3, head_count)
     part_stats = part_stats[:, :, :, 0] + part_stats[:, :, :, 1] + part_stats[:, :, :, 2]
-    part_top = part_stats[:, :, 0]
+    part_sum = part_stats[:, :, 0]
+    part_top = jnp.where(part_sum > 0.0, part_stats[:, :, 1], NEG_FILL)
     part_weight = jnp.exp(part_top - jnp.max(part_top, axis=0, keepdims=True))
-    total_sum = jnp.sum(part_weight * part_stats[:, :, 1], axis=0)
+    total_sum = jnp.sum(part_weight * part_sum, axis=0)
     accum = jnp.sum(part_out * jnp.repeat(part_weight, HEAD_SIZE, axis=-1), axis=0)
     attended = (accum / jnp.repeat(total_sum, HEAD_SIZE, axis=-1)).astype(jnp.bfloat16)
     projected = sum_exp(jnp.dot(attended, w_out, preferred_element_type=jnp.float32))
@@ -173,9 +310,9 @@
     gate_act = jnp.dot(row_block, w_gate[0], preferred_element_type=jnp.float32)
     up_act = jnp.dot(row_block, w_up[0], preferred_element_type=jnp.float32)
     hidden = (jax.nn.silu(gate_act) * up_act).astype(jnp.bfloat16)
-    expert_low = jnp.dot(hidden, w_down[0], preferred_element_type=jnp.float32).astype(jnp.bfloat16)
-    expert_low = expert_low.reshape(sources, slots_here, model_width)
-    expert_out = lax.dynamic_slice_in_dim(expert_low, exp_index * quarter, quarter, 2)
+    down_share = lax.dynamic_slice_in_dim(w_down[0], exp_index * quarter, quarter, 1)
+    expert_low = jnp.dot(hidden, down_share, preferred_element_type=jnp.float32).astype(jnp.bfloat16)
+    expert_out = expert_low.reshape(sources, slots_here, quarter)
     returned = lax.all_to_all(expert_out, "pool", split_axis=0, concat_axis=0, tiled=True)
     moe_share = jnp.dot(
         combine_map,

time: 120 us -> 104 us (0.87)
  local copies, waits for them, and re-layouts: 22.3 us -> 8.88 us
  matrix products: 21.4 us -> 11.2 us
  Pallas kernels: 0 us -> 8.23 us
    dot_general x6 -> x1, matrix products: 11.4 us -> 2.23 us  [on_device(): jnp.dot(hidden, down_share, preferred_element_type=jnp.float32)]
    pallas_call x0 -> x1, Pallas kernels: none -> 8.23 us  [attend(): pl.pallas_call(attend_kernel, out_shape=jax.ShapeDtypeStruct((requests, 3...]
    unnamed x18, local copies, waits for them, and re-layouts: 14 us -> 6.2 us
    concatenate x5 -> x0, local copies, waits for them, and re-layouts: 2.3 us -> none  [the longest x2 1.07 us: on_device(): keys_here = jnp.concatenate([k_cache, key_new], axis=0)]
    dot_general x1, matrix products: 1.65 us -> 0.43 us  [on_device(): gate_act = jnp.dot(row_block, w_gate[0], preferred_element_type=jnp.float32)]
  transfers between devices with their start and end apart: 6 -> 6, of which waited for: 5 -> 5; matrix products, arithmetic and copies ran while one was open for 25% -> 16% of each run, Pallas kernels for 0% -> 0%
where the time goes in v2:
time: 104 us; the launch traced here: 103 us
  waiting for transfers between devices  31.5 us (30%)
  starting transfers between devices  30.1 us (29%)
  other arithmetic  13.2 us (13%)
  matrix products  11.2 us (11%)
  local copies, waits for them, and re-layouts  8.88 us (9%)
  Pallas kernels  8.23 us (8%)
    all_to_all x1, waiting for transfers between devices, on_device(): lax.all_to_all(outgoing, 'pool', split_axis=0, concat_axis=0, tiled=True)  11 us
    all_to_all x1, waiting for transfers between devices, on_device(): lax.all_to_all(parcel, 'pool', split_axis=0, concat_axis=0, tiled=True)  9.78 us
    all_to_all x1, starting transfers between devices, gather_pool(): lax.all_to_all(copies, 'pool', split_axis=0, concat_axis=0, tiled=True)  9.43 us
    pallas_call x1, Pallas kernels, attend(): pl.pallas_call(attend_kernel, out_shape=jax.ShapeDtypeStruct((requests, 3...  8.23 us
    all_to_all x1, starting transfers between devices, on_device(): lax.all_to_all(parcel, 'pool', split_axis=0, concat_axis=0, tiled=True)  7.52 us
    all_to_all x1, waiting for transfers between devices, on_device(): lax.all_to_all(expert_out, 'pool', split_axis=0, concat_axis=0, tiled=True)  7.38 us
    reduce_sum x1, other arithmetic, on_device(): jnp.sum(jnp.where(flat_ids[None, :] == global_slot[:, None], entry_index[...  6.55 us
    unnamed x18, local copies, waits for them, and re-layouts  6.2 us
  transfers between devices with their start and end apart: 6, of which 5 were waited for; matrix products, arithmetic and copies ran while one was open for 16% of the time, Pallas kernels for 0%

profile of v2, /device:TPU:1, one launch (start us, length us, event | category | flops | bytes accessed | tf_op | source)
XLA Modules:
  0.0 103.4 jit_solution(4919610871731925694)
XLA Ops:
  0.0 0.8 convert_element_type.60
  0.8 0.9 fusion.25
  1.7 1.3 %convolution_convert_fusion.3 = bf16[16,256]{1,0:T(8,128)(2,1)S(1)} fusion(bf16[1024,256]{1,0:T(8,128)(2,1)} %param.24, bf16[16,1024]{1,0:T(8,128)(2,1)} %param.17, f32[1024]{0:T(1024)S(1)} %convert_element_type.60, f32[16]{0:T(128)S(1)} %add_rsqrt_fusion.1), kind=kOutput, calls=%fused_computation.10 | convolution fusion | flops 8458240 | bytes 569408 | tf_op jit(solution)/shard_map/dot_general | solution.py:236
  3.7 9.4 %all-to-all-start = ((bf16[32,16,256]{2,1,0:T(8,128)(2,1)}), bf16[32,16,256]{2,1,0:T(8,128)(2,1)S(1)}, u32[]{:S(2)}, u32[]{:S(2)}) async-start(bf16[32,16,256]{2,1,0:T(8,128)(2,1)} %broadcast_in_dim.40), calls=%async_computation | async-start | bytes 524288 | tf_op jit(solution)/shard_map/all_to_all | solution.py:19
  13.1 6.6 %select_reduce_fusion = s32[144]{0:T(256)S(1)} fusion(s32[65536]{0:T(1024)} %bitcast.83, s32[144]{0:T(256)S(1)} %iota_add_fusion), kind=kLoop, calls=%fused_computation | loop fusion | flops 28311408 | bytes 263296 | tf_op jit(solution)/shard_map/reduce_sum | solution.py:259
  19.9 0.9 select_reduce_fusion.1
  22.0 3.6 %convolution_convert_fusion.1 = bf16[2048,128]{1,0:T(8,128)(2,1)S(1)} fusion(bf16[2048,1024]{1,0:T(8,128)(2,1)} %bitcast.88, bf16[1024,128]{1,0:T(8,128)(2,1)} %param.25), kind=kOutput, calls=%fused_computation.2 | convolution fusion | flops 537133056 | bytes 4980736 | tf_op jit(solution)/shard_map/dot_general | solution.py:241
  25.7 1.3 %convolution_convert_fusion = bf16[2048,128]{1,0:T(8,128)(2,1)S(1)} fusion(bf16[2048,1024]{1,0:T(8,128)(2,1)S(1)} %bitcast.89, bf16[1024,128]{1,0:T(8,128)(2,1)S(1)} %copy-done.6), kind=kOutput, calls=%fused_computation.1 | convolution fusion | flops 537133056 | bytes 4980736 | tf_op jit(solution)/shard_map/dot_general | solution.py:246
  27.0 2.2 %copy-done.1 = bf16[128,128,128]{2,1,0:T(8,128)(2,1)S(1)} copy-done((bf16[128,128,128]{2,1,0:T(8,128)(2,1)S(1)}, bf16[128,128,128]{2,1,0:T(8,128)(2,1)}, u32[]{:S(2)}) %copy-start.1) | copy-done | bytes 4194328
  29.2 2.2 %copy-done.2 = bf16[128,128,128]{2,1,0:T(8,128)(2,1)S(1)} copy-done((bf16[128,128,128]{2,1,0:T(8,128)(2,1)S(1)}, bf16[128,128,128]{2,1,0:T(8,128)(2,1)}, u32[]{:S(2)}) %copy-start.2) | copy-done | bytes 4194328
  31.4 8.2 %attend.1 = bf16[512,384]{1,0:T(8,128)(2,1)} custom-call(bf16[128,128,128]{2,1,0:T(8,128)(2,1)S(1)} %copy-done.1, bf16[128,128,128]{2,1,0:T(8,128)(2,1)S(1)} %copy-done.2, bf16[16,128,128]{2,1,0:T(8,128)(2,1)S(1)} %bitcast.80, bf16[16,128,128]{2,1,0:T(8,128)(2,1)S(1)} %bitcast.81, bf16[512,256]{1,0:T(8,128)(2,1)S(1)} %bitcast.79, s32[576,3]{1,0:T(8,128)S(1)} %bitcast.78, ...), custom_call_target="tpu_custom_call" | custom-call | flops 603979776 | bytes 11534336 | tf_op jit(solution)/shard_map/attend/pallas_call | solution.py:182
  39.6 7.5 %all-to-all-start.1 = ((bf16[32,16,384]{2,1,0:T(8,128)(2,1)}), bf16[32,16,384]{2,1,0:T(8,128)(2,1)S(1)}, u32[]{:S(2)}, u32[]{:S(2)}) async-start(bf16[32,16,384]{2,1,0:T(8,128)(2,1)} %bitcast.9), calls=%async_computation.1 | async-start | bytes 786432 | tf_op jit(solution)/shard_map/all_to_all | solution.py:276
  47.7 9.8 %all-to-all-done.1 = bf16[32,16,384]{2,1,0:T(8,128)(2,1)S(1)} async-done(((bf16[32,16,384]{2,1,0:T(8,128)(2,1)}), bf16[32,16,384]{2,1,0:T(8,128)(2,1)S(1)}, u32[]{:S(2)}, u32[]{:S(2)}) %all-to-all-start.1) | async-done | bytes 393248 | tf_op jit(solution)/shard_map/all_to_all | solution.py:276
  61.2 1.3 %collective-permute-start = (f32[16,1024]{1,0:T(8,128)S(1)}, f32[16,1024]{1,0:T(8,128)S(1)}, u32[]{:S(2)}, u32[]{:S(2)}) collective-permute-start(f32[16,1024]{1,0:T(8,128)S(1)} %fusion.45), channel_id=1, source_target_pairs={{0,1},{1,0},{2,3},{3,2},{4,5},{5,4},{6,7},{7,6},{8,9},{9,8},{10,11... | collective-permute-start | bytes 196616 | tf_op jit(solution)/shard_map/ppermute | solution.py:26
  63.2 1.8 %collective-permute-done = f32[16,1024]{1,0:T(8,128)S(1)} collective-permute-done((f32[16,1024]{1,0:T(8,128)S(1)}, f32[16,1024]{1,0:T(8,128)S(1)}, u32[]{:S(2)}, u32[]{:S(2)}) %collective-permute-start) | collective-permute-done | bytes 65568 | tf_op jit(solution)/shard_map/ppermute | solution.py:26
  65.0 2.8 %collective-permute-start.1 = (f32[16,1024]{1,0:T(8,128)S(1)}, f32[16,1024]{1,0:T(8,128)S(1)}, u32[]{:S(2)}, u32[]{:S(2)}) collective-permute-start(f32[16,1024]{1,0:T(8,128)S(1)} %add.104), channel_id=1, source_target_pairs={{0,3},{3,0},{1,2},{2,1},{4,7},{7,4},{5,6},{6,5},{8,11},{11,8},{9,1... | collective-permute-start | bytes 196616 | tf_op jit(solution)/shard_map/ppermute | solution.py:27
  67.9 1.5 %collective-permute-done.1 = f32[16,1024]{1,0:T(8,128)S(1)} collective-permute-done((f32[16,1024]{1,0:T(8,128)S(1)}, f32[16,1024]{1,0:T(8,128)S(1)}, u32[]{:S(2)}, u32[]{:S(2)}) %collective-permute-start.1) | collective-permute-done | bytes 65568 | tf_op jit(solution)/shard_map/ppermute | solution.py:27
  69.4 0.9 multiply_reduce_fusion.1
  70.3 1.1 %fusion = bf16[32,8,1024]{2,1,0:T(8,128)(2,1)} fusion(f32[16,1024]{1,0:T(8,128)S(1)} %get-tuple-element.6, f32[1024]{0:T(1024)S(1)} %convert_element_type.69, f32[16]{0:T(128)S(1)} %add_rsqrt_fusion, bf16[16,256]{1,0:T(8,128)(2,1)S(1)} %convert_reduce_fusion.1), kind=kOutput, calls=%fused_computation.4 | convolution fusion | flops 8699904 | bytes 602176 | tf_op jit(solution)/shard_map/tc,td->cd/dot_general | solution.py:304
  71.5 5.4 %all-to-all-start.2 = ((bf16[32,8,1024]{2,1,0:T(8,128)(2,1)}), bf16[32,8,1024]{2,1,0:T(8,128)(2,1)S(1)}, u32[]{:S(2)}, u32[]{:S(2)}) async-start(bf16[32,8,1024]{2,1,0:T(8,128)(2,1)} %fusion), calls=%async_computation.2 | async-start | bytes 1048576 | tf_op jit(solution)/shard_map/all_to_all | solution.py:306
  77.6 11.0 %all-to-all-done.2 = bf16[32,8,1024]{2,1,0:T(8,128)(2,1)S(1)} async-done(((bf16[32,8,1024]{2,1,0:T(8,128)(2,1)}), bf16[32,8,1024]{2,1,0:T(8,128)(2,1)S(1)}, u32[]{:S(2)}, u32[]{:S(2)}) %all-to-all-start.2) | async-done | bytes 524320 | tf_op jit(solution)/shard_map/all_to_all | solution.py:306
  89.0 2.2 %fusion.4 = bf16[32,8,256]{2,1,0:T(8,128)(2,1)} fusion(bf16[1,1024,512]{2,1,0:T(8,128)(2,1)S(1)} %copy-done.5, bf16[32,8,1024]{2,1,0:T(8,128)(2,1)S(1)} %all-to-all-done.2, f32[256,512]{1,0:T(8,128)S(1)} %fusion.7, bf16[1,512,1024]{2,1,0:T(8,128)(2,1)} %param.33, s32[]{:T(128)S(6)} %select_n.55), kind=kOutput, calls=%fused_computation.9 | convolution fusion | flops 336396288 | bytes 2490372 | tf_op jit(solution)/shard_map/dot_general | solution.py:314
  91.3 3.6 %all-to-all-start.3 = ((bf16[32,8,256]{2,1,0:T(8,128)(2,1)}), bf16[32,8,256]{2,1,0:T(8,128)(2,1)S(1)}, u32[]{:S(2)}, u32[]{:S(2)}) async-start(bf16[32,8,256]{2,1,0:T(8,128)(2,1)} %fusion.4), calls=%async_computation.3 | async-start | bytes 262144 | tf_op jit(solution)/shard_map/all_to_all | solution.py:316
  95.2 7.4 %all-to-all-done.3 = bf16[32,8,256]{2,1,0:T(8,128)(2,1)S(1)} async-done(((bf16[32,8,256]{2,1,0:T(8,128)(2,1)}), bf16[32,8,256]{2,1,0:T(8,128)(2,1)S(1)}, u32[]{:S(2)}, u32[]{:S(2)}) %all-to-all-start.3) | async-done | bytes 131104 | tf_op jit(solution)/shard_map/all_to_all | solution.py:316
  (56 shorter events, 9.4 us)
Async XLA Ops:
  0.0 88.6 %copy-start = (bf16[1,1024,512]{2,1,0:T(8,128)(2,1)S(1)}, bf16[1,1024,512]{2,1,0:T(8,128)(2,1)}, u32[]{:S(2)}) copy-start(bf16[1,1024,512]{2,1,0:T(8,128)(2,1)} %param.31) | copy-start | bytes 3145732
  0.0 25.6 %copy-start.6 = (bf16[1024,128]{1,0:T(8,128)(2,1)S(1)}, bf16[1024,128]{1,0:T(8,128)(2,1)}, u32[]{:S(2)}) copy-start(bf16[1024,128]{1,0:T(8,128)(2,1)} %param.26) | copy-start | bytes 786436
  3.7 23.3 %all-to-all-start = ((bf16[32,16,256]{2,1,0:T(8,128)(2,1)}), bf16[32,16,256]{2,1,0:T(8,128)(2,1)S(1)}, u32[]{:S(2)}, u32[]{:S(2)}) async-start(bf16[32,16,256]{2,1,0:T(8,128)(2,1)} %broadcast_in_dim.40), calls=%async_computation | async-start | bytes 524288 | tf_op jit(solution)/shard_map/all_to_all | solution.py:19
  22.0 3.6 %copy-start.4 = (bf16[16,128,1024]{2,1,0:T(8,128)(2,1)S(1)}, bf16[16,128,1024]{2,1,0:T(8,128)(2,1)}, u32[]{:S(2)}) copy-start(bf16[16,128,1024]{2,1,0:T(8,128)(2,1)} %param.22) | copy-start | bytes 12582916
  27.0 2.2 %copy-start.1 = (bf16[128,128,128]{2,1,0:T(8,128)(2,1)S(1)}, bf16[128,128,128]{2,1,0:T(8,128)(2,1)}, u32[]{:S(2)}) copy-start(bf16[128,128,128]{2,1,0:T(8,128)(2,1)} %k_ref.1) | copy-start | bytes 12582916
  29.2 2.2 %copy-start.2 = (bf16[128,128,128]{2,1,0:T(8,128)(2,1)S(1)}, bf16[128,128,128]{2,1,0:T(8,128)(2,1)}, u32[]{:S(2)}) copy-start(bf16[128,128,128]{2,1,0:T(8,128)(2,1)} %v_ref.1) | copy-start | bytes 12582916
  39.6 21.3 %copy-start.3 = (bf16[256,1024]{1,0:T(8,128)(2,1)S(1)}, bf16[256,1024]{1,0:T(8,128)(2,1)}, u32[]{:S(2)}) copy-start(bf16[256,1024]{1,0:T(8,128)(2,1)} %param.27) | copy-start | bytes 1572868
  39.6 17.8 %all-to-all-start.1 = ((bf16[32,16,384]{2,1,0:T(8,128)(2,1)}), bf16[32,16,384]{2,1,0:T(8,128)(2,1)S(1)}, u32[]{:S(2)}, u32[]{:S(2)}) async-start(bf16[32,16,384]{2,1,0:T(8,128)(2,1)} %bitcast.9), calls=%async_computation.1 | async-start | bytes 786432 | tf_op jit(solution)/shard_map/all_to_all | solution.py:276
  60.1 28.9 %copy-start.5 = (bf16[1,1024,512]{2,1,0:T(8,128)(2,1)S(1)}, bf16[1,1024,512]{2,1,0:T(8,128)(2,1)}, u32[]{:S(2)}) copy-start(bf16[1,1024,512]{2,1,0:T(8,128)(2,1)} %param.32) | copy-start | bytes 3145732
  61.2 3.8 %collective-permute-start = (f32[16,1024]{1,0:T(8,128)S(1)}, f32[16,1024]{1,0:T(8,128)S(1)}, u32[]{:S(2)}, u32[]{:S(2)}) collective-permute-start(f32[16,1024]{1,0:T(8,128)S(1)} %fusion.45), channel_id=1, source_target_pairs={{0,1},{1,0},{2,3},{3,2},{4,5},{5,4},{6,7},{7,6},{8,9},{9,8},{10,11... | collective-permute-start | bytes 196616 | tf_op jit(solution)/shard_map/ppermute | solution.py:26
  65.0 4.5 %collective-permute-start.1 = (f32[16,1024]{1,0:T(8,128)S(1)}, f32[16,1024]{1,0:T(8,128)S(1)}, u32[]{:S(2)}, u32[]{:S(2)}) collective-permute-start(f32[16,1024]{1,0:T(8,128)S(1)} %add.104), channel_id=1, source_target_pairs={{0,3},{3,0},{1,2},{2,1},{4,7},{7,4},{5,6},{6,5},{8,11},{11,8},{9,1... | collective-permute-start | bytes 196616 | tf_op jit(solution)/shard_map/ppermute | solution.py:27
  71.5 17.1 %all-to-all-start.2 = ((bf16[32,8,1024]{2,1,0:T(8,128)(2,1)}), bf16[32,8,1024]{2,1,0:T(8,128)(2,1)S(1)}, u32[]{:S(2)}, u32[]{:S(2)}) async-start(bf16[32,8,1024]{2,1,0:T(8,128)(2,1)} %fusion), calls=%async_computation.2 | async-start | bytes 1048576 | tf_op jit(solution)/shard_map/all_to_all | solution.py:306
  91.3 11.3 %all-to-all-start.3 = ((bf16[32,8,256]{2,1,0:T(8,128)(2,1)}), bf16[32,8,256]{2,1,0:T(8,128)(2,1)S(1)}, u32[]{:S(2)}, u32[]{:S(2)}) async-start(bf16[32,8,256]{2,1,0:T(8,128)(2,1)} %fusion.4), calls=%async_computation.3 | async-start | bytes 262144 | tf_op jit(solution)/shard_map/all_to_all | solution.py:316

commit v3 on v2

v3 whole, which is shorter than its diff:
```python
import jax
import jax.numpy as jnp
from jax import lax
from jax.experimental import pallas as pl
from jax.experimental.pallas import tpu as pltpu
from jax.sharding import PartitionSpec as P

HEAD_SIZE = 64


NEG_FILL = -1e30
EPSILON = 1e-05
SCORE_SCALE = 0.125
HIGHEST = lax.Precision.HIGHEST


def others(value, axis):
    size = lax.axis_size(axis)
    return [
        lax.ppermute(value, axis, [(i, (i + step) % size) for i in range(size)])
        for step in range(1, size)
    ]


def split_three(value):
    high = value.astype(jnp.bfloat16).astype(jnp.float32)
    rest = value - high
    middle = rest.astype(jnp.bfloat16).astype(jnp.float32)
    return high, middle, rest - middle


HEADS = 4
QUAD = 4
ROWS = HEADS * QUAD
CHUNK = 64
PARTS = 4


def attend_kernel(
    k_hbm, v_hbm, kn_hbm, vn_hbm, q_ref, cols_ref, req_ref, out_ref,
    k_ref, v_ref, kn_ref, vn_ref, qs, sc, ob, cb, sems,
):
    rows, page_len = sc.shape
    part = k_ref.shape[0] // PARTS
    copies = []
    streams = ((k_hbm, k_ref, kn_hbm, kn_ref), (v_hbm, v_ref, vn_hbm, vn_ref))
    for whole, held, new, new_held in streams:
        for c in range(PARTS):
            at = pl.ds(c * part, part)
            copies.append(
                pltpu.make_async_copy(whole.at[at], held.at[at], sems.at[len(copies)])
            )
        copies.append(pltpu.make_async_copy(new, new_held, sems.at[len(copies)]))
    for copy in copies:
        copy.start()
    requests = q_ref.shape[0]
    half = page_len // 2
    old_quads = k_ref.shape[0] // QUAD
    quads = rows // ROWS

    def head_of(shape):
        return lax.broadcasted_iota(jnp.int32, shape, 0) % HEADS

    def lane_of(shape):
        return lax.broadcasted_iota(jnp.int32, shape, 1)

    for c in range(rows // CHUNK):
        at = slice(c * CHUNK, (c + 1) * CHUNK)
        hit = cols_ref[at, 0:1] == lane_of((CHUNK, requests))
        picked = jnp.dot(
            jnp.where(hit, 1.0, 0.0).astype(jnp.bfloat16),
            q_ref[...],
            preferred_element_type=jnp.float32,
        )
        low, high = picked[:, :page_len], picked[:, page_len:]
        head = head_of((CHUNK, page_len))
        first = lane_of((CHUNK, page_len)) < half
        near = jnp.where(head == 0, low, pltpu.roll(low, half, 1))
        far = jnp.where(head == 2, pltpu.roll(high, half, 1), high)
        keep = first == (head < 2)
        qs[at, :] = jnp.where(keep, jnp.where(head < 2, near, far), 0.0).astype(jnp.bfloat16)

    quad_row = lax.broadcasted_iota(jnp.int32, (ROWS, page_len), 0) // HEADS

    def score(i, keys):
        q16 = qs[pl.ds(pl.multiple_of(i * ROWS, ROWS), ROWS), :]
        wide = lax.dot_general(
            q16,
            keys.reshape(QUAD * page_len, page_len),
            (((1,), (1,)), ((), ())),
            preferred_element_type=jnp.float32,
        )
        got = wide[:, :page_len]
        for n in range(1, QUAD):
            got = jnp.where(quad_row == n, wide[:, n * page_len : (n + 1) * page_len], got)
        sc[pl.ds(pl.multiple_of(i * ROWS, ROWS), ROWS), :] = got * SCORE_SCALE

    for c in range(PARTS):
        copies[c].wait()

        @pl.loop(c * old_quads // PARTS, (c + 1) * old_quads // PARTS, step=8)
        def _(i):
            for n in range(8):
                score(i + n, k_ref[pl.ds((i + n) * QUAD, QUAD)])

    copies[PARTS].wait()
    for i in range(old_quads, quads):
        score(i, kn_ref[(i - old_quads) * QUAD : (i - old_quads + 1) * QUAD])

    tops, sums = [], []
    ceiling = jnp.full((8, requests), NEG_FILL, jnp.float32)
    for c in range(rows // CHUNK):
        at = slice(c * CHUNK, (c + 1) * CHUNK)
        valid = lane_of((CHUNK, page_len)) < cols_ref[at, 1:2]
        masked = jnp.where(valid, sc[at, :], NEG_FILL)
        top = jnp.max(masked, axis=1, keepdims=True)
        weight = jnp.where(valid, jnp.exp(masked - top), 0.0)
        sc[at, :] = weight
        tops.append(top)
        sums.append(jnp.sum(weight, axis=1, keepdims=True))
        hit = cols_ref[at, 0:1] == lane_of((CHUNK, requests))
        spread = jnp.where(hit, top, NEG_FILL).reshape(CHUNK // 8, 8, requests)
        ceiling = jnp.maximum(ceiling, jnp.max(spread, axis=0))
    ceiling = jnp.maximum(ceiling, pltpu.roll(ceiling, HEADS, 0))

    ob[rows:, :] = jnp.zeros((ob.shape[0] - rows, ob.shape[1]), ob.dtype)
    cb[rows:, :] = jnp.zeros((cb.shape[0] - rows, cb.shape[1]), cb.dtype)
    factors = []
    for c in range(rows // CHUNK):
        at = slice(c * CHUNK, (c + 1) * CHUNK)
        hit = cols_ref[at, 0:1] == lane_of((CHUNK, requests))
        limit = jnp.broadcast_to(ceiling[None], (CHUNK // 8, 8, requests))
        own = jnp.max(
            jnp.where(hit, limit.reshape(CHUNK, requests), NEG_FILL), axis=1, keepdims=True
        )
        factor = jnp.exp(tops[c] - own)
        factors.append(factor)
        lane = lane_of((CHUNK, page_len))
        leader = jnp.where(cols_ref[at, 2:3] > 0, own, 0.0)
        pieces = split_three(jnp.where(lane < 3 * HEADS, sums[c] * factor, leader))
        turn = (lane // HEADS) % 3
        stats = jnp.where(turn == 0, pieces[0], jnp.where(turn == 1, pieces[1], pieces[2]))
        keep = (lane % HEADS == head_of((CHUNK, page_len))) & (lane < 6 * HEADS)
        cb[at, :] = jnp.where(keep, stats, 0.0).astype(jnp.bfloat16)

    step = requests // 4

    def member(c):
        owner = lax.broadcasted_iota(jnp.int32, (step, ob.shape[0]), 0) + c * step
        return jnp.where(owner == req_ref[0:1, :], 1.0, 0.0).astype(jnp.bfloat16)

    for c in range(4):
        stats = jnp.dot(member(c), cb[...], preferred_element_type=jnp.float32)
        lane = lane_of((step, page_len))
        joined = (
            stats
            + pltpu.roll(stats, page_len - HEADS, 1)
            + pltpu.roll(stats, page_len - 2 * HEADS, 1)
        )
        high, middle, rest = split_three(joined)
        middle, rest = pltpu.roll(middle, HEADS, 1), pltpu.roll(rest, 2 * HEADS, 1)
        stats = jnp.where(lane < 3 * HEADS, rest, stats)
        stats = jnp.where(lane < 2 * HEADS, middle, stats)
        stats = jnp.where(lane < HEADS, high, stats)
        out_ref[c * step : (c + 1) * step, 2 * page_len :] = stats.astype(jnp.bfloat16)

    def blend(i, values):
        p16 = sc[pl.ds(pl.multiple_of(i * ROWS, ROWS), ROWS), :]
        parts = [jnp.where(quad_row == n, p16, 0.0) for n in range(QUAD)]
        sc[pl.ds(pl.multiple_of(i * ROWS, ROWS), ROWS), :] = jnp.dot(
            jnp.concatenate(parts, axis=1).astype(jnp.bfloat16),
            values.reshape(QUAD * page_len, page_len),
            preferred_element_type=jnp.float32,
        )

    for c in range(PARTS):
        copies[c + PARTS + 1].wait()

        @pl.loop(c * old_quads // PARTS, (c + 1) * old_quads // PARTS, step=8)
        def _(i):
            for n in range(8):
                blend(i + n, v_ref[pl.ds((i + n) * QUAD, QUAD)])

    copies[2 * PARTS + 1].wait()
    for i in range(old_quads, quads):
        blend(i, vn_ref[(i - old_quads) * QUAD : (i - old_quads + 1) * QUAD])

    for c in range(rows // CHUNK):
        at = slice(c * CHUNK, (c + 1) * CHUNK)
        value = sc[at, :] * factors[c]
        turned = pltpu.roll(value, half, 1)
        head = head_of((CHUNK, page_len))
        first = lane_of((CHUNK, page_len)) < half
        low = jnp.where(first, jnp.where(head == 0, value, 0.0), jnp.where(head == 1, turned, 0.0))
        high = jnp.where(first, jnp.where(head == 2, turned, 0.0), jnp.where(head == 3, value, 0.0))
        ob[at, :page_len] = low.astype(jnp.bfloat16)
        ob[at, page_len:] = high.astype(jnp.bfloat16)
    for c in range(4):
        total = jnp.dot(member(c), ob[...], preferred_element_type=jnp.float32)
        out_ref[c * step : (c + 1) * step, : 2 * page_len] = total.astype(jnp.bfloat16)


def attend(k_cache, v_cache, key_new, value_new, all_queries, columns, owner_row):
    slots = k_cache.shape[0] + key_new.shape[0]
    page_len, width = k_cache.shape[1:]
    rows = slots * HEADS
    padded = owner_row.shape[1]
    requests = all_queries.shape[0]
    return pl.pallas_call(
        attend_kernel,
        out_shape=jax.ShapeDtypeStruct((requests, 3 * width), jnp.bfloat16),
        in_specs=[pl.BlockSpec(memory_space=pltpu.HBM)] * 4
        + [pl.BlockSpec(memory_space=pltpu.VMEM)] * 3,
        out_specs=pl.BlockSpec(memory_space=pltpu.VMEM),
        scratch_shapes=[
            pltpu.VMEM(k_cache.shape, k_cache.dtype),
            pltpu.VMEM(v_cache.shape, v_cache.dtype),
            pltpu.VMEM(key_new.shape, key_new.dtype),
            pltpu.VMEM(value_new.shape, value_new.dtype),
            pltpu.VMEM((rows, width), jnp.bfloat16),
            pltpu.VMEM((rows, page_len), jnp.float32),
            pltpu.VMEM((padded, 2 * width), jnp.bfloat16),
            pltpu.VMEM((padded, width), jnp.bfloat16),
            pltpu.SemaphoreType.DMA((2 * PARTS + 2,)),
        ],
        compiler_params=pltpu.CompilerParams(vmem_limit_bytes=59 << 20),
        cost_estimate=pl.CostEstimate(
            flops=4 * slots * ROWS * page_len * width * 4,
            bytes_accessed=4 * slots * page_len * width + (2 << 20),
            transcendentals=rows * page_len,
        ),
        name="attend",
    )(k_cache, v_cache, key_new, value_new, all_queries, columns, owner_row)


def call(kernel, outs, args, name, scratch=(), spaces=None, flops=0, limit=24 << 20):
    spaces = spaces or [pltpu.VMEM] * len(args)
    moved = sum(part.size * part.dtype.itemsize for part in list(args) + list(outs))
    return pl.pallas_call(
        kernel,
        out_shape=tuple(outs),
        in_specs=[pl.BlockSpec(memory_space=space) for space in spaces],
        out_specs=tuple(pl.BlockSpec(memory_space=pltpu.VMEM) for _ in outs),
        scratch_shapes=list(scratch),
        compiler_params=pltpu.CompilerParams(vmem_limit_bytes=limit),
        cost_estimate=pl.CostEstimate(flops=flops, bytes_accessed=moved, transcendentals=0),
        name=name,
    )(*args)


def query_kernel(tokens_ref, gain_ref, w_ref, out_ref):
    rows = rms_scale(tokens_ref[...].astype(jnp.float32), gain_ref[...].astype(jnp.float32))
    queries = jnp.dot(rows.astype(jnp.bfloat16), w_ref[...], preferred_element_type=jnp.float32)
    out_ref[...] = jnp.broadcast_to(queries.astype(jnp.bfloat16)[None], out_ref.shape)


def prepare_kernel(
    first_ref, hidden_hbm, table_ref, lengths_ref, wk_ref, wv_ref,
    kn_ref, vn_ref, cols_ref, row_ref,
    hidden_ref, turned, places, w_both, sems,
):
    part = hidden_ref.shape[0] // PARTS
    copies = []
    for c in range(PARTS):
        at = pl.ds(c * part, part)
        copies.append(pltpu.make_async_copy(hidden_hbm.at[at], hidden_ref.at[at], sems.at[c]))
    for copy in copies:
        copy.start()
    slots, requests = places.shape
    page_len = turned.shape[0]
    lanes = 128
    width = kn_ref.shape[1]
    w_both[:, :width] = wk_ref[...]
    w_both[:, width:] = wv_ref[...]
    ids = lax.broadcasted_iota(jnp.int32, (slots, lanes), 0) + first_ref[0]
    for g in range(requests // lanes):
        at = slice(g * lanes, (g + 1) * lanes)
        turned[:, at] = jnp.transpose(table_ref[at, :])
        longest = jnp.max(lengths_ref[g : g + 1, :].astype(jnp.float32)).astype(jnp.int32)

        def look(n, found, at=at):
            block = turned[pl.ds(pl.multiple_of(n * 8, 8), 8), at]
            for u in range(8):
                found = jnp.where(block[u : u + 1, :] == ids, n * 8 + u + 1, found)
            return found

        steps = (longest + 8 * page_len - 1) // (8 * page_len)
        places[:, at] = lax.fori_loop(0, steps, look, jnp.zeros((slots, lanes), jnp.int32))
    request = jnp.zeros((slots, 1), jnp.float32)
    limit = jnp.zeros((slots, 1), jnp.float32)
    leads = jnp.zeros((slots, 1), jnp.float32)
    slot = lax.broadcasted_iota(jnp.int32, (slots, lanes), 0)
    lane = lax.broadcasted_iota(jnp.int32, (slots, lanes), 1)

    def total(hit, value):
        return jnp.sum(jnp.where(hit, value.astype(jnp.float32), 0.0), axis=1, keepdims=True)

    for g in range(requests // lanes):
        place = places[:, g * lanes : (g + 1) * lanes]
        hit = place > 0
        request += total(hit, lane + g * lanes)
        limit += total(hit, lengths_ref[g : g + 1, :] - (place - 1) * page_len)
        order = jnp.where(hit, slot, slots).astype(jnp.float32)
        leads += total(hit & (order == jnp.min(order, axis=0, keepdims=True)), jnp.ones_like(lane))
    info = jnp.where(lane == 0, request, jnp.where(lane == 1, limit, leads)).astype(jnp.int32)
    rows = slots * HEADS
    cols_ref[rows:, :] = jnp.full((cols_ref.shape[0] - rows, lanes), -1, jnp.int32)
    for h in range(HEADS):
        cols_ref[pl.ds(h, slots, stride=HEADS), :] = info
    for c in range(cols_ref.shape[0] // lanes):
        at = slice(c * lanes, (c + 1) * lanes)
        row_ref[:, at] = jnp.transpose(cols_ref[at, :])[:8]
    for c in range(PARTS):
        copies[c].wait()
        at = slice(c * part, (c + 1) * part)
        both = jnp.dot(hidden_ref[at, :], w_both[...], preferred_element_type=jnp.float32)
        kn_ref[at, :] = both[:, :width].astype(jnp.bfloat16)
        vn_ref[at, :] = both[:, width:].astype(jnp.bfloat16)


def join_kernel(landed_ref, w_ref, out_ref):
    sources, owned, wide = landed_ref.shape
    lanes = wide // 3
    stats = landed_ref[:, :, 2 * lanes :].astype(jnp.float32).reshape(sources * owned, lanes)
    stats = (
        stats + pltpu.roll(stats, lanes - HEADS, 1) + pltpu.roll(stats, lanes - 2 * HEADS, 1)
    )
    lane = lax.broadcasted_iota(jnp.int32, stats.shape, 1)
    sums = jnp.where(lane < HEADS, stats, 0.0)
    tops = jnp.where(sums > 0.0, pltpu.roll(stats, lanes - 3 * HEADS, 1), NEG_FILL)
    tops = tops.reshape(sources, owned, lanes)
    weights = jnp.exp(tops - jnp.max(tops, axis=0, keepdims=True))
    totals = jnp.sum(weights * sums.reshape(sources, owned, lanes), axis=0)
    lane = lax.broadcasted_iota(jnp.int32, (1, lanes), 1)
    weights = weights.reshape(sources * owned, lanes)

    def spread(value, n):
        return jnp.where(lane < lanes // 2, value[:, 2 * n : 2 * n + 1], value[:, 2 * n + 1 : 2 * n + 2])

    projected = jnp.zeros(out_ref.shape, jnp.float32)
    for n in range(2):
        at = slice(n * lanes, (n + 1) * lanes)
        value = landed_ref[:, :, at].astype(jnp.float32).reshape(sources * owned, lanes)
        value = jnp.sum((value * spread(weights, n)).reshape(sources, owned, lanes), axis=0)
        attended = (value / spread(totals, n)).astype(jnp.bfloat16)
        projected += jnp.dot(attended, w_ref[at, :], preferred_element_type=jnp.float32)
    out_ref[...] = projected


def dispatch_kernel(tokens_ref, gain_ref, send_ref, *refs):
    *share_refs, mixed_ref, out_ref = refs
    mixed = tokens_ref[...].astype(jnp.float32) + sum(share[...] for share in share_refs)
    mixed_ref[...] = mixed
    normed = rms_scale(mixed, gain_ref[...].astype(jnp.float32)).astype(jnp.bfloat16)
    out_ref[...] = jnp.dot(send_ref[...], normed, preferred_element_type=jnp.float32).astype(
        jnp.bfloat16
    )


def rms_scale(row_vals, gain_row):
    mean_sq = jnp.mean(row_vals * row_vals, axis=-1, keepdims=True)
    return row_vals * lax.rsqrt(mean_sq + EPSILON) * gain_row


def on_device(
    tokens,
    block_table,
    lengths,
    k_cache,
    v_cache,
    hidden_store,
    norm_attn,
    w_query,
    w_key,
    w_value,
    w_out,
    norm_moe,
    expert_ids,
    gate_weights,
    w_gate,
    w_up,
    w_down,
):
    pool_count = lax.axis_size("pool")
    exp_count = lax.axis_size("exp")
    pool_index = lax.axis_index("pool")
    exp_index = lax.axis_index("exp")
    req_dev = tokens.shape[0]
    model_width = tokens.shape[1]
    quarter = model_width // exp_count
    bf16 = jnp.bfloat16
    query_width = w_query.shape[1]
    head_count = query_width // HEAD_SIZE
    (copies,) = call(
        query_kernel,
        [jax.ShapeDtypeStruct((pool_count, req_dev, query_width), bf16)],
        [tokens, norm_attn, w_query],
        "query",
        limit=60 << 20,
    )
    all_queries = lax.all_to_all(copies, "pool", split_axis=0, concat_axis=0, tiled=True)
    all_queries = all_queries.reshape(-1, query_width)
    slot_count = k_cache.shape[0] + hidden_store.shape[0]
    page_len, key_width = k_cache.shape[1:]
    requests = block_table.shape[0]
    stored_rows = hidden_store.reshape(-1, model_width)
    padded = -(-slot_count * head_count // 128) * 128
    key_new, value_new, columns, owner_row = call(
        prepare_kernel,
        [jax.ShapeDtypeStruct((stored_rows.shape[0], key_width), bf16)] * 2
        + [
            jax.ShapeDtypeStruct((padded, 128), jnp.int32),
            jax.ShapeDtypeStruct((8, padded), jnp.int32),
        ],
        [
            jnp.full((1,), pool_index * slot_count, jnp.int32),
            stored_rows,
            block_table,
            lengths.reshape(-1, 128),
            w_key,
            w_value,
        ],
        "prepare",
        [
            pltpu.VMEM(stored_rows.shape, bf16),
            pltpu.VMEM((block_table.shape[1], requests), jnp.int32),
            pltpu.VMEM((slot_count, requests), jnp.int32),
            pltpu.VMEM((model_width, 2 * key_width), bf16),
            pltpu.SemaphoreType.DMA((PARTS,)),
        ],
        [pltpu.SMEM, pltpu.HBM] + [pltpu.VMEM] * 4,
        4 * stored_rows.size * key_width,
        60 << 20,
    )
    key_new = key_new.reshape(-1, page_len, key_width)
    value_new = value_new.reshape(-1, page_len, key_width)
    parcel = attend(k_cache, v_cache, key_new, value_new, all_queries, columns, owner_row)
    parcel = parcel.reshape(pool_count, req_dev, -1)
    landed = lax.all_to_all(parcel, "pool", split_axis=0, concat_axis=0, tiled=True)
    (projected,) = call(
        join_kernel,
        [jax.ShapeDtypeStruct((req_dev, model_width), jnp.float32)],
        [landed, w_out],
        "join",
    )
    shares = [projected] + others(projected, "exp")
    top_count = expert_ids.shape[1]
    capacity = min(req_dev, 2 * ((req_dev * top_count + pool_count - 1) // pool_count))
    route_flat = expert_ids.reshape(-1)
    expert_hit = (route_flat[:, None] == jnp.arange(pool_count, dtype=jnp.int32)[None, :]).astype(
        jnp.int32
    )
    slot_rank = jnp.sum(jnp.cumsum(expert_hit, axis=0) * expert_hit, axis=1) - 1
    slot_pos = route_flat * capacity + slot_rank
    placed = (
        slot_pos[:, None] == jnp.arange(pool_count * capacity, dtype=jnp.int32)[None, :]
    ).astype(jnp.float32)
    placed = placed.reshape(req_dev, top_count, pool_count * capacity)
    send_map = jnp.sum(placed, axis=1).astype(jnp.bfloat16)
    combine_map = jnp.einsum("tk,tkc->tc", gate_weights, placed, precision=HIGHEST)
    mixed, outgoing = call(
        dispatch_kernel,
        [
            jax.ShapeDtypeStruct((req_dev, model_width), jnp.float32),
            jax.ShapeDtypeStruct((pool_count * capacity, model_width), bf16),
        ],
        [tokens, norm_moe, send_map.T] + shares,
        "dispatch",
    )
    outgoing = outgoing.reshape(pool_count, capacity, model_width)
    arrived = lax.all_to_all(outgoing, "pool", split_axis=0, concat_axis=0, tiled=True)
    sources = arrived.shape[0]
    slots_here = arrived.shape[1]
    row_block = arrived.reshape(-1, model_width)
    gate_act = jnp.dot(row_block, w_gate[0], preferred_element_type=jnp.float32)
    up_act = jnp.dot(row_block, w_up[0], preferred_element_type=jnp.float32)
    hidden = (jax.nn.silu(gate_act) * up_act).astype(jnp.bfloat16)
    down_share = lax.dynamic_slice_in_dim(w_down[0], exp_index * quarter, quarter, 1)
    expert_low = jnp.dot(hidden, down_share, preferred_element_type=jnp.float32).astype(jnp.bfloat16)
    expert_out = expert_low.reshape(sources, slots_here, quarter)
    returned = lax.all_to_all(expert_out, "pool", split_axis=0, concat_axis=0, tiled=True)
    moe_share = jnp.dot(
        combine_map,
        returned.reshape(pool_count * capacity, quarter).astype(jnp.float32),
        precision=HIGHEST,
    )
    mixed_share = lax.dynamic_slice_in_dim(mixed, exp_index * quarter, quarter, 1)
    return (mixed_share + moe_share).astype(jnp.bfloat16)


def solution(mesh):
    placed = (
        P("pool", None),
        P(),
        P(),
        P("pool", None, "exp"),
        P("pool", None, "exp"),
        P("pool", None, None),
        P(),
        P(None, "exp"),
        P(None, "exp"),
        P(None, "exp"),
        P("exp", None),
        P(),
        P("pool", None),
        P("pool", None),
        P("pool", None, None),
        P("pool", None, None),
        P("pool", None, None),
    )
    return jax.shard_map(
        on_device, mesh=mesh, in_specs=placed, out_specs=P("pool", "exp"), check_vma=False
    )
```

time: 104 us -> 89.6 us (0.86)
  Pallas kernels: 8.23 us -> 21 us
  other arithmetic: 13.2 us -> 0.56 us
  matrix products: 11.2 us -> 3.72 us
  local copies, waits for them, and re-layouts: 8.88 us -> 1.84 us
    pallas_call x0 -> x4, Pallas kernels: none -> 11.2 us  [call(): pl.pallas_call(kernel, out_shape=tuple(outs), in_specs=[pl.BlockSpec(memo...]
    reduce_sum x6 -> x0, other arithmetic: 10 us -> none  [the longest x1 6.55 us: on_device(): jnp.sum(jnp.where(flat_ids[None, :] == global_slot[:, None], entry_index[...]
    dot_general x5 -> x0, matrix products: 7.53 us -> none  [the longest x1 3.61 us: on_device(): jnp.dot(stored_rows, w_key, preferred_element_type=jnp.float32)]
    unnamed x18 -> x16, local copies, waits for them, and re-layouts: 6.2 us -> 1.56 us
    convert_element_type x3 -> x0, other arithmetic: 2.24 us -> none  [the longest x1 0.79 us: on_device(): norm_attn.astype(jnp.float32)]
    pallas_call x1, Pallas kernels: 8.23 us -> 9.78 us  [attend(): pl.pallas_call(attend_kernel, out_shape=jax.ShapeDtypeStruct((requests, 3...]
    broadcast_in_dim x5 -> x0, local copies, waits for them, and re-layouts: 1.46 us -> none  [the longest x1 0.73 us: gather_pool(): jnp.broadcast_to(value[None], (lax.axis_size('pool'),) + value.shape)]
    ppermute x2 -> x3, waiting for transfers between devices: 3.33 us -> 2.39 us  [others(): lax.ppermute(value, axis, [(i, (i + step) % size) for i in range(size)])]
  transfers between devices with their start and end apart: 6 -> 7, of which waited for: 5 -> 5; matrix products, arithmetic and copies ran while one was open for 16% -> 2% of each run, Pallas kernels for 0% -> 8%
where the time goes in v3:
time: 89.6 us; the launch traced here: 89.1 us
  waiting for transfers between devices  32.2 us (36%)
  starting transfers between devices  29.6 us (33%)
  Pallas kernels  21 us (23%)
  matrix products  3.72 us (4%)
  local copies, waits for them, and re-layouts  1.84 us (2%)
    all_to_all x1, waiting for transfers between devices, on_device(): lax.all_to_all(outgoing, 'pool', split_axis=0, concat_axis=0, tiled=True)  11.5 us
    pallas_call x4, Pallas kernels, call(): pl.pallas_call(kernel, out_shape=tuple(outs), in_specs=[pl.BlockSpec(memo...  11.2 us
    all_to_all x1, waiting for transfers between devices, on_device(): lax.all_to_all(parcel, 'pool', split_axis=0, concat_axis=0, tiled=True)  10.2 us
    pallas_call x1, Pallas kernels, attend(): pl.pallas_call(attend_kernel, out_shape=jax.ShapeDtypeStruct((requests, 3...  9.78 us
    all_to_all x1, starting transfers between devices, on_device(): lax.all_to_all(copies, 'pool', split_axis=0, concat_axis=0, tiled=True)  9.43 us
    all_to_all x1, waiting for transfers between devices, on_device(): lax.all_to_all(expert_out, 'pool', split_axis=0, concat_axis=0, tiled=True)  7.43 us
    all_to_all x1, starting transfers between devices, on_device(): lax.all_to_all(parcel, 'pool', split_axis=0, concat_axis=0, tiled=True)  6.92 us
    ppermute x3, starting transfers between devices, others(): lax.ppermute(value, axis, [(i, (i + step) % size) for i in range(size)])  5 us
  transfers between devices with their start and end apart: 7, of which 5 were waited for; matrix products, arithmetic and copies ran while one was open for 2% of the time, Pallas kernels for 8%

profile of v3, /device:TPU:1, one launch (start us, length us, event | category | flops | bytes accessed | tf_op | source)
XLA Modules:
  0.0 89.1 jit_solution(15466899558047219407)
XLA Ops:
  0.0 2.1 %query.1 = bf16[32,16,256]{2,1,0:T(8,128)(2,1)} custom-call(bf16[16,1024]{1,0:T(8,128)(2,1)} %tokens_ref.3, bf16[1024]{0:T(1024)(128)(2,1)} %gain_ref.2, bf16[1024,256]{1,0:T(8,128)(2,1)} %w_ref.2), custom_call_target="tpu_custom_call" | custom-call | bytes 821248 | tf_op jit(solution)/shard_map/query/pallas_call | solution.py:239
  2.1 9.4 %all-to-all-start = ((bf16[32,16,256]{2,1,0:T(8,128)(2,1)}), bf16[32,16,256]{2,1,0:T(8,128)(2,1)S(1)}, u32[]{:S(2)}, u32[]{:S(2)}) async-start(bf16[32,16,256]{2,1,0:T(8,128)(2,1)} %query.1), calls=%async_computation | async-start | bytes 524288 | tf_op jit(solution)/shard_map/all_to_all | solution.py:401
  11.6 0.8 copy.22
  12.5 0.2 reduce_window_sum.11
  12.7 7.1 %prepare.1 = (bf16[2048,128]{1,0:T(8,128)(2,1)}, bf16[2048,128]{1,0:T(8,128)(2,1)}, s32[640,128]{1,0:T(8,128)}, s32[8,640]{1,0:T(8,128)}) custom-call(s32[1]{0:T(128)} %bitcast.1.first_ref, bf16[2048,1024]{1,0:T(8,128)(2,1)} %bitcast.40, s32[512,128]{1,0:T(8,128)} %table_ref.1, s32[4,128]{1,0:T(4,128)} %bitcast.46, bf16[1024,128]{1,0:T(8,128)(2,1)} %wk_ref.1, ...), custom_call_target="tpu_custom_call" | custom-call | flops 1073741824 | bytes 6379524 | tf_op jit(solution)/shard_map/prepare/pallas_call | solution.py:239
  20.0 0.6 all-to-all-done
  20.6 0.7 copy-done.4
  21.3 9.8 %attend.1 = bf16[512,384]{1,0:T(8,128)(2,1)} custom-call(bf16[128,128,128]{2,1,0:T(8,128)(2,1)} %k_hbm.1, bf16[128,128,128]{2,1,0:T(8,128)(2,1)} %v_hbm.1, bf16[16,128,128]{2,1,0:T(8,128)(2,1)} %bitcast.43, bf16[16,128,128]{2,1,0:T(8,128)(2,1)} %bitcast.44, bf16[512,256]{1,0:T(8,128)(2,1)} %bitcast.42, s32[640,128]{1,0:T(8,128)} %get-tuple-element.13.cols_ref, ...), custom_call_target="tpu_custom_call" | custom-call | flops 603979776 | bytes 11534336 | tf_op jit(solution)/shard_map/attend/pallas_call | solution.py:209
  31.1 6.9 %all-to-all-start.1 = ((bf16[32,16,384]{2,1,0:T(8,128)(2,1)}), bf16[32,16,384]{2,1,0:T(8,128)(2,1)S(1)}, u32[]{:S(2)}, u32[]{:S(2)}) async-start(bf16[32,16,384]{2,1,0:T(8,128)(2,1)} %bitcast.41), calls=%async_computation.1 | async-start | bytes 786432 | tf_op jit(solution)/shard_map/all_to_all | solution.py:439
  38.1 10.2 %all-to-all-done.1.landed_ref = bf16[32,16,384]{2,1,0:T(8,128)(2,1)S(1)} async-done(((bf16[32,16,384]{2,1,0:T(8,128)(2,1)}), bf16[32,16,384]{2,1,0:T(8,128)(2,1)S(1)}, u32[]{:S(2)}, u32[]{:S(2)}) %all-to-all-start.1) | async-done | bytes 393248 | tf_op jit(solution)/shard_map/all_to_all | solution.py:439
  48.3 0.8 join.1.refs_0_
  49.1 1.3 %collective-permute-start = (f32[16,1024]{1,0:T(8,128)S(1)}, f32[16,1024]{1,0:T(8,128)S(1)}, u32[]{:S(2)}, u32[]{:S(2)}) collective-permute-start(f32[16,1024]{1,0:T(8,128)S(1)} %join.1.refs_0_), channel_id=1, source_target_pairs={{0,1},{1,2},{2,3},{3,0},{4,5},{5,6},{6,7},{7,4},{8,9},{9,10},{10,1... | collective-permute-start | bytes 196616 | tf_op jit(solution)/shard_map/ppermute | solution.py:20
  50.4 2.6 %collective-permute-start.1 = (f32[16,1024]{1,0:T(8,128)S(1)}, f32[16,1024]{1,0:T(8,128)S(1)}, u32[]{:S(2)}, u32[]{:S(2)}) collective-permute-start(f32[16,1024]{1,0:T(8,128)S(1)} %join.1.refs_0_), channel_id=1, source_target_pairs={{0,2},{1,3},{2,0},{3,1},{4,6},{5,7},{6,4},{7,5},{8,10},{9,11},{10,... | collective-permute-start | bytes 196616 | tf_op jit(solution)/shard_map/ppermute | solution.py:20
  53.1 1.1 %collective-permute-start.2 = (f32[16,1024]{1,0:T(8,128)S(1)}, f32[16,1024]{1,0:T(8,128)S(1)}, u32[]{:S(2)}, u32[]{:S(2)}) collective-permute-start(f32[16,1024]{1,0:T(8,128)S(1)} %join.1.refs_0_), channel_id=1, source_target_pairs={{0,3},{1,0},{2,1},{3,2},{4,7},{5,4},{6,5},{7,6},{8,11},{9,8},{10,9... | collective-permute-start | bytes 196616 | tf_op jit(solution)/shard_map/ppermute | solution.py:20
  54.4 2.4 %collective-permute-done.1.refs_2_ = f32[16,1024]{1,0:T(8,128)S(1)} collective-permute-done((f32[16,1024]{1,0:T(8,128)S(1)}, f32[16,1024]{1,0:T(8,128)S(1)}, u32[]{:S(2)}, u32[]{:S(2)}) %collective-permute-start.1) | collective-permute-done | bytes 65568 | tf_op jit(solution)/shard_map/ppermute | solution.py:20
  56.8 1.2 %dispatch.1 = (f32[16,1024]{1,0:T(8,128)S(1)}, bf16[256,1024]{1,0:T(8,128)(2,1)}) custom-call(bf16[16,1024]{1,0:T(8,128)(2,1)S(1)} %copy-done.2, bf16[1024]{0:T(1024)(128)(2,1)S(1)} %copy-done.3, bf16[256,16]{1,0:T(8,128)(2,1)S(1)} %bitcast.39, f32[16,1024]{1,0:T(8,128)S(1)} %join.1.refs_0_, f32[16,1024]{1,0:T(8,128)S(1)} %collective-permute-done.refs_1_, ...), custom_call_target="tpu_custom_call" | custom-call | bytes 894976 | tf_op jit(solution)/shard_map/dispatch/pallas_call | solution.py:239
  57.9 4.7 %all-to-all-start.2 = ((bf16[32,8,1024]{2,1,0:T(8,128)(2,1)}), bf16[32,8,1024]{2,1,0:T(8,128)(2,1)S(1)}, u32[]{:S(2)}, u32[]{:S(2)}) async-start(bf16[32,8,1024]{2,1,0:T(8,128)(2,1)} %bitcast.10), calls=%async_computation.2 | async-start | bytes 1048576 | tf_op jit(solution)/shard_map/all_to_all | solution.py:471
  62.7 11.5 %all-to-all-done.2 = bf16[32,8,1024]{2,1,0:T(8,128)(2,1)S(1)} async-done(((bf16[32,8,1024]{2,1,0:T(8,128)(2,1)}), bf16[32,8,1024]{2,1,0:T(8,128)(2,1)S(1)}, u32[]{:S(2)}, u32[]{:S(2)}) %all-to-all-start.2) | async-done | bytes 524320 | tf_op jit(solution)/shard_map/all_to_all | solution.py:471
  74.2 0.4 fusion.6
  74.7 2.2 %fusion.3 = bf16[32,8,256]{2,1,0:T(8,128)(2,1)} fusion(bf16[1,1024,512]{2,1,0:T(8,128)(2,1)S(1)} %copy-done.6, bf16[32,8,1024]{2,1,0:T(8,128)(2,1)S(1)} %all-to-all-done.2, f32[256,512]{1,0:T(8,128)S(1)} %fusion.6, bf16[1,512,1024]{2,1,0:T(8,128)(2,1)} %param.33, s32[]{:T(128)S(6)} %select_n.4), kind=kOutput, calls=%fused_computation.4 | convolution fusion | flops 336396288 | bytes 2490372 | tf_op jit(solution)/shard_map/dot_general | solution.py:479
  76.9 3.6 %all-to-all-start.3 = ((bf16[32,8,256]{2,1,0:T(8,128)(2,1)}), bf16[32,8,256]{2,1,0:T(8,128)(2,1)S(1)}, u32[]{:S(2)}, u32[]{:S(2)}) async-start(bf16[32,8,256]{2,1,0:T(8,128)(2,1)} %fusion.3), calls=%async_computation.3 | async-start | bytes 262144 | tf_op jit(solution)/shard_map/all_to_all | solution.py:481
  80.6 0.3 fusion.21
  80.8 7.4 %all-to-all-done.3 = bf16[32,8,256]{2,1,0:T(8,128)(2,1)S(1)} async-done(((bf16[32,8,256]{2,1,0:T(8,128)(2,1)}), bf16[32,8,256]{2,1,0:T(8,128)(2,1)S(1)}, u32[]{:S(2)}, u32[]{:S(2)}) %all-to-all-start.3) | async-done | bytes 131104 | tf_op jit(solution)/shard_map/all_to_all | solution.py:481
  88.3 0.8 add_convert_fusion
  (24 shorter events, 0.8 us)
Async XLA Ops:
  0.0 74.2 %copy-start = (bf16[1,1024,512]{2,1,0:T(8,128)(2,1)S(1)}, bf16[1,1024,512]{2,1,0:T(8,128)(2,1)}, u32[]{:S(2)}) copy-start(bf16[1,1024,512]{2,1,0:T(8,128)(2,1)} %param.31) | copy-start | bytes 3145732
  2.1 18.4 %all-to-all-start = ((bf16[32,16,256]{2,1,0:T(8,128)(2,1)}), bf16[32,16,256]{2,1,0:T(8,128)(2,1)S(1)}, u32[]{:S(2)}, u32[]{:S(2)}) async-start(bf16[32,16,256]{2,1,0:T(8,128)(2,1)} %query.1), calls=%async_computation | async-start | bytes 524288 | tf_op jit(solution)/shard_map/all_to_all | solution.py:401
  20.6 0.7 copy-start.4
  21.3 27.0 %copy-start.1 = (bf16[256,1024]{1,0:T(8,128)(2,1)S(1)}, bf16[256,1024]{1,0:T(8,128)(2,1)}, u32[]{:S(2)}) copy-start(bf16[256,1024]{1,0:T(8,128)(2,1)} %w_ref.3) | copy-start | bytes 1572868
  21.3 35.5 %copy-start.2 = (bf16[16,1024]{1,0:T(8,128)(2,1)S(1)}, bf16[16,1024]{1,0:T(8,128)(2,1)}, u32[]{:S(2)}) copy-start(bf16[16,1024]{1,0:T(8,128)(2,1)} %tokens_ref.3) | copy-start | bytes 98308
  21.3 35.5 %copy-start.3 = (bf16[1024]{0:T(1024)(128)(2,1)S(1)}, bf16[1024]{0:T(1024)(128)(2,1)}, u32[]{:S(2)}) copy-start(bf16[1024]{0:T(1024)(128)(2,1)} %gain_ref.3) | copy-start | bytes 6148
  21.3 41.3 %copy-start.5 = (f32[16,8]{0,1:T(8,128)S(1)}, f32[16,8]{0,1:T(8,128)}, u32[]{:S(2)}) copy-start(f32[16,8]{0,1:T(8,128)} %param.30) | copy-start | bytes 1540
  31.1 43.6 %copy-start.6 = (bf16[1,1024,512]{2,1,0:T(8,128)(2,1)S(1)}, bf16[1,1024,512]{2,1,0:T(8,128)(2,1)}, u32[]{:S(2)}) copy-start(bf16[1,1024,512]{2,1,0:T(8,128)(2,1)} %param.32) | copy-start | bytes 3145732
  31.1 17.2 %all-to-all-start.1 = ((bf16[32,16,384]{2,1,0:T(8,128)(2,1)}), bf16[32,16,384]{2,1,0:T(8,128)(2,1)S(1)}, u32[]{:S(2)}, u32[]{:S(2)}) async-start(bf16[32,16,384]{2,1,0:T(8,128)(2,1)} %bitcast.41), calls=%async_computation.1 | async-start | bytes 786432 | tf_op jit(solution)/shard_map/all_to_all | solution.py:439
  49.1 5.2 %collective-permute-start = (f32[16,1024]{1,0:T(8,128)S(1)}, f32[16,1024]{1,0:T(8,128)S(1)}, u32[]{:S(2)}, u32[]{:S(2)}) collective-permute-start(f32[16,1024]{1,0:T(8,128)S(1)} %join.1.refs_0_), channel_id=1, source_target_pairs={{0,1},{1,2},{2,3},{3,0},{4,5},{5,6},{6,7},{7,4},{8,9},{9,10},{10,1... | collective-permute-start | bytes 196616 | tf_op jit(solution)/shard_map/ppermute | solution.py:20
  50.4 6.3 %collective-permute-start.1 = (f32[16,1024]{1,0:T(8,128)S(1)}, f32[16,1024]{1,0:T(8,128)S(1)}, u32[]{:S(2)}, u32[]{:S(2)}) collective-permute-start(f32[16,1024]{1,0:T(8,128)S(1)} %join.1.refs_0_), channel_id=1, source_target_pairs={{0,2},{1,3},{2,0},{3,1},{4,6},{5,7},{6,4},{7,5},{8,10},{9,11},{10,... | collective-permute-start | bytes 196616 | tf_op jit(solution)/shard_map/ppermute | solution.py:20
  53.1 3.7 %collective-permute-start.2 = (f32[16,1024]{1,0:T(8,128)S(1)}, f32[16,1024]{1,0:T(8,128)S(1)}, u32[]{:S(2)}, u32[]{:S(2)}) collective-permute-start(f32[16,1024]{1,0:T(8,128)S(1)} %join.1.refs_0_), channel_id=1, source_target_pairs={{0,3},{1,0},{2,1},{3,2},{4,7},{5,4},{6,5},{7,6},{8,11},{9,8},{10,9... | collective-permute-start | bytes 196616 | tf_op jit(solution)/shard_map/ppermute | solution.py:20
  57.9 16.3 %all-to-all-start.2 = ((bf16[32,8,1024]{2,1,0:T(8,128)(2,1)}), bf16[32,8,1024]{2,1,0:T(8,128)(2,1)S(1)}, u32[]{:S(2)}, u32[]{:S(2)}) async-start(bf16[32,8,1024]{2,1,0:T(8,128)(2,1)} %bitcast.10), calls=%async_computation.2 | async-start | bytes 1048576 | tf_op jit(solution)/shard_map/all_to_all | solution.py:471
  76.9 11.3 %all-to-all-start.3 = ((bf16[32,8,256]{2,1,0:T(8,128)(2,1)}), bf16[32,8,256]{2,1,0:T(8,128)(2,1)S(1)}, u32[]{:S(2)}, u32[]{:S(2)}) async-start(bf16[32,8,256]{2,1,0:T(8,128)(2,1)} %fusion.3), calls=%async_computation.3 | async-start | bytes 262144 | tf_op jit(solution)/shard_map/all_to_all | solution.py:481

commit v4 on v3

--- a/solution.py
+++ b/solution.py
@@ -34,6 +34,8 @@
 ROWS = HEADS * QUAD
 CHUNK = 64
 PARTS = 4
+SPLIT = 2
+FLIGHT = 3
 
 
 def attend_kernel(
@@ -41,18 +43,24 @@
     k_ref, v_ref, kn_ref, vn_ref, qs, sc, ob, cb, sems,
 ):
     rows, page_len = sc.shape
-    part = k_ref.shape[0] // PARTS
+    part = k_ref.shape[0] // SPLIT
     copies = []
     streams = ((k_hbm, k_ref, kn_hbm, kn_ref), (v_hbm, v_ref, vn_hbm, vn_ref))
     for whole, held, new, new_held in streams:
-        for c in range(PARTS):
+        for c in range(SPLIT):
             at = pl.ds(c * part, part)
             copies.append(
                 pltpu.make_async_copy(whole.at[at], held.at[at], sems.at[len(copies)])
             )
         copies.append(pltpu.make_async_copy(new, new_held, sems.at[len(copies)]))
-    for copy in copies:
+    for copy in copies[:FLIGHT]:
         copy.start()
+
+    def arrive(n):
+        copies[n].wait()
+        if n + FLIGHT < len(copies):
+            copies[n + FLIGHT].start()
+
     requests = q_ref.shape[0]
     half = page_len // 2
     old_quads = k_ref.shape[0] // QUAD
@@ -83,7 +91,7 @@
     quad_row = lax.broadcasted_iota(jnp.int32, (ROWS, page_len), 0) // HEADS
 
     def score(i, keys):
-        q16 = qs[pl.ds(pl.multiple_of(i * ROWS, ROWS), ROWS), :]
+        q16 = qs[i * ROWS : (i + 1) * ROWS, :]
         wide = lax.dot_general(
             q16,
             keys.reshape(QUAD * page_len, page_len),
@@ -93,17 +101,14 @@
         got = wide[:, :page_len]
         for n in range(1, QUAD):
             got = jnp.where(quad_row == n, wide[:, n * page_len : (n + 1) * page_len], got)
-        sc[pl.ds(pl.multiple_of(i * ROWS, ROWS), ROWS), :] = got * SCORE_SCALE
-
-    for c in range(PARTS):
-        copies[c].wait()
-
-        @pl.loop(c * old_quads // PARTS, (c + 1) * old_quads // PARTS, step=8)
-        def _(i):
-            for n in range(8):
-                score(i + n, k_ref[pl.ds((i + n) * QUAD, QUAD)])
-
-    copies[PARTS].wait()
+        sc[i * ROWS : (i + 1) * ROWS, :] = got * SCORE_SCALE
+
+    for c in range(SPLIT):
+        arrive(c)
+        for i in range(c * old_quads // SPLIT, (c + 1) * old_quads // SPLIT):
+            score(i, k_ref[i * QUAD : (i + 1) * QUAD])
+
+    arrive(SPLIT)
     for i in range(old_quads, quads):
         score(i, kn_ref[(i - old_quads) * QUAD : (i - old_quads + 1) * QUAD])
 
@@ -165,23 +170,20 @@
         out_ref[c * step : (c + 1) * step, 2 * page_len :] = stats.astype(jnp.bfloat16)
 
     def blend(i, values):
-        p16 = sc[pl.ds(pl.multiple_of(i * ROWS, ROWS), ROWS), :]
+        p16 = sc[i * ROWS : (i + 1) * ROWS, :]
         parts = [jnp.where(quad_row == n, p16, 0.0) for n in range(QUAD)]
-        sc[pl.ds(pl.multiple_of(i * ROWS, ROWS), ROWS), :] = jnp.dot(
+        sc[i * ROWS : (i + 1) * ROWS, :] = jnp.dot(
             jnp.concatenate(parts, axis=1).astype(jnp.bfloat16),
             values.reshape(QUAD * page_len, page_len),
             preferred_element_type=jnp.float32,
         )
 
-    for c in range(PARTS):
-        copies[c + PARTS + 1].wait()
-
-        @pl.loop(c * old_quads // PARTS, (c + 1) * old_quads // PARTS, step=8)
-        def _(i):
-            for n in range(8):
-                blend(i + n, v_ref[pl.ds((i + n) * QUAD, QUAD)])
-
-    copies[2 * PARTS + 1].wait()
+    for c in range(SPLIT):
+        arrive(c + SPLIT + 1)
+        for i in range(c * old_quads // SPLIT, (c + 1) * old_quads // SPLIT):
+            blend(i, v_ref[i * QUAD : (i + 1) * QUAD])
+
+    arrive(2 * SPLIT + 1)
     for i in range(old_quads, quads):
         blend(i, vn_ref[(i - old_quads) * QUAD : (i - old_quads + 1) * QUAD])
 
@@ -221,7 +223,7 @@
             pltpu.VMEM((rows, page_len), jnp.float32),
             pltpu.VMEM((padded, 2 * width), jnp.bfloat16),
             pltpu.VMEM((padded, width), jnp.bfloat16),
-            pltpu.SemaphoreType.DMA((2 * PARTS + 2,)),
+            pltpu.SemaphoreType.DMA((2 * SPLIT + 2,)),
         ],
         compiler_params=pltpu.CompilerParams(vmem_limit_bytes=59 << 20),
         cost_estimate=pl.CostEstimate(
@@ -255,12 +257,23 @@
 
 
 def prepare_kernel(
-    first_ref, hidden_hbm, table_ref, lengths_ref, wk_ref, wv_ref,
+    first_ref, hidden_hbm, table_hbm, lengths_ref, wk_hbm, wv_hbm,
     kn_ref, vn_ref, cols_ref, row_ref,
-    hidden_ref, turned, places, w_both, sems,
+    hidden_ref, table_ref, turned, places, w_both, sems,
 ):
     part = hidden_ref.shape[0] // PARTS
+    width = kn_ref.shape[1]
     copies = []
+    early = (
+        (table_hbm, table_ref),
+        (wk_hbm, w_both.at[:, pl.ds(0, width)]),
+        (wv_hbm, w_both.at[:, pl.ds(width, width)]),
+    )
+    first_copies = []
+    for n, (whole, held) in enumerate(early):
+        first_copies.append(pltpu.make_async_copy(whole, held, sems.at[PARTS + n]))
+    for copy in first_copies:
+        copy.start()
     for c in range(PARTS):
         at = pl.ds(c * part, part)
         copies.append(pltpu.make_async_copy(hidden_hbm.at[at], hidden_ref.at[at], sems.at[c]))
@@ -269,9 +282,7 @@
     slots, requests = places.shape
     page_len = turned.shape[0]
     lanes = 128
-    width = kn_ref.shape[1]
-    w_both[:, :width] = wk_ref[...]
-    w_both[:, width:] = wv_ref[...]
+    first_copies[0].wait()
     ids = lax.broadcasted_iota(jnp.int32, (slots, lanes), 0) + first_ref[0]
     for g in range(requests // lanes):
         at = slice(g * lanes, (g + 1) * lanes)
@@ -310,6 +321,8 @@
     for c in range(cols_ref.shape[0] // lanes):
         at = slice(c * lanes, (c + 1) * lanes)
         row_ref[:, at] = jnp.transpose(cols_ref[at, :])[:8]
+    for copy in first_copies[1:]:
+        copy.wait()
     for c in range(PARTS):
         copies[c].wait()
         at = slice(c * part, (c + 1) * part)
@@ -353,6 +366,16 @@
     mixed_ref[...] = mixed
     normed = rms_scale(mixed, gain_ref[...].astype(jnp.float32)).astype(jnp.bfloat16)
     out_ref[...] = jnp.dot(send_ref[...], normed, preferred_element_type=jnp.float32).astype(
+        jnp.bfloat16
+    )
+
+
+def expert_kernel(rows_ref, gate_ref, up_ref, down_ref, out_ref):
+    rows = rows_ref[...]
+    gate = jnp.dot(rows, gate_ref[...], preferred_element_type=jnp.float32)
+    up = jnp.dot(rows, up_ref[...], preferred_element_type=jnp.float32)
+    hidden = (gate / (1.0 + jnp.exp(-gate)) * up).astype(jnp.bfloat16)
+    out_ref[...] = jnp.dot(hidden, down_ref[...], preferred_element_type=jnp.float32).astype(
         jnp.bfloat16
     )
 
@@ -423,18 +446,21 @@
         "prepare",
         [
             pltpu.VMEM(stored_rows.shape, bf16),
+            pltpu.VMEM(block_table.shape, jnp.int32),
             pltpu.VMEM((block_table.shape[1], requests), jnp.int32),
             pltpu.VMEM((slot_count, requests), jnp.int32),
             pltpu.VMEM((model_width, 2 * key_width), bf16),
-            pltpu.SemaphoreType.DMA((PARTS,)),
+            pltpu.SemaphoreType.DMA((PARTS + 3,)),
         ],
-        [pltpu.SMEM, pltpu.HBM] + [pltpu.VMEM] * 4,
+        [pltpu.SMEM, pltpu.HBM, pltpu.HBM, pltpu.VMEM, pltpu.HBM, pltpu.HBM],
         4 * stored_rows.size * key_width,
         60 << 20,
     )
     key_new = key_new.reshape(-1, page_len, key_width)
     value_new = value_new.reshape(-1, page_len, key_width)
     parcel = attend(k_cache, v_cache, key_new, value_new, all_queries, columns, owner_row)
+    parcel, expert_ids, w_down = lax.optimization_barrier((parcel, expert_ids, w_down))
+    down_share = lax.dynamic_slice_in_dim(w_down[0], exp_index * quarter, quarter, 1)
     parcel = parcel.reshape(pool_count, req_dev, -1)
     landed = lax.all_to_all(parcel, "pool", split_axis=0, concat_axis=0, tiled=True)
     (projected,) = call(
@@ -472,11 +498,14 @@
     sources = arrived.shape[0]
     slots_here = arrived.shape[1]
     row_block = arrived.reshape(-1, model_width)
-    gate_act = jnp.dot(row_block, w_gate[0], preferred_element_type=jnp.float32)
-    up_act = jnp.dot(row_block, w_up[0], preferred_element_type=jnp.float32)
-    hidden = (jax.nn.silu(gate_act) * up_act).astype(jnp.bfloat16)
-    down_share = lax.dynamic_slice_in_dim(w_down[0], exp_index * quarter, quarter, 1)
-    expert_low = jnp.dot(hidden, down_share, preferred_element_type=jnp.float32).astype(jnp.bfloat16)
+    (expert_low,) = call(
+        expert_kernel,
+        [jax.ShapeDtypeStruct((row_block.shape[0], quarter), bf16)],
+        [row_block, w_gate[0], w_up[0], down_share],
+        "expert",
+        flops=4 * row_block.size * w_up.shape[2],
+        limit=16 << 20,
+    )
     expert_out = expert_low.reshape(sources, slots_here, quarter)
     returned = lax.all_to_all(expert_out, "pool", split_axis=0, concat_axis=0, tiled=True)
     moe_share = jnp.dot(

time: 89.6 us -> 89.2 us (level)
  matrix products: 3.72 us -> 1.04 us
  Pallas kernels: 21 us -> 22.8 us
  starting transfers between devices: 29.6 us -> 28.7 us
    dot_general x2 -> x0, matrix products: 2.68 us -> none  [the longest x1 2.24 us: on_device(): jnp.dot(hidden, down_share, preferred_element_type=jnp.float32)]
    pallas_call x4 -> x5, Pallas kernels: 11.2 us -> 13.2 us  [call(): pl.pallas_call(kernel, out_shape=tuple(outs), in_specs=[pl.BlockSpec(memo...]
    all_to_all x1, starting transfers between devices: 6.92 us -> 5.93 us  [on_device(): lax.all_to_all(parcel, 'pool', split_axis=0, concat_axis=0, tiled=True)]
    unnamed x16 -> x19, local copies, waits for them, and re-layouts: 1.56 us -> 2.04 us
  transfers between devices with their start and end apart: 7 -> 7, of which waited for: 5 -> 5; matrix products, arithmetic and copies ran while one was open for 2% -> 1% of each run, Pallas kernels for 8% -> 8%
where the time goes in v4:
time: 89.2 us; the launch traced here: 88.7 us
  waiting for transfers between devices  33 us (37%)
  starting transfers between devices  28.7 us (32%)
  Pallas kernels  22.8 us (26%)
  local copies, waits for them, and re-layouts  2.43 us (3%)
  matrix products  1.04 us (1%)
    pallas_call x5, Pallas kernels, call(): pl.pallas_call(kernel, out_shape=tuple(outs), in_specs=[pl.BlockSpec(memo...  13.2 us
    all_to_all x1, waiting for transfers between devices, on_device(): lax.all_to_all(outgoing, 'pool', split_axis=0, concat_axis=0, tiled=True)  11.5 us
    all_to_all x1, waiting for transfers between devices, on_device(): lax.all_to_all(parcel, 'pool', split_axis=0, concat_axis=0, tiled=True)  10.2 us
    pallas_call x1, Pallas kernels, attend(): pl.pallas_call(attend_kernel, out_shape=jax.ShapeDtypeStruct((requests, 3...  9.63 us
    all_to_all x1, starting transfers between devices, on_device(): lax.all_to_all(copies, 'pool', split_axis=0, concat_axis=0, tiled=True)  9.43 us
    all_to_all x1, waiting for transfers between devices, on_device(): lax.all_to_all(expert_out, 'pool', split_axis=0, concat_axis=0, tiled=True)  7.42 us
    all_to_all x1, starting transfers between devices, on_device(): lax.all_to_all(parcel, 'pool', split_axis=0, concat_axis=0, tiled=True)  5.93 us
    ppermute x3, starting transfers between devices, others(): lax.ppermute(value, axis, [(i, (i + step) % size) for i in range(size)])  5 us
  transfers between devices with their start and end apart: 7, of which 5 were waited for; matrix products, arithmetic and copies ran while one was open for 1% of the time, Pallas kernels for 8%

profile of v4, /device:TPU:1, one launch (start us, length us, event | category | flops | bytes accessed | tf_op | source)
XLA Modules:
  0.0 88.7 jit_solution(7075037653498496075)
XLA Ops:
  0.0 2.1 %query.1 = bf16[32,16,256]{2,1,0:T(8,128)(2,1)} custom-call(bf16[16,1024]{1,0:T(8,128)(2,1)} %tokens_ref.3, bf16[1024]{0:T(1024)(128)(2,1)} %gain_ref.2, bf16[1024,256]{1,0:T(8,128)(2,1)} %w_ref.2), custom_call_target="tpu_custom_call" | custom-call | bytes 821248 | tf_op jit(solution)/shard_map/query/pallas_call | solution.py:241
  2.2 9.4 %all-to-all-start = ((bf16[32,16,256]{2,1,0:T(8,128)(2,1)}), bf16[32,16,256]{2,1,0:T(8,128)(2,1)S(1)}, u32[]{:S(2)}, u32[]{:S(2)}) async-start(bf16[32,16,256]{2,1,0:T(8,128)(2,1)} %query.1), calls=%async_computation | async-start | bytes 524288 | tf_op jit(solution)/shard_map/all_to_all | solution.py:424
  11.6 7.5 %prepare.1 = (bf16[2048,128]{1,0:T(8,128)(2,1)}, bf16[2048,128]{1,0:T(8,128)(2,1)}, s32[640,128]{1,0:T(8,128)}, s32[8,640]{1,0:T(8,128)}) custom-call(s32[1]{0:T(128)} %bitcast.first_ref, bf16[2048,1024]{1,0:T(8,128)(2,1)} %bitcast.31, s32[512,128]{1,0:T(8,128)} %table_hbm.1, s32[4,128]{1,0:T(4,128)} %bitcast.37, bf16[1024,128]{1,0:T(8,128)(2,1)} %wk_hbm.1, ...), custom_call_target="tpu_custom_call" | custom-call | flops 1073741824 | bytes 6379524 | tf_op jit(solution)/shard_map/prepare/pallas_call | solution.py:241
  19.1 1.5 %all-to-all-done = bf16[32,16,256]{2,1,0:T(8,128)(2,1)S(1)} async-done(((bf16[32,16,256]{2,1,0:T(8,128)(2,1)}), bf16[32,16,256]{2,1,0:T(8,128)(2,1)S(1)}, u32[]{:S(2)}, u32[]{:S(2)}) %all-to-all-start) | async-done | bytes 262176 | tf_op jit(solution)/shard_map/all_to_all | solution.py:424
  20.6 0.7 copy-done.6
  21.3 9.6 %attend.1 = bf16[512,384]{1,0:T(8,128)(2,1)} custom-call(bf16[128,128,128]{2,1,0:T(8,128)(2,1)} %k_hbm.1, bf16[128,128,128]{2,1,0:T(8,128)(2,1)} %v_hbm.1, bf16[16,128,128]{2,1,0:T(8,128)(2,1)} %bitcast.34, bf16[16,128,128]{2,1,0:T(8,128)(2,1)} %bitcast.35, bf16[512,256]{1,0:T(8,128)(2,1)} %bitcast.33, s32[640,128]{1,0:T(8,128)} %get-tuple-element.16.cols_ref, ...), custom_call_target="tpu_custom_call" | custom-call | flops 603979776 | bytes 11534336 | tf_op jit(solution)/shard_map/attend/pallas_call | solution.py:211
  31.2 0.2 reduce_window_sum.11
  31.4 0.2 select_reduce_fusion
  31.6 5.9 %all-to-all-start.1 = ((bf16[32,16,384]{2,1,0:T(8,128)(2,1)}), bf16[32,16,384]{2,1,0:T(8,128)(2,1)S(1)}, u32[]{:S(2)}, u32[]{:S(2)}) async-start(bf16[32,16,384]{2,1,0:T(8,128)(2,1)} %bitcast.32), calls=%async_computation.1 | async-start | bytes 786432 | tf_op jit(solution)/shard_map/all_to_all | solution.py:465
  37.6 10.2 %all-to-all-done.1.landed_ref = bf16[32,16,384]{2,1,0:T(8,128)(2,1)S(1)} async-done(((bf16[32,16,384]{2,1,0:T(8,128)(2,1)}), bf16[32,16,384]{2,1,0:T(8,128)(2,1)S(1)}, u32[]{:S(2)}, u32[]{:S(2)}) %all-to-all-start.1) | async-done | bytes 393248 | tf_op jit(solution)/shard_map/all_to_all | solution.py:465
  47.8 0.8 join.1.refs_0_
  48.7 1.3 %collective-permute-start = (f32[16,1024]{1,0:T(8,128)S(1)}, f32[16,1024]{1,0:T(8,128)S(1)}, u32[]{:S(2)}, u32[]{:S(2)}) collective-permute-start(f32[16,1024]{1,0:T(8,128)S(1)} %join.1.refs_0_), channel_id=1, source_target_pairs={{0,1},{1,2},{2,3},{3,0},{4,5},{5,6},{6,7},{7,4},{8,9},{9,10},{10,1... | collective-permute-start | bytes 196616 | tf_op jit(solution)/shard_map/ppermute | solution.py:20
  50.0 2.6 %collective-permute-start.1 = (f32[16,1024]{1,0:T(8,128)S(1)}, f32[16,1024]{1,0:T(8,128)S(1)}, u32[]{:S(2)}, u32[]{:S(2)}) collective-permute-start(f32[16,1024]{1,0:T(8,128)S(1)} %join.1.refs_0_), channel_id=1, source_target_pairs={{0,2},{1,3},{2,0},{3,1},{4,6},{5,7},{6,4},{7,5},{8,10},{9,11},{10,... | collective-permute-start | bytes 196616 | tf_op jit(solution)/shard_map/ppermute | solution.py:20
  52.6 1.1 %collective-permute-start.2 = (f32[16,1024]{1,0:T(8,128)S(1)}, f32[16,1024]{1,0:T(8,128)S(1)}, u32[]{:S(2)}, u32[]{:S(2)}) collective-permute-start(f32[16,1024]{1,0:T(8,128)S(1)} %join.1.refs_0_), channel_id=1, source_target_pairs={{0,3},{1,0},{2,1},{3,2},{4,7},{5,4},{6,5},{7,6},{8,11},{9,8},{10,9... | collective-permute-start | bytes 196616 | tf_op jit(solution)/shard_map/ppermute | solution.py:20
  53.9 2.4 %collective-permute-done.1.refs_2_ = f32[16,1024]{1,0:T(8,128)S(1)} collective-permute-done((f32[16,1024]{1,0:T(8,128)S(1)}, f32[16,1024]{1,0:T(8,128)S(1)}, u32[]{:S(2)}, u32[]{:S(2)}) %collective-permute-start.1) | collective-permute-done | bytes 65568 | tf_op jit(solution)/shard_map/ppermute | solution.py:20
  56.3 1.2 %dispatch.1 = (f32[16,1024]{1,0:T(8,128)S(1)}, bf16[256,1024]{1,0:T(8,128)(2,1)}) custom-call(bf16[16,1024]{1,0:T(8,128)(2,1)S(1)} %copy-done.4, bf16[1024]{0:T(1024)(128)(2,1)S(1)} %copy-done.5, bf16[256,16]{1,0:T(8,128)(2,1)S(1)} %bitcast.30, f32[16,1024]{1,0:T(8,128)S(1)} %join.1.refs_0_, f32[16,1024]{1,0:T(8,128)S(1)} %collective-permute-done.refs_1_, ...), custom_call_target="tpu_custom_call" | custom-call | bytes 894976 | tf_op jit(solution)/shard_map/dispatch/pallas_call | solution.py:241
  57.5 4.6 %all-to-all-start.2 = ((bf16[32,8,1024]{2,1,0:T(8,128)(2,1)}), bf16[32,8,1024]{2,1,0:T(8,128)(2,1)S(1)}, u32[]{:S(2)}, u32[]{:S(2)}) async-start(bf16[32,8,1024]{2,1,0:T(8,128)(2,1)} %bitcast.10), calls=%async_computation.2 | async-start | bytes 1048576 | tf_op jit(solution)/shard_map/all_to_all | solution.py:497
  62.3 11.5 %all-to-all-done.2 = bf16[32,8,1024]{2,1,0:T(8,128)(2,1)S(1)} async-done(((bf16[32,8,1024]{2,1,0:T(8,128)(2,1)}), bf16[32,8,1024]{2,1,0:T(8,128)(2,1)S(1)}, u32[]{:S(2)}, u32[]{:S(2)}) %all-to-all-start.2) | async-done | bytes 524320 | tf_op jit(solution)/shard_map/all_to_all | solution.py:497
  73.8 1.2 %copy-done.2 = bf16[1,1024,512]{2,1,0:T(8,128)(2,1)S(1)} copy-done((bf16[1,1024,512]{2,1,0:T(8,128)(2,1)S(1)}, bf16[1,1024,512]{2,1,0:T(8,128)(2,1)}, u32[]{:S(2)}) %copy-start.2) | copy-done | bytes 1048600
  75.0 1.6 %expert.1 = bf16[256,256]{1,0:T(8,128)(2,1)} custom-call(bf16[256,1024]{1,0:T(8,128)(2,1)S(1)} %bitcast.27, bf16[1024,512]{1,0:T(8,128)(2,1)S(1)} %bitcast.28, bf16[1024,512]{1,0:T(8,128)(2,1)S(1)} %bitcast.29, bf16[512,256]{1,0:T(8,128)(2,1)S(1)} %dynamic-slice_bitcast_fusion.down_ref), custom_call_target="tpu_custom_call" | custom-call | flops 536870912 | bytes 3014656 | tf_op jit(solution)/shard_map/expert/pallas_call | solution.py:241
  76.5 3.6 %all-to-all-start.3 = ((bf16[32,8,256]{2,1,0:T(8,128)(2,1)}), bf16[32,8,256]{2,1,0:T(8,128)(2,1)S(1)}, u32[]{:S(2)}, u32[]{:S(2)}) async-start(bf16[32,8,256]{2,1,0:T(8,128)(2,1)} %bitcast.15), calls=%async_computation.3 | async-start | bytes 262144 | tf_op jit(solution)/shard_map/all_to_all | solution.py:510
  80.2 0.3 fusion.2
  80.5 7.4 %all-to-all-done.3 = bf16[32,8,256]{2,1,0:T(8,128)(2,1)S(1)} async-done(((bf16[32,8,256]{2,1,0:T(8,128)(2,1)}), bf16[32,8,256]{2,1,0:T(8,128)(2,1)S(1)}, u32[]{:S(2)}, u32[]{:S(2)}) %all-to-all-start.3) | async-done | bytes 131104 | tf_op jit(solution)/shard_map/all_to_all | solution.py:510
  87.9 0.8 add_convert_fusion
  (28 shorter events, 0.7 us)
Async XLA Ops:
  0.0 62.2 %copy-start = (bf16[1,512,1024]{2,1,0:T(8,128)(2,1)S(1)}, bf16[1,512,1024]{2,1,0:T(8,128)(2,1)}, u32[]{:S(2)}) copy-start(bf16[1,512,1024]{2,1,0:T(8,128)(2,1)} %param.33) | copy-start | bytes 3145732
  2.2 18.4 %all-to-all-start = ((bf16[32,16,256]{2,1,0:T(8,128)(2,1)}), bf16[32,16,256]{2,1,0:T(8,128)(2,1)S(1)}, u32[]{:S(2)}, u32[]{:S(2)}) async-start(bf16[32,16,256]{2,1,0:T(8,128)(2,1)} %query.1), calls=%async_computation | async-start | bytes 524288 | tf_op jit(solution)/shard_map/all_to_all | solution.py:424
  20.6 0.7 copy-start.6
  21.3 9.7 %copy-start.7 = (s32[16,8]{0,1:T(8,128)S(1)}, s32[16,8]{0,1:T(8,128)}, u32[]{:S(2)}) copy-start(s32[16,8]{0,1:T(8,128)} %param.29) | copy-start | bytes 1540
  21.3 26.5 %copy-start.3 = (bf16[256,1024]{1,0:T(8,128)(2,1)S(1)}, bf16[256,1024]{1,0:T(8,128)(2,1)}, u32[]{:S(2)}) copy-start(bf16[256,1024]{1,0:T(8,128)(2,1)} %w_ref.3) | copy-start | bytes 1572868
  21.3 35.0 %copy-start.4 = (bf16[16,1024]{1,0:T(8,128)(2,1)S(1)}, bf16[16,1024]{1,0:T(8,128)(2,1)}, u32[]{:S(2)}) copy-start(bf16[16,1024]{1,0:T(8,128)(2,1)} %tokens_ref.3) | copy-start | bytes 98308
  21.3 35.0 %copy-start.5 = (bf16[1024]{0:T(1024)(128)(2,1)S(1)}, bf16[1024]{0:T(1024)(128)(2,1)}, u32[]{:S(2)}) copy-start(bf16[1024]{0:T(1024)(128)(2,1)} %gain_ref.3) | copy-start | bytes 6148
  21.3 40.8 %copy-start.8 = (f32[16,8]{0,1:T(8,128)S(1)}, f32[16,8]{0,1:T(8,128)}, u32[]{:S(2)}) copy-start(f32[16,8]{0,1:T(8,128)} %param.30) | copy-start | bytes 1540
  31.0 42.8 %copy-start.1 = (bf16[1,1024,512]{2,1,0:T(8,128)(2,1)S(1)}, bf16[1,1024,512]{2,1,0:T(8,128)(2,1)}, u32[]{:S(2)}) copy-start(bf16[1,1024,512]{2,1,0:T(8,128)(2,1)} %param.31) | copy-start | bytes 3145732
  31.6 16.2 %all-to-all-start.1 = ((bf16[32,16,384]{2,1,0:T(8,128)(2,1)}), bf16[32,16,384]{2,1,0:T(8,128)(2,1)S(1)}, u32[]{:S(2)}, u32[]{:S(2)}) async-start(bf16[32,16,384]{2,1,0:T(8,128)(2,1)} %bitcast.32), calls=%async_computation.1 | async-start | bytes 786432 | tf_op jit(solution)/shard_map/all_to_all | solution.py:465
  48.7 5.2 %collective-permute-start = (f32[16,1024]{1,0:T(8,128)S(1)}, f32[16,1024]{1,0:T(8,128)S(1)}, u32[]{:S(2)}, u32[]{:S(2)}) collective-permute-start(f32[16,1024]{1,0:T(8,128)S(1)} %join.1.refs_0_), channel_id=1, source_target_pairs={{0,1},{1,2},{2,3},{3,0},{4,5},{5,6},{6,7},{7,4},{8,9},{9,10},{10,1... | collective-permute-start | bytes 196616 | tf_op jit(solution)/shard_map/ppermute | solution.py:20
  50.0 6.3 %collective-permute-start.1 = (f32[16,1024]{1,0:T(8,128)S(1)}, f32[16,1024]{1,0:T(8,128)S(1)}, u32[]{:S(2)}, u32[]{:S(2)}) collective-permute-start(f32[16,1024]{1,0:T(8,128)S(1)} %join.1.refs_0_), channel_id=1, source_target_pairs={{0,2},{1,3},{2,0},{3,1},{4,6},{5,7},{6,4},{7,5},{8,10},{9,11},{10,... | collective-permute-start | bytes 196616 | tf_op jit(solution)/shard_map/ppermute | solution.py:20
  52.6 3.7 %collective-permute-start.2 = (f32[16,1024]{1,0:T(8,128)S(1)}, f32[16,1024]{1,0:T(8,128)S(1)}, u32[]{:S(2)}, u32[]{:S(2)}) collective-permute-start(f32[16,1024]{1,0:T(8,128)S(1)} %join.1.refs_0_), channel_id=1, source_target_pairs={{0,3},{1,0},{2,1},{3,2},{4,7},{5,4},{6,5},{7,6},{8,11},{9,8},{10,9... | collective-permute-start | bytes 196616 | tf_op jit(solution)/shard_map/ppermute | solution.py:20
  57.5 16.3 %all-to-all-start.2 = ((bf16[32,8,1024]{2,1,0:T(8,128)(2,1)}), bf16[32,8,1024]{2,1,0:T(8,128)(2,1)S(1)}, u32[]{:S(2)}, u32[]{:S(2)}) async-start(bf16[32,8,1024]{2,1,0:T(8,128)(2,1)} %bitcast.10), calls=%async_computation.2 | async-start | bytes 1048576 | tf_op jit(solution)/shard_map/all_to_all | solution.py:497
  73.8 1.2 %copy-start.2 = (bf16[1,1024,512]{2,1,0:T(8,128)(2,1)S(1)}, bf16[1,1024,512]{2,1,0:T(8,128)(2,1)}, u32[]{:S(2)}) copy-start(bf16[1,1024,512]{2,1,0:T(8,128)(2,1)} %param.32) | copy-start | bytes 3145732
  76.5 11.3 %all-to-all-start.3 = ((bf16[32,8,256]{2,1,0:T(8,128)(2,1)}), bf16[32,8,256]{2,1,0:T(8,128)(2,1)S(1)}, u32[]{:S(2)}, u32[]{:S(2)}) async-start(bf16[32,8,256]{2,1,0:T(8,128)(2,1)} %bitcast.15), calls=%async_computation.3 | async-start | bytes 262144 | tf_op jit(solution)/shard_map/all_to_all | solution.py:510

commit v5 on v4

--- a/solution.py
+++ b/solution.py
@@ -35,7 +35,7 @@
 CHUNK = 64
 PARTS = 4
 SPLIT = 2
-FLIGHT = 3
+FLIGHT = 6
 
 
 def attend_kernel(
@@ -459,7 +459,7 @@
     key_new = key_new.reshape(-1, page_len, key_width)
     value_new = value_new.reshape(-1, page_len, key_width)
     parcel = attend(k_cache, v_cache, key_new, value_new, all_queries, columns, owner_row)
-    parcel, expert_ids, w_down = lax.optimization_barrier((parcel, expert_ids, w_down))
+    parcel, w_down = lax.optimization_barrier((parcel, w_down))
     down_share = lax.dynamic_slice_in_dim(w_down[0], exp_index * quarter, quarter, 1)
     parcel = parcel.reshape(pool_count, req_dev, -1)
     landed = lax.all_to_all(parcel, "pool", split_axis=0, concat_axis=0, tiled=True)
@@ -469,6 +469,7 @@
         [landed, w_out],
         "join",
     )
+    projected, expert_ids = lax.optimization_barrier((projected, expert_ids))
     shares = [projected] + others(projected, "exp")
     top_count = expert_ids.shape[1]
     capacity = min(req_dev, 2 * ((req_dev * top_count + pool_count - 1) // pool_count))

time: 89.2 us -> 88.7 us (level)
  blocking collectives: 0 us -> 16.4 us
  waiting for transfers between devices: 33 us -> 22 us
  starting transfers between devices: 28.7 us -> 22.7 us
    all_to_all x0 -> x1, blocking collectives: none -> 16.4 us  [on_device(): lax.all_to_all(parcel, 'pool', split_axis=0, concat_axis=0, tiled=True)]
    all_to_all x1 -> x0, waiting for transfers between devices: 10.2 us -> none  [on_device(): lax.all_to_all(parcel, 'pool', split_axis=0, concat_axis=0, tiled=True)]
    all_to_all x1 -> x0, starting transfers between devices: 5.93 us -> none  [on_device(): lax.all_to_all(parcel, 'pool', split_axis=0, concat_axis=0, tiled=True)]
  transfers between devices with their start and end apart: 7 -> 6, of which waited for: 5 -> 4; matrix products, arithmetic and copies ran while one was open for 1% -> 1% of each run, Pallas kernels for 8% -> 9%
where the time goes in v5:
time: 88.7 us; the launch traced here: 88.1 us
  Pallas kernels  22.8 us (26%)
  starting transfers between devices  22.7 us (26%)
  waiting for transfers between devices  22 us (25%)
  blocking collectives  16.4 us (18%)
  local copies, waits for them, and re-layouts  2.42 us (3%)
  matrix products  1.04 us (1%)
    all_to_all x1, blocking collectives, on_device(): lax.all_to_all(parcel, 'pool', split_axis=0, concat_axis=0, tiled=True)  16.4 us
    pallas_call x5, Pallas kernels, call(): pl.pallas_call(kernel, out_shape=tuple(outs), in_specs=[pl.BlockSpec(memo...  13.2 us
    all_to_all x1, waiting for transfers between devices, on_device(): lax.all_to_all(outgoing, 'pool', split_axis=0, concat_axis=0, tiled=True)  11.5 us
    pallas_call x1, Pallas kernels, attend(): pl.pallas_call(attend_kernel, out_shape=jax.ShapeDtypeStruct((requests, 3...  9.64 us
    all_to_all x1, starting transfers between devices, on_device(): lax.all_to_all(copies, 'pool', split_axis=0, concat_axis=0, tiled=True)  9.43 us
    all_to_all x1, waiting for transfers between devices, on_device(): lax.all_to_all(expert_out, 'pool', split_axis=0, concat_axis=0, tiled=True)  7.43 us
    ppermute x3, starting transfers between devices, others(): lax.ppermute(value, axis, [(i, (i + step) % size) for i in range(size)])  5 us
    all_to_all x1, starting transfers between devices, on_device(): lax.all_to_all(outgoing, 'pool', split_axis=0, concat_axis=0, tiled=True)  4.65 us
  transfers between devices with their start and end apart: 6, of which 4 were waited for; matrix products, arithmetic and copies ran while one was open for 1% of the time, Pallas kernels for 9%

profile of v5, /device:TPU:1, one launch (start us, length us, event | category | flops | bytes accessed | tf_op | source)
XLA Modules:
  0.0 88.1 jit_solution(12862391820740696148)
XLA Ops:
  0.0 2.1 %query.1 = bf16[32,16,256]{2,1,0:T(8,128)(2,1)} custom-call(bf16[16,1024]{1,0:T(8,128)(2,1)} %tokens_ref.3, bf16[1024]{0:T(1024)(128)(2,1)} %gain_ref.2, bf16[1024,256]{1,0:T(8,128)(2,1)} %w_ref.2), custom_call_target="tpu_custom_call" | custom-call | bytes 821248 | tf_op jit(solution)/shard_map/query/pallas_call | solution.py:241
  2.1 9.4 %all-to-all-start = ((bf16[32,16,256]{2,1,0:T(8,128)(2,1)}), bf16[32,16,256]{2,1,0:T(8,128)(2,1)S(1)}, u32[]{:S(2)}, u32[]{:S(2)}) async-start(bf16[32,16,256]{2,1,0:T(8,128)(2,1)} %query.1), calls=%async_computation | async-start | bytes 524288 | tf_op jit(solution)/shard_map/all_to_all | solution.py:424
  11.6 7.5 %prepare.1 = (bf16[2048,128]{1,0:T(8,128)(2,1)}, bf16[2048,128]{1,0:T(8,128)(2,1)}, s32[640,128]{1,0:T(8,128)}, s32[8,640]{1,0:T(8,128)}) custom-call(s32[1]{0:T(128)} %bitcast.first_ref, bf16[2048,1024]{1,0:T(8,128)(2,1)} %bitcast.31, s32[512,128]{1,0:T(8,128)} %table_hbm.1, s32[4,128]{1,0:T(4,128)} %bitcast.37, bf16[1024,128]{1,0:T(8,128)(2,1)} %wk_hbm.1, ...), custom_call_target="tpu_custom_call" | custom-call | flops 1073741824 | bytes 6379524 | tf_op jit(solution)/shard_map/prepare/pallas_call | solution.py:241
  19.1 1.5 %all-to-all-done = bf16[32,16,256]{2,1,0:T(8,128)(2,1)S(1)} async-done(((bf16[32,16,256]{2,1,0:T(8,128)(2,1)}), bf16[32,16,256]{2,1,0:T(8,128)(2,1)S(1)}, u32[]{:S(2)}, u32[]{:S(2)}) %all-to-all-start) | async-done | bytes 262176 | tf_op jit(solution)/shard_map/all_to_all | solution.py:424
  20.6 0.7 copy-done.6
  21.3 9.6 %attend.1 = bf16[512,384]{1,0:T(8,128)(2,1)} custom-call(bf16[128,128,128]{2,1,0:T(8,128)(2,1)} %k_hbm.1, bf16[128,128,128]{2,1,0:T(8,128)(2,1)} %v_hbm.1, bf16[16,128,128]{2,1,0:T(8,128)(2,1)} %bitcast.34, bf16[16,128,128]{2,1,0:T(8,128)(2,1)} %bitcast.35, bf16[512,256]{1,0:T(8,128)(2,1)} %bitcast.33, s32[640,128]{1,0:T(8,128)} %get-tuple-element.17.cols_ref, ...), custom_call_target="tpu_custom_call" | custom-call | flops 603979776 | bytes 11534336 | tf_op jit(solution)/shard_map/attend/pallas_call | solution.py:211
  31.0 16.4 %all_to_all.20.landed_ref = bf16[32,16,384]{2,1,0:T(8,128)(2,1)S(1)} all-to-all(bf16[32,16,384]{2,1,0:T(8,128)(2,1)} %bitcast.32), channel_id=1, replica_groups=mesh['pool'=32,'exp'=4] {'pool'}, dimensions={0} | all-to-all | bytes 786432 | tf_op jit(solution)/shard_map/all_to_all | solution.py:465
  47.3 0.8 join.1.refs_0_
  48.1 1.3 %collective-permute-start = (f32[16,1024]{1,0:T(8,128)S(1)}, f32[16,1024]{1,0:T(8,128)S(1)}, u32[]{:S(2)}, u32[]{:S(2)}) collective-permute-start(f32[16,1024]{1,0:T(8,128)S(1)} %join.1.refs_0_), channel_id=1, source_target_pairs={{0,1},{1,2},{2,3},{3,0},{4,5},{5,6},{6,7},{7,4},{8,9},{9,10},{10,1... | collective-permute-start | bytes 196616 | tf_op jit(solution)/shard_map/ppermute | solution.py:20
  49.5 2.6 %collective-permute-start.1 = (f32[16,1024]{1,0:T(8,128)S(1)}, f32[16,1024]{1,0:T(8,128)S(1)}, u32[]{:S(2)}, u32[]{:S(2)}) collective-permute-start(f32[16,1024]{1,0:T(8,128)S(1)} %join.1.refs_0_), channel_id=1, source_target_pairs={{0,2},{1,3},{2,0},{3,1},{4,6},{5,7},{6,4},{7,5},{8,10},{9,11},{10,... | collective-permute-start | bytes 196616 | tf_op jit(solution)/shard_map/ppermute | solution.py:20
  52.1 1.1 %collective-permute-start.2 = (f32[16,1024]{1,0:T(8,128)S(1)}, f32[16,1024]{1,0:T(8,128)S(1)}, u32[]{:S(2)}, u32[]{:S(2)}) collective-permute-start(f32[16,1024]{1,0:T(8,128)S(1)} %join.1.refs_0_), channel_id=1, source_target_pairs={{0,3},{1,0},{2,1},{3,2},{4,7},{5,4},{6,5},{7,6},{8,11},{9,8},{10,9... | collective-permute-start | bytes 196616 | tf_op jit(solution)/shard_map/ppermute | solution.py:20
  53.4 0.2 reduce_window_sum.11
  53.6 0.2 select_reduce_fusion
  53.9 0.1 convert_reduce_fusion
  54.1 1.7 %collective-permute-done.1.refs_2_ = f32[16,1024]{1,0:T(8,128)S(1)} collective-permute-done((f32[16,1024]{1,0:T(8,128)S(1)}, f32[16,1024]{1,0:T(8,128)S(1)}, u32[]{:S(2)}, u32[]{:S(2)}) %collective-permute-start.1) | collective-permute-done | bytes 65568 | tf_op jit(solution)/shard_map/ppermute | solution.py:20
  55.8 1.2 %dispatch.1 = (f32[16,1024]{1,0:T(8,128)S(1)}, bf16[256,1024]{1,0:T(8,128)(2,1)}) custom-call(bf16[16,1024]{1,0:T(8,128)(2,1)S(1)} %copy-done.4, bf16[1024]{0:T(1024)(128)(2,1)S(1)} %copy-done.5, bf16[256,16]{1,0:T(8,128)(2,1)S(1)} %bitcast.30, f32[16,1024]{1,0:T(8,128)S(1)} %join.1.refs_0_, f32[16,1024]{1,0:T(8,128)S(1)} %collective-permute-done.refs_1_, ...), custom_call_target="tpu_custom_call" | custom-call | bytes 894976 | tf_op jit(solution)/shard_map/dispatch/pallas_call | solution.py:241
  57.0 4.6 %all-to-all-start.2 = ((bf16[32,8,1024]{2,1,0:T(8,128)(2,1)}), bf16[32,8,1024]{2,1,0:T(8,128)(2,1)S(1)}, u32[]{:S(2)}, u32[]{:S(2)}) async-start(bf16[32,8,1024]{2,1,0:T(8,128)(2,1)} %bitcast.10), calls=%async_computation.2 | async-start | bytes 1048576 | tf_op jit(solution)/shard_map/all_to_all | solution.py:498
  61.7 11.5 %all-to-all-done.2 = bf16[32,8,1024]{2,1,0:T(8,128)(2,1)S(1)} async-done(((bf16[32,8,1024]{2,1,0:T(8,128)(2,1)}), bf16[32,8,1024]{2,1,0:T(8,128)(2,1)S(1)}, u32[]{:S(2)}, u32[]{:S(2)}) %all-to-all-start.2) | async-done | bytes 524320 | tf_op jit(solution)/shard_map/all_to_all | solution.py:498
  73.3 1.2 %copy-done.2 = bf16[1,1024,512]{2,1,0:T(8,128)(2,1)S(1)} copy-done((bf16[1,1024,512]{2,1,0:T(8,128)(2,1)S(1)}, bf16[1,1024,512]{2,1,0:T(8,128)(2,1)}, u32[]{:S(2)}) %copy-start.2) | copy-done | bytes 1048600
  74.5 1.5 %expert.1 = bf16[256,256]{1,0:T(8,128)(2,1)} custom-call(bf16[256,1024]{1,0:T(8,128)(2,1)S(1)} %bitcast.27, bf16[1024,512]{1,0:T(8,128)(2,1)S(1)} %bitcast.28, bf16[1024,512]{1,0:T(8,128)(2,1)S(1)} %bitcast.29, bf16[512,256]{1,0:T(8,128)(2,1)S(1)} %dynamic-slice_bitcast_fusion.down_ref), custom_call_target="tpu_custom_call" | custom-call | flops 536870912 | bytes 3014656 | tf_op jit(solution)/shard_map/expert/pallas_call | solution.py:241
  76.0 3.6 %all-to-all-start.3 = ((bf16[32,8,256]{2,1,0:T(8,128)(2,1)}), bf16[32,8,256]{2,1,0:T(8,128)(2,1)S(1)}, u32[]{:S(2)}, u32[]{:S(2)}) async-start(bf16[32,8,256]{2,1,0:T(8,128)(2,1)} %bitcast.15), calls=%async_computation.3 | async-start | bytes 262144 | tf_op jit(solution)/shard_map/all_to_all | solution.py:511
  79.7 0.3 fusion.2
  79.9 7.4 %all-to-all-done.3 = bf16[32,8,256]{2,1,0:T(8,128)(2,1)S(1)} async-done(((bf16[32,8,256]{2,1,0:T(8,128)(2,1)}), bf16[32,8,256]{2,1,0:T(8,128)(2,1)S(1)}, u32[]{:S(2)}, u32[]{:S(2)}) %all-to-all-start.3) | async-done | bytes 131104 | tf_op jit(solution)/shard_map/all_to_all | solution.py:511
  87.4 0.8 add_convert_fusion
  (27 shorter events, 0.6 us)
Async XLA Ops:
  0.0 61.7 %copy-start = (bf16[1,512,1024]{2,1,0:T(8,128)(2,1)S(1)}, bf16[1,512,1024]{2,1,0:T(8,128)(2,1)}, u32[]{:S(2)}) copy-start(bf16[1,512,1024]{2,1,0:T(8,128)(2,1)} %param.33) | copy-start | bytes 3145732
  2.1 18.4 %all-to-all-start = ((bf16[32,16,256]{2,1,0:T(8,128)(2,1)}), bf16[32,16,256]{2,1,0:T(8,128)(2,1)S(1)}, u32[]{:S(2)}, u32[]{:S(2)}) async-start(bf16[32,16,256]{2,1,0:T(8,128)(2,1)} %query.1), calls=%async_computation | async-start | bytes 524288 | tf_op jit(solution)/shard_map/all_to_all | solution.py:424
  20.6 0.7 copy-start.6
  21.3 26.1 %copy-start.3 = (bf16[256,1024]{1,0:T(8,128)(2,1)S(1)}, bf16[256,1024]{1,0:T(8,128)(2,1)}, u32[]{:S(2)}) copy-start(bf16[256,1024]{1,0:T(8,128)(2,1)} %w_ref.3) | copy-start | bytes 1572868
  21.3 31.9 %copy-start.7 = (s32[16,8]{0,1:T(8,128)S(1)}, s32[16,8]{0,1:T(8,128)}, u32[]{:S(2)}) copy-start(s32[16,8]{0,1:T(8,128)} %param.29) | copy-start | bytes 1540
  21.3 34.5 %copy-start.4 = (bf16[16,1024]{1,0:T(8,128)(2,1)S(1)}, bf16[16,1024]{1,0:T(8,128)(2,1)}, u32[]{:S(2)}) copy-start(bf16[16,1024]{1,0:T(8,128)(2,1)} %tokens_ref.3) | copy-start | bytes 98308
  21.3 34.5 %copy-start.5 = (bf16[1024]{0:T(1024)(128)(2,1)S(1)}, bf16[1024]{0:T(1024)(128)(2,1)}, u32[]{:S(2)}) copy-start(bf16[1024]{0:T(1024)(128)(2,1)} %gain_ref.3) | copy-start | bytes 6148
  21.3 40.3 %copy-start.8 = (f32[16,8]{0,1:T(8,128)S(1)}, f32[16,8]{0,1:T(8,128)}, u32[]{:S(2)}) copy-start(f32[16,8]{0,1:T(8,128)} %param.30) | copy-start | bytes 1540
  30.9 42.3 %copy-start.1 = (bf16[1,1024,512]{2,1,0:T(8,128)(2,1)S(1)}, bf16[1,1024,512]{2,1,0:T(8,128)(2,1)}, u32[]{:S(2)}) copy-start(bf16[1,1024,512]{2,1,0:T(8,128)(2,1)} %param.31) | copy-start | bytes 3145732
  48.1 6.0 %collective-permute-start = (f32[16,1024]{1,0:T(8,128)S(1)}, f32[16,1024]{1,0:T(8,128)S(1)}, u32[]{:S(2)}, u32[]{:S(2)}) collective-permute-start(f32[16,1024]{1,0:T(8,128)S(1)} %join.1.refs_0_), channel_id=1, source_target_pairs={{0,1},{1,2},{2,3},{3,0},{4,5},{5,6},{6,7},{7,4},{8,9},{9,10},{10,1... | collective-permute-start | bytes 196616 | tf_op jit(solution)/shard_map/ppermute | solution.py:20
  49.5 6.3 %collective-permute-start.1 = (f32[16,1024]{1,0:T(8,128)S(1)}, f32[16,1024]{1,0:T(8,128)S(1)}, u32[]{:S(2)}, u32[]{:S(2)}) collective-permute-start(f32[16,1024]{1,0:T(8,128)S(1)} %join.1.refs_0_), channel_id=1, source_target_pairs={{0,2},{1,3},{2,0},{3,1},{4,6},{5,7},{6,4},{7,5},{8,10},{9,11},{10,... | collective-permute-start | bytes 196616 | tf_op jit(solution)/shard_map/ppermute | solution.py:20
  52.1 3.7 %collective-permute-start.2 = (f32[16,1024]{1,0:T(8,128)S(1)}, f32[16,1024]{1,0:T(8,128)S(1)}, u32[]{:S(2)}, u32[]{:S(2)}) collective-permute-start(f32[16,1024]{1,0:T(8,128)S(1)} %join.1.refs_0_), channel_id=1, source_target_pairs={{0,3},{1,0},{2,1},{3,2},{4,7},{5,4},{6,5},{7,6},{8,11},{9,8},{10,9... | collective-permute-start | bytes 196616 | tf_op jit(solution)/shard_map/ppermute | solution.py:20
  57.0 16.3 %all-to-all-start.2 = ((bf16[32,8,1024]{2,1,0:T(8,128)(2,1)}), bf16[32,8,1024]{2,1,0:T(8,128)(2,1)S(1)}, u32[]{:S(2)}, u32[]{:S(2)}) async-start(bf16[32,8,1024]{2,1,0:T(8,128)(2,1)} %bitcast.10), calls=%async_computation.2 | async-start | bytes 1048576 | tf_op jit(solution)/shard_map/all_to_all | solution.py:498
  73.2 1.2 %copy-start.2 = (bf16[1,1024,512]{2,1,0:T(8,128)(2,1)S(1)}, bf16[1,1024,512]{2,1,0:T(8,128)(2,1)}, u32[]{:S(2)}) copy-start(bf16[1,1024,512]{2,1,0:T(8,128)(2,1)} %param.32) | copy-start | bytes 3145732
  76.0 11.3 %all-to-all-start.3 = ((bf16[32,8,256]{2,1,0:T(8,128)(2,1)}), bf16[32,8,256]{2,1,0:T(8,128)(2,1)S(1)}, u32[]{:S(2)}, u32[]{:S(2)}) async-start(bf16[32,8,256]{2,1,0:T(8,128)(2,1)} %bitcast.15), calls=%async_computation.3 | async-start | bytes 262144 | tf_op jit(solution)/shard_map/all_to_all | solution.py:511

commit v6 on v5

--- a/solution.py
+++ b/solution.py
@@ -362,7 +362,7 @@
 
 def dispatch_kernel(tokens_ref, gain_ref, send_ref, *refs):
     *share_refs, mixed_ref, out_ref = refs
-    mixed = tokens_ref[...].astype(jnp.float32) + sum(share[...] for share in share_refs)
+    mixed = tokens_ref[...].astype(jnp.float32) + sum(share[...].astype(jnp.float32) for share in share_refs)
     mixed_ref[...] = mixed
     normed = rms_scale(mixed, gain_ref[...].astype(jnp.float32)).astype(jnp.bfloat16)
     out_ref[...] = jnp.dot(send_ref[...], normed, preferred_element_type=jnp.float32).astype(
@@ -470,7 +470,7 @@
         "join",
     )
     projected, expert_ids = lax.optimization_barrier((projected, expert_ids))
-    shares = [projected] + others(projected, "exp")
+    shares = [projected] + others(projected.astype(bf16), "exp")
     top_count = expert_ids.shape[1]
     capacity = min(req_dev, 2 * ((req_dev * top_count + pool_count - 1) // pool_count))
     route_flat = expert_ids.reshape(-1)

time: 88.7 us -> 88.4 us (level)
  waiting for transfers between devices: 22 us -> 21.1 us
    ppermute x3, waiting for transfers between devices: 1.66 us -> 0.72 us  [others(): lax.ppermute(value, axis, [(i, (i + step) % size) for i in range(size)])]
  transfers between devices with their start and end apart: 6 -> 6, of which waited for: 4 -> 5; matrix products, arithmetic and copies ran while one was open for 1% -> 1% of each run, Pallas kernels for 9% -> 9%
where the time goes in v6:
time: 88.4 us; the launch traced here: 87.9 us
  starting transfers between devices  23.4 us (26%)
  Pallas kernels  22.8 us (26%)
  waiting for transfers between devices  21.1 us (24%)
  blocking collectives  16.4 us (19%)
  local copies, waits for them, and re-layouts  2.42 us (3%)
  matrix products  1.04 us (1%)
    all_to_all x1, blocking collectives, on_device(): lax.all_to_all(parcel, 'pool', split_axis=0, concat_axis=0, tiled=True)  16.4 us
    pallas_call x5, Pallas kernels, call(): pl.pallas_call(kernel, out_shape=tuple(outs), in_specs=[pl.BlockSpec(memo...  13.2 us
    all_to_all x1, waiting for transfers between devices, on_device(): lax.all_to_all(outgoing, 'pool', split_axis=0, concat_axis=0, tiled=True)  11.5 us
    pallas_call x1, Pallas kernels, attend(): pl.pallas_call(attend_kernel, out_shape=jax.ShapeDtypeStruct((requests, 3...  9.64 us
    all_to_all x1, starting transfers between devices, on_device(): lax.all_to_all(copies, 'pool', split_axis=0, concat_axis=0, tiled=True)  9.43 us
    all_to_all x1, waiting for transfers between devices, on_device(): lax.all_to_all(expert_out, 'pool', split_axis=0, concat_axis=0, tiled=True)  7.43 us
    all_to_all x1, starting transfers between devices, on_device(): lax.all_to_all(outgoing, 'pool', split_axis=0, concat_axis=0, tiled=True)  5.25 us
    ppermute x3, starting transfers between devices, others(): lax.ppermute(value, axis, [(i, (i + step) % size) for i in range(size)])  5.06 us
  transfers between devices with their start and end apart: 6, of which 5 were waited for; matrix products, arithmetic and copies ran while one was open for 1% of the time, Pallas kernels for 9%

profile of v6, /device:TPU:1, one launch (start us, length us, event | category | flops | bytes accessed | tf_op | source)
XLA Modules:
  0.0 87.9 jit_solution(10912602034912519142)
XLA Ops:
  0.0 2.1 %query.1 = bf16[32,16,256]{2,1,0:T(8,128)(2,1)} custom-call(bf16[16,1024]{1,0:T(8,128)(2,1)} %tokens_ref.3, bf16[1024]{0:T(1024)(128)(2,1)} %gain_ref.2, bf16[1024,256]{1,0:T(8,128)(2,1)} %w_ref.2), custom_call_target="tpu_custom_call" | custom-call | bytes 821248 | tf_op jit(solution)/shard_map/query/pallas_call | solution.py:241
  2.1 9.4 %all-to-all-start = ((bf16[32,16,256]{2,1,0:T(8,128)(2,1)}), bf16[32,16,256]{2,1,0:T(8,128)(2,1)S(1)}, u32[]{:S(2)}, u32[]{:S(2)}) async-start(bf16[32,16,256]{2,1,0:T(8,128)(2,1)} %query.1), calls=%async_computation | async-start | bytes 524288 | tf_op jit(solution)/shard_map/all_to_all | solution.py:424
  11.6 7.5 %prepare.1 = (bf16[2048,128]{1,0:T(8,128)(2,1)}, bf16[2048,128]{1,0:T(8,128)(2,1)}, s32[640,128]{1,0:T(8,128)}, s32[8,640]{1,0:T(8,128)}) custom-call(s32[1]{0:T(128)} %bitcast.first_ref, bf16[2048,1024]{1,0:T(8,128)(2,1)} %bitcast.31, s32[512,128]{1,0:T(8,128)} %table_hbm.1, s32[4,128]{1,0:T(4,128)} %bitcast.37, bf16[1024,128]{1,0:T(8,128)(2,1)} %wk_hbm.1, ...), custom_call_target="tpu_custom_call" | custom-call | flops 1073741824 | bytes 6379524 | tf_op jit(solution)/shard_map/prepare/pallas_call | solution.py:241
  19.1 1.5 %all-to-all-done = bf16[32,16,256]{2,1,0:T(8,128)(2,1)S(1)} async-done(((bf16[32,16,256]{2,1,0:T(8,128)(2,1)}), bf16[32,16,256]{2,1,0:T(8,128)(2,1)S(1)}, u32[]{:S(2)}, u32[]{:S(2)}) %all-to-all-start) | async-done | bytes 262176 | tf_op jit(solution)/shard_map/all_to_all | solution.py:424
  20.6 0.7 copy-done.6
  21.3 9.6 %attend.1 = bf16[512,384]{1,0:T(8,128)(2,1)} custom-call(bf16[128,128,128]{2,1,0:T(8,128)(2,1)} %k_hbm.1, bf16[128,128,128]{2,1,0:T(8,128)(2,1)} %v_hbm.1, bf16[16,128,128]{2,1,0:T(8,128)(2,1)} %bitcast.34, bf16[16,128,128]{2,1,0:T(8,128)(2,1)} %bitcast.35, bf16[512,256]{1,0:T(8,128)(2,1)} %bitcast.33, s32[640,128]{1,0:T(8,128)} %get-tuple-element.17.cols_ref, ...), custom_call_target="tpu_custom_call" | custom-call | flops 603979776 | bytes 11534336 | tf_op jit(solution)/shard_map/attend/pallas_call | solution.py:211
  31.0 16.4 %all_to_all.20.landed_ref = bf16[32,16,384]{2,1,0:T(8,128)(2,1)S(1)} all-to-all(bf16[32,16,384]{2,1,0:T(8,128)(2,1)} %bitcast.32), channel_id=1, replica_groups=mesh['pool'=32,'exp'=4] {'pool'}, dimensions={0} | all-to-all | bytes 786432 | tf_op jit(solution)/shard_map/all_to_all | solution.py:465
  47.3 0.8 join.1.refs_0_
  48.1 1.4 %collective-permute-start = (bf16[16,1024]{1,0:T(8,128)(2,1)S(1)}, bf16[16,1024]{1,0:T(8,128)(2,1)S(1)}, u32[]{:S(2)}, u32[]{:S(2)}) collective-permute-start(bf16[16,1024]{1,0:T(8,128)(2,1)S(1)} %convert_element_type.25), channel_id=1, source_target_pairs={{0,1},{1,2},{2,3},{3,0},{4,5},{5,6},{6,7},{7,4},{8,9},{9,10},{10,1... | collective-permute-start | bytes 98312 | tf_op jit(solution)/shard_map/ppermute | solution.py:20
  49.5 2.6 %collective-permute-start.1 = (bf16[16,1024]{1,0:T(8,128)(2,1)S(1)}, bf16[16,1024]{1,0:T(8,128)(2,1)S(1)}, u32[]{:S(2)}, u32[]{:S(2)}) collective-permute-start(bf16[16,1024]{1,0:T(8,128)(2,1)S(1)} %convert_element_type.25), channel_id=1, source_target_pairs={{0,2},{1,3},{2,0},{3,1},{4,6},{5,7},{6,4},{7,5},{8,10},{9,11},{10,... | collective-permute-start | bytes 98312 | tf_op jit(solution)/shard_map/ppermute | solution.py:20
  52.1 1.1 %collective-permute-start.2 = (bf16[16,1024]{1,0:T(8,128)(2,1)S(1)}, bf16[16,1024]{1,0:T(8,128)(2,1)S(1)}, u32[]{:S(2)}, u32[]{:S(2)}) collective-permute-start(bf16[16,1024]{1,0:T(8,128)(2,1)S(1)} %convert_element_type.25), channel_id=1, source_target_pairs={{0,3},{1,0},{2,1},{3,2},{4,7},{5,4},{6,5},{7,6},{8,11},{9,8},{10,9... | collective-permute-start | bytes 98312 | tf_op jit(solution)/shard_map/ppermute | solution.py:20
  53.5 0.2 reduce_window_sum.11
  53.6 0.2 select_reduce_fusion
  54.2 0.2 collective-permute-done.1.refs_2_
  54.4 0.5 collective-permute-done.2.refs_3_
  54.9 1.2 %dispatch.1 = (f32[16,1024]{1,0:T(8,128)S(1)}, bf16[256,1024]{1,0:T(8,128)(2,1)}) custom-call(bf16[16,1024]{1,0:T(8,128)(2,1)S(1)} %copy-done.4, bf16[1024]{0:T(1024)(128)(2,1)S(1)} %copy-done.5, bf16[256,16]{1,0:T(8,128)(2,1)S(1)} %bitcast.30, f32[16,1024]{1,0:T(8,128)S(1)} %join.1.refs_0_, bf16[16,1024]{1,0:T(8,128)(2,1)S(1)} %collective-permute-done.refs_1_, ...), custom_call_target="tpu_custom_call" | custom-call | bytes 796672 | tf_op jit(solution)/shard_map/dispatch/pallas_call | solution.py:241
  56.1 5.3 %all-to-all-start.2 = ((bf16[32,8,1024]{2,1,0:T(8,128)(2,1)}), bf16[32,8,1024]{2,1,0:T(8,128)(2,1)S(1)}, u32[]{:S(2)}, u32[]{:S(2)}) async-start(bf16[32,8,1024]{2,1,0:T(8,128)(2,1)} %bitcast.10), calls=%async_computation.2 | async-start | bytes 1048576 | tf_op jit(solution)/shard_map/all_to_all | solution.py:498
  61.5 11.5 %all-to-all-done.2 = bf16[32,8,1024]{2,1,0:T(8,128)(2,1)S(1)} async-done(((bf16[32,8,1024]{2,1,0:T(8,128)(2,1)}), bf16[32,8,1024]{2,1,0:T(8,128)(2,1)S(1)}, u32[]{:S(2)}, u32[]{:S(2)}) %all-to-all-start.2) | async-done | bytes 524320 | tf_op jit(solution)/shard_map/all_to_all | solution.py:498
  73.0 1.2 %copy-done.2 = bf16[1,1024,512]{2,1,0:T(8,128)(2,1)S(1)} copy-done((bf16[1,1024,512]{2,1,0:T(8,128)(2,1)S(1)}, bf16[1,1024,512]{2,1,0:T(8,128)(2,1)}, u32[]{:S(2)}) %copy-start.2) | copy-done | bytes 1048600
  74.2 1.5 %expert.1 = bf16[256,256]{1,0:T(8,128)(2,1)} custom-call(bf16[256,1024]{1,0:T(8,128)(2,1)S(1)} %bitcast.27, bf16[1024,512]{1,0:T(8,128)(2,1)S(1)} %bitcast.28, bf16[1024,512]{1,0:T(8,128)(2,1)S(1)} %bitcast.29, bf16[512,256]{1,0:T(8,128)(2,1)S(1)} %dynamic-slice_bitcast_fusion.down_ref), custom_call_target="tpu_custom_call" | custom-call | flops 536870912 | bytes 3014656 | tf_op jit(solution)/shard_map/expert/pallas_call | solution.py:241
  75.7 3.6 %all-to-all-start.3 = ((bf16[32,8,256]{2,1,0:T(8,128)(2,1)}), bf16[32,8,256]{2,1,0:T(8,128)(2,1)S(1)}, u32[]{:S(2)}, u32[]{:S(2)}) async-start(bf16[32,8,256]{2,1,0:T(8,128)(2,1)} %bitcast.15), calls=%async_computation.3 | async-start | bytes 262144 | tf_op jit(solution)/shard_map/all_to_all | solution.py:511
  79.4 0.3 fusion.2
  79.6 7.4 %all-to-all-done.3 = bf16[32,8,256]{2,1,0:T(8,128)(2,1)S(1)} async-done(((bf16[32,8,256]{2,1,0:T(8,128)(2,1)}), bf16[32,8,256]{2,1,0:T(8,128)(2,1)S(1)}, u32[]{:S(2)}, u32[]{:S(2)}) %all-to-all-start.3) | async-done | bytes 131104 | tf_op jit(solution)/shard_map/all_to_all | solution.py:511
  87.1 0.8 add_convert_fusion
  (28 shorter events, 0.7 us)
Async XLA Ops:
  0.0 61.4 %copy-start = (bf16[1,512,1024]{2,1,0:T(8,128)(2,1)S(1)}, bf16[1,512,1024]{2,1,0:T(8,128)(2,1)}, u32[]{:S(2)}) copy-start(bf16[1,512,1024]{2,1,0:T(8,128)(2,1)} %param.33) | copy-start | bytes 3145732
  2.1 18.4 %all-to-all-start = ((bf16[32,16,256]{2,1,0:T(8,128)(2,1)}), bf16[32,16,256]{2,1,0:T(8,128)(2,1)S(1)}, u32[]{:S(2)}, u32[]{:S(2)}) async-start(bf16[32,16,256]{2,1,0:T(8,128)(2,1)} %query.1), calls=%async_computation | async-start | bytes 524288 | tf_op jit(solution)/shard_map/all_to_all | solution.py:424
  20.6 0.7 copy-start.6
  21.3 26.0 %copy-start.3 = (bf16[256,1024]{1,0:T(8,128)(2,1)S(1)}, bf16[256,1024]{1,0:T(8,128)(2,1)}, u32[]{:S(2)}) copy-start(bf16[256,1024]{1,0:T(8,128)(2,1)} %w_ref.3) | copy-start | bytes 1572868
  21.3 31.9 %copy-start.7 = (s32[16,8]{0,1:T(8,128)S(1)}, s32[16,8]{0,1:T(8,128)}, u32[]{:S(2)}) copy-start(s32[16,8]{0,1:T(8,128)} %param.29) | copy-start | bytes 1540
  21.3 33.6 %copy-start.4 = (bf16[16,1024]{1,0:T(8,128)(2,1)S(1)}, bf16[16,1024]{1,0:T(8,128)(2,1)}, u32[]{:S(2)}) copy-start(bf16[16,1024]{1,0:T(8,128)(2,1)} %tokens_ref.3) | copy-start | bytes 98308
  21.3 33.6 %copy-start.5 = (bf16[1024]{0:T(1024)(128)(2,1)S(1)}, bf16[1024]{0:T(1024)(128)(2,1)}, u32[]{:S(2)}) copy-start(bf16[1024]{0:T(1024)(128)(2,1)} %gain_ref.3) | copy-start | bytes 6148
  21.3 40.1 %copy-start.8 = (f32[16,8]{0,1:T(8,128)S(1)}, f32[16,8]{0,1:T(8,128)}, u32[]{:S(2)}) copy-start(f32[16,8]{0,1:T(8,128)} %param.30) | copy-start | bytes 1540
  30.9 42.0 %copy-start.1 = (bf16[1,1024,512]{2,1,0:T(8,128)(2,1)S(1)}, bf16[1,1024,512]{2,1,0:T(8,128)(2,1)}, u32[]{:S(2)}) copy-start(bf16[1,1024,512]{2,1,0:T(8,128)(2,1)} %param.31) | copy-start | bytes 3145732
  48.1 6.0 %collective-permute-start = (bf16[16,1024]{1,0:T(8,128)(2,1)S(1)}, bf16[16,1024]{1,0:T(8,128)(2,1)S(1)}, u32[]{:S(2)}, u32[]{:S(2)}) collective-permute-start(bf16[16,1024]{1,0:T(8,128)(2,1)S(1)} %convert_element_type.25), channel_id=1, source_target_pairs={{0,1},{1,2},{2,3},{3,0},{4,5},{5,6},{6,7},{7,4},{8,9},{9,10},{10,1... | collective-permute-start | bytes 98312 | tf_op jit(solution)/shard_map/ppermute | solution.py:20
  49.5 4.9 %collective-permute-start.1 = (bf16[16,1024]{1,0:T(8,128)(2,1)S(1)}, bf16[16,1024]{1,0:T(8,128)(2,1)S(1)}, u32[]{:S(2)}, u32[]{:S(2)}) collective-permute-start(bf16[16,1024]{1,0:T(8,128)(2,1)S(1)} %convert_element_type.25), channel_id=1, source_target_pairs={{0,2},{1,3},{2,0},{3,1},{4,6},{5,7},{6,4},{7,5},{8,10},{9,11},{10,... | collective-permute-start | bytes 98312 | tf_op jit(solution)/shard_map/ppermute | solution.py:20
  52.1 2.8 %collective-permute-start.2 = (bf16[16,1024]{1,0:T(8,128)(2,1)S(1)}, bf16[16,1024]{1,0:T(8,128)(2,1)S(1)}, u32[]{:S(2)}, u32[]{:S(2)}) collective-permute-start(bf16[16,1024]{1,0:T(8,128)(2,1)S(1)} %convert_element_type.25), channel_id=1, source_target_pairs={{0,3},{1,0},{2,1},{3,2},{4,7},{5,4},{6,5},{7,6},{8,11},{9,8},{10,9... | collective-permute-start | bytes 98312 | tf_op jit(solution)/shard_map/ppermute | solution.py:20
  56.1 16.9 %all-to-all-start.2 = ((bf16[32,8,1024]{2,1,0:T(8,128)(2,1)}), bf16[32,8,1024]{2,1,0:T(8,128)(2,1)S(1)}, u32[]{:S(2)}, u32[]{:S(2)}) async-start(bf16[32,8,1024]{2,1,0:T(8,128)(2,1)} %bitcast.10), calls=%async_computation.2 | async-start | bytes 1048576 | tf_op jit(solution)/shard_map/all_to_all | solution.py:498
  73.0 1.2 %copy-start.2 = (bf16[1,1024,512]{2,1,0:T(8,128)(2,1)S(1)}, bf16[1,1024,512]{2,1,0:T(8,128)(2,1)}, u32[]{:S(2)}) copy-start(bf16[1,1024,512]{2,1,0:T(8,128)(2,1)} %param.32) | copy-start | bytes 3145732
  75.7 11.3 %all-to-all-start.3 = ((bf16[32,8,256]{2,1,0:T(8,128)(2,1)}), bf16[32,8,256]{2,1,0:T(8,128)(2,1)S(1)}, u32[]{:S(2)}, u32[]{:S(2)}) async-start(bf16[32,8,256]{2,1,0:T(8,128)(2,1)} %bitcast.15), calls=%async_computation.3 | async-start | bytes 262144 | tf_op jit(solution)/shard_map/all_to_all | solution.py:511
